TPU v7x, 256 devices: a whole 4x4x8 slice. The times are simulated.
256 devices in a mesh: depth: 8 (over x_lo, y), row: 32 (over x_hi, z, core).
Axes of the slice: x: 4 (x_hi: 2, x_lo: 2; x = x_hi * 2 + x_lo), y: 4, z: 8, core: 2. Of those that a mesh axis runs over, the one named last changes fastest.
Arguments:
- field: float32 [2, 8, 4096, 4096], P(None, 'depth', 'row'), may hold values from -6 to 6
- hologram: float32 [4096, 4096], P('row'), may hold values from -16 to 16
- defocus: float32 [8], P('depth'), may hold values from 512 to 2048
Outputs:
- estimate: float32 [2, 8, 4096, 4096], P(None, 'depth', 'row')
All inputs are finite; a program needn't handle non-finite values.
Results may differ from a plain program's by a relative error of at most 0.00045.
Values sent between devices are 32-bit elements; how exact they have to be, the bound alone decides.
A program may use at most 320 MiB of HBM per device.

v0:
```python
import math

import jax
import jax.numpy as jnp
from jax import lax
from jax.sharding import PartitionSpec as P

tv_step_size = 1.0 / 12.0
tv_sharpness = 0.25


def passed_along(block, axis, distance):
    devices = range(lax.axis_size(axis))
    route = [(i - distance, i) for i in devices if i - distance in devices]
    return lax.ppermute(block, axis, route)


def split_length(length_total):
    smaller = 1
    candidate = 1
    while candidate * candidate <= length_total:
        if length_total % candidate == 0:
            smaller = candidate
        candidate = candidate + 1
    return (smaller, length_total // smaller)


def block_table(cosines, sines):
    return jnp.stack([jnp.stack([cosines, -sines]), jnp.stack([sines, cosines])])


def dft_tables(length_total, inverse):
    outer_len, inner_len = split_length(length_total)
    direction = 2.0 * math.pi if inverse else -2.0 * math.pi
    first_k = jnp.arange(outer_len, dtype=jnp.int32)[:, None]
    first_a = jnp.arange(outer_len, dtype=jnp.int32)[None, :]
    radians_one = (first_k * first_a % outer_len).astype(jnp.float32) * (direction / outer_len)
    first_table = block_table(jnp.cos(radians_one), jnp.sin(radians_one))
    second_k = jnp.arange(outer_len, dtype=jnp.int32)[:, None, None]
    second_b = jnp.arange(inner_len, dtype=jnp.int32)[None, :, None]
    second_m = jnp.arange(inner_len, dtype=jnp.int32)[None, None, :]
    whole_index = (second_k * second_b + second_b * second_m * outer_len) % length_total
    radians_two = whole_index.astype(jnp.float32) * (direction / length_total)
    scale = 1.0 / length_total if inverse else 1.0
    second_table = block_table(jnp.cos(radians_two) * scale, jnp.sin(radians_two) * scale)
    return (first_table, second_table, outer_len, inner_len)


def contract(formula, table, data):
    return jnp.einsum(
        formula, table, data, precision=lax.Precision.HIGHEST, preferred_element_type=jnp.float32
    )


def transform_last(data, tables, real_input, real_only):
    first_table, second_table, outer_len, inner_len = tables
    if real_input:
        data = data[None]
        first_table = first_table[:, :1]
    if real_only:
        second_table = second_table[:1]
    leading = data.shape[1:-1]
    folded = data.reshape((data.shape[0],) + leading + (outer_len, inner_len))
    middle = contract("rqka,q...ab->r...kb", first_table, folded)
    result = contract("rqkbm,q...kb->r...mk", second_table, middle)
    result = result.reshape((result.shape[0],) + leading + (outer_len * inner_len,))
    if real_only:
        return result[0]
    return result


def transform_rows(data, tables):
    first_table, second_table, outer_len, inner_len = tables
    leading = data.shape[1:-2]
    trailing = data.shape[-1]
    folded = data.reshape((2,) + leading + (outer_len, inner_len, trailing))
    middle = contract("rqka,q...abc->r...kbc", first_table, folded)
    result = contract("rqkbm,q...kbc->r...mkc", second_table, middle)
    return result.reshape((2,) + leading + (outer_len * inner_len, trailing))


def centred_squares(length_total, offset_start, length_part):
    indices = offset_start + jnp.arange(length_part, dtype=jnp.int32)
    centred = jnp.where(indices < length_total // 2, indices, indices - length_total)
    return (centred * centred).astype(jnp.float32)


def transfer_phase(depth_values, length_total, column_start, column_len):
    ky_squares = centred_squares(length_total, 0, length_total)
    kx_squares = centred_squares(length_total, column_start, column_len)
    grid_sum = (ky_squares[:, None] + kx_squares[None, :]) * (
        math.pi / (length_total * length_total)
    )
    return depth_values[:, None, None] * grid_sum[None]


def ahead_diff(values, incoming, axis_pos):
    extent = values.shape[axis_pos]
    shifted = jnp.concatenate(
        [lax.slice_in_dim(values, 1, extent, axis=axis_pos), incoming], axis=axis_pos
    )
    return shifted - values


def behind_diff(values, incoming, axis_pos):
    extent = values.shape[axis_pos]
    shifted = jnp.concatenate(
        [incoming, lax.slice_in_dim(values, 0, extent - 1, axis=axis_pos)], axis=axis_pos
    )
    return values - shifted


def flux_terms(depth_diff, row_diff, col_diff):
    magnitude = jnp.sqrt(
        jnp.sum(depth_diff * depth_diff + row_diff * row_diff + col_diff * col_diff, axis=0)
    )
    factor = 1.0 / (1.0 + tv_sharpness * magnitude)
    return (depth_diff * factor, row_diff * factor, col_diff * factor)


def shrink_shifts(moved_field, depth_index, row_index, plane_total, length_total):
    planes_dev = moved_field.shape[1]
    rows_dev = moved_field.shape[2]
    plane_next = passed_along(moved_field, "depth", -1)
    row_next = passed_along(moved_field[:, :, :1], "row", -1)
    plane_ids = depth_index * planes_dev + jnp.arange(planes_dev, dtype=jnp.int32)
    row_ids = row_index * rows_dev + jnp.arange(rows_dev, dtype=jnp.int32)
    depth_diff = jnp.where(
        (plane_ids == plane_total - 1)[None, :, None, None],
        0.0,
        ahead_diff(moved_field, plane_next, 1),
    )
    row_diff = jnp.where(
        (row_ids == length_total - 1)[None, None, :, None],
        0.0,
        ahead_diff(moved_field, row_next, 2),
    )
    col_diff = ahead_diff(moved_field, moved_field[..., -1:], 3)
    flux_z, flux_y, flux_x = flux_terms(depth_diff, row_diff, col_diff)
    prior_plane = passed_along(flux_z, "depth", 1)
    prior_row = passed_along(flux_y[:, :, -1:], "row", 1)
    divergence = (
        behind_diff(flux_z, prior_plane, 1)
        + behind_diff(flux_y, prior_row, 2)
        + behind_diff(flux_x, jnp.zeros_like(flux_x[..., :1]), 3)
    )
    return moved_field + tv_step_size * divergence


def per_device(field, hologram, defocus):
    planes_dev = field.shape[1]
    rows_dev = field.shape[2]
    length_total = field.shape[3]
    row_devices = lax.axis_size("row")
    depth_devices = lax.axis_size("depth")
    row_index = lax.axis_index("row")
    depth_index = lax.axis_index("depth")
    cols_dev = length_total // row_devices
    rows_piece = rows_dev // depth_devices
    plane_total = planes_dev * depth_devices
    forward_tables = dft_tables(length_total, False)
    inverse_tables = dft_tables(length_total, True)
    phase_table = transfer_phase(defocus, length_total, row_index * cols_dev, cols_dev)
    cosine_table = jnp.cos(phase_table)
    sine_table = jnp.sin(phase_table)
    hologram_part = lax.dynamic_slice_in_dim(hologram, depth_index * rows_piece, rows_piece, 0)
    estimate = field
    spectrum = transform_last(estimate, forward_tables, False, False)
    spectrum = lax.all_to_all(spectrum, "row", split_axis=3, concat_axis=2, tiled=True)
    spectrum = transform_rows(spectrum, forward_tables)
    sum_real = jnp.sum(spectrum[0] * cosine_table + spectrum[1] * sine_table, axis=0)
    sum_imag = jnp.sum(spectrum[1] * cosine_table - spectrum[0] * sine_table, axis=0)
    summed = transform_rows(jnp.stack([sum_real, sum_imag]), inverse_tables)
    by_rows = lax.all_to_all(summed, "row", split_axis=1, concat_axis=2, tiled=True)
    image_part = transform_last(by_rows, inverse_tables, False, True)
    image_sum = lax.psum_scatter(image_part, "depth", scatter_dimension=0, tiled=True)
    misfit = image_sum - hologram_part
    misfit_block = lax.all_gather(misfit, "depth", axis=0, tiled=True)
    misfit_pair = transform_last(misfit_block, forward_tables, True, False)
    misfit_spec = lax.all_to_all(misfit_pair, "row", split_axis=2, concat_axis=1, tiled=True)
    misfit_spec = transform_rows(misfit_spec, forward_tables)
    adj_real = misfit_spec[0][None] * cosine_table - misfit_spec[1][None] * sine_table
    adj_imag = misfit_spec[0][None] * sine_table + misfit_spec[1][None] * cosine_table
    adjoint = transform_rows(jnp.stack([adj_real, adj_imag]), inverse_tables)
    adjoint = lax.all_to_all(adjoint, "row", split_axis=2, concat_axis=3, tiled=True)
    gradient = transform_last(adjoint, inverse_tables, False, False)
    moved_field = estimate - 1.0 / plane_total * gradient
    estimate = shrink_shifts(moved_field, depth_index, row_index, plane_total, length_total)
    return estimate


def solution(mesh):
    return jax.shard_map(
        per_device,
        mesh=mesh,
        in_specs=(P(None, "depth", "row", None), P("row", None), P("depth")),
        out_specs=P(None, "depth", "row", None),
        check_vma=False,
    )
```

profile of v0, /device:TPU:2, one launch (start us, length us, event | category | flops | bytes accessed | tf_op | source)
XLA Modules:
  0.0 1047.4 jit_solution(16027976916007795739)
XLA Ops:
  12.7 17.3 %fusion.100 = (f32[1,64,64,64]{2,3,0,1:T(8,128)S(1)}, f32[1,64,64,64]{2,3,0,1:T(8,128)}, f32[1,64,64,64]{2,3,0,1:T(8,128)}, f32[1,64,64,64]{2,3,0,1:T(8,128)}, f...) fusion(s32[64,64]{0,1:T(8,128)S(1)} %broadcast_multiply_fusion.3, s32[64,64]{1,0:T(8,128)S(1)} %copy.91), kind=kLoop, calls=%fused_computation.103 | loop fusion | flops 4980736 | bytes 6324224 | tf_op jit(solution)/shard_map/neg | solution.py:29
  38.1 11.0 %fusion.46 = f32[2,1,128,64,64]{2,3,0,4,1:T(8,128)S(1)} fusion(f32[1,2,64,64,64]{3,4,1,0,2:T(8,128)S(1)} %get-tuple-element.13, f32[1,2,64,64,64]{3,4,1,0,2:T(8,128)S(1)} %get-tuple-element.12, f32[2,128,64,64,1]{1,2,3,0,4:T(8,128)S(1)} %fusion.43), kind=kOutput, calls=%fused_computation.64 | convolution fusion | flops 1611661312 | bytes 12582912 | tf_op jit(solution)/shard_map/rqkbm,q...kb->r...mk/dot_general | solution.py:50
  51.6 16.2 %copy.95 = f32[2,1,128,4096]{2,0,1,3:T(2,128)} copy(f32[2,1,128,4096]{2,3,0,1:T(8,128)S(1)} %bitcast.244) | data formatting | bytes 8388608 | tf_op jit(solution)/shard_map/reshape | solution.py:66
  67.8 10.5 %all-to-all-start = ((f32[2,1,128,4096]{2,0,1,3:T(2,128)}), f32[2,1,128,4096]{2,0,1,3:T(2,128)}, u32[]{:S(2)}, u32[]{:S(2)}) async-start(f32[2,1,128,4096]{2,0,1,3:T(2,128)} %copy.95), calls=%async_computation | async-start | bytes 8388608 | tf_op jit(solution)/shard_map/all_to_all | solution.py:169
  88.1 87.1 %all-to-all-done = f32[2,1,128,4096]{2,0,1,3:T(2,128)} async-done(((f32[2,1,128,4096]{2,0,1,3:T(2,128)}), f32[2,1,128,4096]{2,0,1,3:T(2,128)}, u32[]{:S(2)}, u32[]{:S(2)}) %all-to-all-start) | async-done | bytes 4194336 | tf_op jit(solution)/shard_map/all_to_all | solution.py:169
  194.2 10.0 fusion.52
  216.4 10.4 fusion.76
  229.2 15.6 %copy.105 = f32[2,4096,128]{2,0,1:T(2,128)S(1)} copy(f32[2,4096,128]{2,1,0:T(8,128)S(1)} %bitcast.247) | data formatting | bytes 8388608 | tf_op jit(solution)/shard_map/reshape | solution.py:79
  244.8 103.6 %all_to_all.60 = f32[2,4096,128]{2,0,1:T(2,128)S(1)} all-to-all(f32[2,4096,128]{2,0,1:T(2,128)S(1)} %copy.105), channel_id=1, replica_groups=mesh['depth'=8,'row'=32] {'row'}, dimensions={1} | all-to-all | bytes 8388608 | tf_op jit(solution)/shard_map/all_to_all | solution.py:174
  356.4 8.8 fusion.58
  377.9 40.2 %reduce-scatter.4.cloned.1.call-done = f32[16,4096]{1,0:T(8,128)} async-done(((f32[128,4096]{1,0:T(8,128)}), f32[16,4096]{1,0:T(8,128)}) %reduce-scatter.4.cloned.1.call-update) | async-done | bytes 262160
  427.1 43.0 %all-gather.2.cloned.1.call-done = f32[128,4096]{1,0:T(8,128)} async-done(((f32[16,4096]{1,0:T(8,128)}), f32[128,4096]{1,0:T(8,128)}) %all-gather.2.cloned.1.call-update) | async-done | bytes 2097168 | tf_op jit(solution)/shard_map/all_gather | solution.py:178
  477.0 12.6 %fusion.61 = f32[2,128,64,64]{1,2,0,3:T(8,128)S(1)} fusion(f32[1,2,64,64,64]{3,4,1,0,2:T(8,128)} %copy-done.6, f32[1,2,64,64,64]{3,4,1,0,2:T(8,128)S(1)} %copy-done.4, f32[2,128,64,64,1]{1,2,0,3,4:T(8,128)S(1)} %convolution_bitcast_fusion), kind=kOutput, calls=%fused_computation.69 | convolution fusion | flops 1611661312 | bytes 12582912 | tf_op jit(solution)/shard_map/rqkbm,q...kb->r...mk/dot_general | solution.py:50
  492.0 15.6 %copy.117 = f32[2,128,4096]{1,0,2:T(2,128)S(1)} copy(f32[2,128,4096]{1,2,0:T(8,128)S(1)} %bitcast.250) | data formatting | bytes 8388608 | tf_op jit(solution)/shard_map/reshape | solution.py:66
  507.7 106.3 %all_to_all.61 = f32[2,128,4096]{1,0,2:T(2,128)S(1)} all-to-all(f32[2,128,4096]{1,0,2:T(2,128)S(1)} %copy.117), channel_id=1, replica_groups=mesh['depth'=8,'row'=32] {'row'}, dimensions={2} | all-to-all | bytes 8388608 | tf_op jit(solution)/shard_map/all_to_all | solution.py:180
  630.6 10.0 fusion.67
  653.0 10.4 fusion.81
  665.8 15.6 %copy.127 = f32[2,1,4096,128]{3,0,1,2:T(2,128)S(1)} copy(f32[2,1,4096,128]{3,2,0,1:T(8,128)S(1)} %bitcast.252) | data formatting | bytes 8388608 | tf_op jit(solution)/shard_map/reshape | solution.py:79
  681.5 101.2 %all_to_all.62 = f32[2,1,4096,128]{3,0,1,2:T(2,128)S(1)} all-to-all(f32[2,1,4096,128]{3,0,1,2:T(2,128)S(1)} %copy.127), channel_id=1, replica_groups=mesh['depth'=8,'row'=32] {'row'}, dimensions={2} | all-to-all | bytes 8388608 | tf_op jit(solution)/shard_map/all_to_all | solution.py:185
  799.4 10.0 fusion.11
  835.8 71.5 %collective-permute-done = f32[2,1,128,4096]{2,3,0,1:T(8,128)} collective-permute-done((f32[2,1,128,4096]{2,3,0,1:T(8,128)}, f32[2,1,128,4096]{2,3,0,1:T(8,128)}, u32[]{:S(2)}, u32[]{:S(2)}) %collective-permute-start) | collective-permute-done | bytes 4194336 | tf_op jit(solution)/shard_map/ppermute | solution.py:15
  907.3 9.1 add_reduce_fusion
  938.6 81.9 %collective-permute-done.2 = f32[2,1,128,4096]{2,3,0,1:T(8,128)} collective-permute-done((f32[2,1,128,4096]{2,3,0,1:T(8,128)}, f32[2,1,128,4096]{2,3,0,1:T(8,128)}, u32[]{:S(2)}, u32[]{:S(2)}) %collective-permute-start.2) | collective-permute-done | bytes 4194336 | tf_op jit(solution)/shard_map/ppermute | solution.py:15
  1020.5 14.0 %fusion.10 = f32[2,1,128,4096]{2,3,0,1:T(8,128)} fusion(f32[2,1,128,4096]{2,3,0,1:T(8,128)} %bitcast_subtract_fusion, f32[2,1,128,4096]{2,3,0,1:T(8,128)} %copy-done.9, f32[2,1,127,4096]{2,3,0,1:T(8,128)} %bitcast.239, f32[2,1,1,4096]{2,3,0,1:T(8,128)} %copy.138, f32[2,1,128,4096]{2,3,0,1:T(8,128)} %get-tuple-element.7, f32[2,1,128,4095]{2,3,0,1:T(8,128)} %bitcast.240, ...), kind=kLoop, calls=%fused_computation.21 | loop fusion | flops 8388608 | bytes 33553408 | tf_op jit(solution)/shard_map/add | solution.py:147
  (114 shorter events, 200.4 us)
Async XLA Ops:
  6.5 370.7 %copy-start = (f32[128,4096]{1,0:T(8,128)S(1)}, f32[128,4096]{1,0:T(8,128)}, u32[]{:S(2)}) copy-start(f32[128,4096]{1,0:T(8,128)} %param.4) | copy-start | bytes 6291460
  31.7 6.4 copy-start.2
  31.7 6.4 copy-start.6
  67.8 107.4 %all-to-all-start = ((f32[2,1,128,4096]{2,0,1,3:T(2,128)}), f32[2,1,128,4096]{2,0,1,3:T(2,128)}, u32[]{:S(2)}, u32[]{:S(2)}) async-start(f32[2,1,128,4096]{2,0,1,3:T(2,128)} %copy.95), calls=%async_computation | async-start | bytes 8388608 | tf_op jit(solution)/shard_map/all_to_all | solution.py:169
  78.4 339.8 %reduce-scatter.4.cloned.1.call-start = ((), (), s32[]{:S(2)}) async-start(), calls=%async_computation.6 | async-start | bytes 2359296
  185.3 8.8 copy-start.3
  185.3 8.8 copy-start.7
  356.4 8.8 copy-start.21
  356.4 8.8 copy-start.22
  377.2 92.9 %all-gather.2.cloned.1.call-start = ((), (), s32[]{:S(2)}) async-start(), calls=%async_computation.5 | async-start | bytes 2359296 | tf_op jit(solution)/shard_map/all_gather | solution.py:178
  472.2 4.8 copy-start.4
  621.9 8.7 copy-start.5
  621.9 8.7 copy-start.8
  648.9 4.1 copy-start.11
  648.9 4.1 copy-start.14
  790.6 8.8 copy-start.12
  790.6 8.8 copy-start.15
  814.5 92.8 %collective-permute-start = (f32[2,1,128,4096]{2,3,0,1:T(8,128)}, f32[2,1,128,4096]{2,3,0,1:T(8,128)}, u32[]{:S(2)}, u32[]{:S(2)}) collective-permute-start(f32[2,1,128,4096]{2,3,0,1:T(8,128)} %bitcast_subtract_fusion), channel_id=1, source_target_pairs={{32,0},{64,32},{96,64},{128,96},{160,128},{192,160},{224,192},{33,... | collective-permute-start | bytes 12582920 | tf_op jit(solution)/shard_map/ppermute | solution.py:15
  821.3 11.9 %collective-permute-start.1 = (f32[2,1,1,4096]{3,0,2,1:T(2,128)S(1)}, f32[2,1,1,4096]{3,0,2,1:T(2,128)S(1)}, u32[]{:S(2)}, u32[]{:S(2)}) collective-permute-start(f32[2,1,1,4096]{3,0,2,1:T(2,128)S(1)} %copy.135), channel_id=1, source_target_pairs={{1,0},{2,1},{3,2},{4,3},{5,4},{6,5},{7,6},{8,7},{9,8},{10,9},{11,1... | collective-permute-start | bytes 98312 | tf_op jit(solution)/shard_map/ppermute | solution.py:15
  907.3 9.9 copy-start.19
  907.3 9.9 copy-start.20
  925.9 94.7 %collective-permute-start.2 = (f32[2,1,128,4096]{2,3,0,1:T(8,128)}, f32[2,1,128,4096]{2,3,0,1:T(8,128)}, u32[]{:S(2)}, u32[]{:S(2)}) collective-permute-start(f32[2,1,128,4096]{2,3,0,1:T(8,128)} %get-tuple-element.5), channel_id=1, source_target_pairs={{0,32},{32,64},{64,96},{96,128},{128,160},{160,192},{192,224},{1,3... | collective-permute-start | bytes 12582920 | tf_op jit(solution)/shard_map/ppermute | solution.py:15
  933.8 2.1 collective-permute-start.3
  1020.5 19.6 %copy-start.1 = (f32[128,4096]{1,0:T(8,128)S(1)}, f32[128,4096]{1,0:T(8,128)}, u32[]{:S(2)}) copy-start(f32[128,4096]{1,0:T(8,128)} %param.4) | copy-start | bytes 6291460
  (6 other events, 16.9 us)
Sparse Core Ops, SparseCore 0:
  377.3 40.7 reduce-scatter.3
  427.3 42.7 all-gather.1
where the time goes:
time: 1060 us; the launch traced here: 1050 us
  waiting for transfers between devices  325 us (31%)
  blocking collectives  311 us (29%)
  local copies, waits for them, and re-layouts  162 us (15%)
  matrix products  134 us (13%)
  other arithmetic  81.5 us (8%)
  starting transfers between devices  19.1 us (2%)
  between operations  15 us (1%)
    ppermute x4, waiting for transfers between devices, passed_along(): return lax.ppermute(block, axis, route)  154 us
    dot_general x16, matrix products, contract(): jnp.einsum(formula, table, data, precision=lax.Precision.HIGHEST, preferr...  134 us
    all_to_all x1, blocking collectives, per_device(): lax.all_to_all(misfit_pair, 'row', split_axis=2, concat_axis=1, tiled=True)  106 us
    all_to_all x1, blocking collectives, per_device(): lax.all_to_all(summed, 'row', split_axis=1, concat_axis=2, tiled=True)  104 us
    all_to_all x1, blocking collectives, per_device(): lax.all_to_all(adjoint, 'row', split_axis=2, concat_axis=3, tiled=True)  101 us
    all_to_all x1, waiting for transfers between devices, per_device(): lax.all_to_all(spectrum, 'row', split_axis=3, concat_axis=2, tiled=True)  87.1 us
    all_gather x1, waiting for transfers between devices, per_device(): misfit_block = lax.all_gather(misfit, 'depth', axis=0, tiled=True)  43 us
    unnamed x3, waiting for transfers between devices  40.3 us
  transfers between devices with their start and end apart: 7, of which 6 were waited for; matrix products, arithmetic and copies ran while one was open for 3% of the time, Pallas kernels for 0%

commit v1 on v0

v1 whole, which is shorter than its diff:
```python
import functools
import math

import jax
import jax.numpy as jnp
import ml_dtypes
import numpy as np
from jax import lax
from jax.experimental import pallas as pl
from jax.experimental.pallas import tpu as pltpu
from jax.sharding import Mesh
from jax.sharding import PartitionSpec as P

tv_step_size = 1.0 / 12.0
tv_sharpness = 0.25

N = 4096
RADIX = 16
INNER = 256
CLASSES = 9
PLANES = 8
LANES = 128
F32 = jnp.float32
BF16 = jnp.bfloat16

DEPTH = ("x_lo", "y")
ROW = ("x_hi", "z", "core")
LAYER = ("x_lo", "y", "x_hi", "core")


def split_table(table):
    high = table.astype(ml_dtypes.bfloat16)
    low = (table - high.astype(np.float64)).astype(ml_dtypes.bfloat16)
    return high, low


def inner_tables():
    index = np.arange(INNER)
    angle = 2.0 * np.pi * (np.outer(index, index) % INNER) / INNER
    cosine, sine = np.cos(angle), np.sin(angle)
    tables = []
    for sign in (1.0, -1.0):
        whole = np.block([[cosine, -sign * sine], [sign * sine, cosine]])
        high, low = split_table(whole)
        tables.append(np.concatenate([high, high, low], axis=0))
    return tables


def twiddles():
    angle = 2.0 * np.pi * np.outer(np.arange(RADIX), np.arange(INNER)) / N
    return np.stack([np.cos(angle), np.sin(angle)]).astype(np.float32)


def class_frequencies():
    return (RADIX * np.arange(INNER)[None, :] + np.arange(CLASSES)[:, None]) % N


def class_tables():
    freq = class_frequencies()
    angle = 2.0 * np.pi * ((freq[:, :, None] * np.arange(INNER)[None, None, :]) % N) / N
    table = np.concatenate([np.cos(angle), np.sin(angle)], axis=1)
    high, low = split_table(table)
    forward = np.concatenate([high, high, low], axis=2)
    high, low = split_table(np.swapaxes(table, 1, 2))
    backward = np.concatenate([high, high, low], axis=2)
    return forward, backward


def squares_of(index):
    centred = np.where(index < N // 2, index, index - N)
    return (centred * centred).astype(np.float32)


def dft4(values, inverse):
    (ar, ai), (br, bi), (cr, ci), (dr, di) = values
    s0r, s0i, s1r, s1i = ar + cr, ai + ci, ar - cr, ai - ci
    s2r, s2i, s3r, s3i = br + dr, bi + di, br - dr, bi - di
    plus = (s1r - s3i, s1i + s3r)
    minus = (s1r + s3i, s1i - s3r)
    first, third = (plus, minus) if inverse else (minus, plus)
    return [(s0r + s2r, s0i + s2i), first, (s0r - s2r, s0i - s2i), third]


def times_constant(value, cosine, sine):
    real, imag = value
    if abs(sine) < 1e-9 and abs(cosine - 1.0) < 1e-9:
        return value
    if abs(cosine) < 1e-9 and abs(sine - 1.0) < 1e-9:
        return (-imag, real)
    if abs(cosine) < 1e-9 and abs(sine + 1.0) < 1e-9:
        return (imag, -real)
    if abs(abs(cosine) - abs(sine)) < 1e-9:
        root = math.sqrt(0.5)
        sc, ss = math.copysign(1.0, cosine), math.copysign(1.0, sine)
        first = (real if sc > 0 else -real) - (imag if ss > 0 else -imag)
        second = (imag if sc > 0 else -imag) + (real if ss > 0 else -real)
        return (first * root, second * root)
    return (real * cosine - imag * sine, imag * cosine + real * sine)


def dft16(values, inverse):
    direction = 1.0 if inverse else -1.0
    stage = [dft4([values[4 * n1 + n2] for n1 in range(4)], inverse) for n2 in range(4)]
    result = [None] * 16
    for k1 in range(4):
        column = []
        for n2 in range(4):
            angle = direction * 2.0 * math.pi * n2 * k1 / 16
            column.append(times_constant(stage[n2][k1], math.cos(angle), math.sin(angle)))
        for k2, value in enumerate(dft4(column, inverse)):
            result[k1 + 4 * k2] = value
    return result


def weighted_sum(terms):
    total = None
    for coefficient, value in terms:
        if abs(coefficient) < 1e-9:
            continue
        if abs(coefficient - 1.0) < 1e-9:
            total = value if total is None else total + value
        elif abs(coefficient + 1.0) < 1e-9:
            total = -value if total is None else total - value
        else:
            piece = value * float(np.float32(coefficient))
            total = piece if total is None else total + piece
    return total


def real_dft16(blocks):
    sums = [blocks[0]] + [blocks[b] + blocks[16 - b] for b in range(1, 8)] + [blocks[8]]
    diffs = [None] + [blocks[b] - blocks[16 - b] for b in range(1, 8)]
    result = []
    for k in range(CLASSES):
        real = weighted_sum([(math.cos(2 * math.pi * k * b / 16), sums[b]) for b in range(9)])
        if k in (0, 8):
            imag = jnp.zeros_like(real)
        else:
            imag = weighted_sum(
                [(-math.sin(2 * math.pi * k * b / 16), diffs[b]) for b in range(1, 8)]
            )
        result.append((real, imag))
    return result


def real_inverse16(values):
    result = [None] * 16
    for b in range(9):
        even = weighted_sum([(math.cos(2 * math.pi * k * b / 16), values[k][0]) for k in range(9)])
        if b in (0, 8):
            result[b] = even
        else:
            odd = weighted_sum(
                [(math.sin(2 * math.pi * k * b / 16), values[k][1]) for k in range(1, 8)]
            )
            result[b] = even - odd
            result[16 - b] = even + odd
    return result


def halves(value):
    high = value.astype(BF16)
    low = (value - high.astype(F32)).astype(BF16)
    return high, low


STEP_ROWS = 32
CHUNK_CLASSES = 8


def filter_rows(load, store, tw_ref, d_ref, wf_ref, wi_ref, x_ref):
    groups = [(r, h) for r in range(STEP_ROWS // 8) for h in range(INNER // LANES)]
    for r, h in groups:
        values = [load(r, b * (INNER // LANES) + h) for b in range(RADIX)]
        lanes = slice(h * LANES, (h + 1) * LANES)
        for k, (real, imag) in enumerate(dft16(values, False)):
            if k:
                cosine, sine = tw_ref[0, k : k + 1, lanes], tw_ref[1, k : k + 1, lanes]
                real, imag = real * cosine + imag * sine, imag * cosine - real * sine
            rows = slice(k * STEP_ROWS + 8 * r, k * STEP_ROWS + 8 * r + 8)
            x_ref[rows, lanes] = real
            x_ref[rows, INNER + h * LANES : INNER + (h + 1) * LANES] = imag
    for chunk in range(RADIX // CHUNK_CLASSES):
        base = chunk * CHUNK_CLASSES * STEP_ROWS
        rows = slice(base, base + CHUNK_CLASSES * STEP_ROWS)
        high, low = halves(x_ref[rows, :])
        spectrum = jnp.dot(
            jnp.concatenate([high, low, high], axis=1), wf_ref[...], preferred_element_type=F32
        )
        pieces = []
        for kk in range(CHUNK_CLASSES):
            k = chunk * CHUNK_CLASSES + kk
            cosine, sine = d_ref[0, k : k + 1, :], d_ref[1, k : k + 1, :]
            real = spectrum[kk * STEP_ROWS : (kk + 1) * STEP_ROWS, :INNER]
            imag = spectrum[kk * STEP_ROWS : (kk + 1) * STEP_ROWS, INNER:]
            pieces.append(
                jnp.concatenate(
                    [real * cosine - imag * sine, imag * cosine + real * sine], axis=1
                )
            )
        high, low = halves(jnp.concatenate(pieces, axis=0))
        x_ref[rows, :] = jnp.dot(
            jnp.concatenate([high, low, high], axis=1), wi_ref[...], preferred_element_type=F32
        )
    for r, h in groups:
        lanes = slice(h * LANES, (h + 1) * LANES)
        values = []
        for k in range(RADIX):
            rows = slice(k * STEP_ROWS + 8 * r, k * STEP_ROWS + 8 * r + 8)
            real = x_ref[rows, lanes]
            imag = x_ref[rows, INNER + h * LANES : INNER + (h + 1) * LANES]
            if k:
                cosine, sine = tw_ref[0, k : k + 1, lanes], tw_ref[1, k : k + 1, lanes]
                real, imag = real * cosine - imag * sine, imag * cosine + real * sine
            values.append((real, imag))
        for b, value in enumerate(dft16(values, True)):
            store(r, b * (INNER // LANES) + h, value)


def forward_x_kernel(f_ref, hol_ref, tw_ref, d_ref, wf_ref, wi_ref, o_ref, x_ref):
    step = pl.program_id(0)

    @pl.when(step == 0)
    def _():
        for j in range(32):
            o_ref[j, 256:272, :] = hol_ref[:, j * LANES : (j + 1) * LANES]

    def load(r, j):
        rows, lanes = slice(8 * r, 8 * r + 8), slice(j * LANES, (j + 1) * LANES)
        return f_ref[0, rows, lanes], f_ref[1, rows, lanes]

    def store(r, j, value):
        for c in range(2):
            start = pl.multiple_of(step * STEP_ROWS + 128 * c + 8 * r, 8)
            o_ref[j, pl.ds(start, 8), :] = value[c]

    filter_rows(load, store, tw_ref, d_ref, wf_ref, wi_ref, x_ref)


def backward_x_kernel(g_ref, f_ref, tw_ref, d_ref, wf_ref, wi_ref, o_ref, x_ref):
    def load(r, j):
        rows = slice(8 * r, 8 * r + 8)
        return g_ref[j, 0, rows, :], g_ref[j, 1, rows, :]

    def store(r, j, value):
        rows, lanes = slice(8 * r, 8 * r + 8), slice(j * LANES, (j + 1) * LANES)
        for c in range(2):
            o_ref[c, rows, lanes] = f_ref[c, rows, lanes] + value[c]

    filter_rows(load, store, tw_ref, d_ref, wf_ref, wi_ref, x_ref)


def whole(shape):
    return pl.BlockSpec(shape, lambda *_: (0,) * len(shape))


def params():
    return pltpu.CompilerParams(vmem_limit_bytes=56 << 20)


def x_tables():
    forward, inverse = inner_tables()
    return jnp.asarray(twiddles()), jnp.asarray(forward), jnp.asarray(inverse)


def forward_x(field, hologram_rows, transfer):
    tw, wf, wi = x_tables()
    return pl.pallas_call(
        forward_x_kernel,
        grid=(128 // STEP_ROWS,),
        in_specs=[
            pl.BlockSpec((2, STEP_ROWS, N), lambda i: (0, i, 0)),
            whole((16, N)),
            whole((2, RADIX, INNER)),
            whole((2, RADIX, INNER)),
            whole((1536, 512)),
            whole((1536, 512)),
        ],
        out_specs=whole((32, 272, LANES)),
        out_shape=jax.ShapeDtypeStruct((32, 272, LANES), F32),
        scratch_shapes=[pltpu.VMEM((RADIX * STEP_ROWS, 2 * INNER), F32)],
        compiler_params=params(),
        name="filter_x_forward",
    )(field, hologram_rows, tw, transfer, wf, wi)


def backward_x(gradient, field, transfer):
    tw, wf, wi = x_tables()
    return pl.pallas_call(
        backward_x_kernel,
        grid=(128 // STEP_ROWS,),
        in_specs=[
            pl.BlockSpec((32, 2, STEP_ROWS, LANES), lambda i: (0, 0, i, 0)),
            pl.BlockSpec((2, STEP_ROWS, N), lambda i: (0, i, 0)),
            whole((2, RADIX, INNER)),
            whole((2, RADIX, INNER)),
            whole((1536, 512)),
            whole((1536, 512)),
        ],
        out_specs=pl.BlockSpec((2, STEP_ROWS, N), lambda i: (0, i, 0)),
        out_shape=jax.ShapeDtypeStruct((2, 128, N), F32),
        scratch_shapes=[pltpu.VMEM((RADIX * STEP_ROWS, 2 * INNER), F32)],
        compiler_params=params(),
        name="filter_x_backward",
    )(gradient, field, tw, transfer, wf, wi)


def forward_y_kernel(z_ref, g_ref, t_ref, tt_ref, cs_ref, o_ref, u_ref, s_ref):
    step = pl.program_id(0)

    @pl.when(step == 0)
    def _():
        @pl.loop(0, PLANES)
        def _(p):
            for core in range(2):
                for c in range(2):
                    rows = slice(c * 128, (c + 1) * 128)
                    upper = g_ref[p * 4 + core, rows, :]
                    lower = g_ref[p * 4 + 2 + core, rows, :]
                    for parity, value in ((0, upper + lower), (1, upper - lower)):
                        high, low = halves(value)
                        for part, piece in ((0, high), (1, low), (2, high)):
                            start = part * INNER + core * 128
                            u_ref[parity, p, start : start + 128, c * LANES : (c + 1) * LANES] = (
                                piece
                            )

    parity = lax.rem(step, 2)
    chunks = []
    for half in range(2):
        rows = slice(half * INNER, (half + 1) * INNER)
        total = None
        for p in range(PLANES):
            result = jnp.dot(t_ref[0, rows, :], u_ref[parity, p], preferred_element_type=F32)
            piece = (
                cs_ref[0, :, 2 * p : 2 * p + 1] * result[:, :LANES]
                + cs_ref[0, :, 2 * p + 1 : 2 * p + 2] * result[:, LANES:]
            )
            total = piece if total is None else total + piece
        chunks.append(total)
    cosine, sine = chunks
    pair = jnp.concatenate(
        [jnp.concatenate([cosine, sine], axis=0), jnp.concatenate([-sine, cosine], axis=0)], axis=1
    )
    high, low = halves(pair)
    s_ref[step] = jnp.dot(
        tt_ref[0], jnp.concatenate([high, low, high], axis=0), preferred_element_type=F32
    )

    @pl.when(step == CLASSES - 1)
    def _():
        shift = z_ref[0]

        @pl.loop(0, INNER // 8)
        def _(i):
            rows = pl.ds(pl.multiple_of(i * 8, 8), 8)
            values = [(s_ref[k, rows, :LANES], s_ref[k, rows, LANES:]) for k in range(CLASSES)]
            for b, value in enumerate(real_inverse16(values)):
                block = lax.rem(shift + b, 16)
                o_ref[lax.rem(block, 8), lax.div(block, 8), rows, :] = value


def forward_y(z_index, received, factors):
    forward, backward = class_tables()
    return pl.pallas_call(
        forward_y_kernel,
        grid=(CLASSES,),
        in_specs=[
            pl.BlockSpec(memory_space=pltpu.SMEM),
            whole((32, 272, LANES)),
            pl.BlockSpec((1, 512, 768), lambda k: (k, 0, 0)),
            pl.BlockSpec((1, 256, 1536), lambda k: (k, 0, 0)),
            pl.BlockSpec((1, 256, 16), lambda k: (k, 0, 0)),
        ],
        out_specs=whole((8, 2, INNER, LANES)),
        out_shape=jax.ShapeDtypeStruct((8, 2, INNER, LANES), F32),
        scratch_shapes=[
            pltpu.VMEM((2, PLANES, 768, 2 * LANES), BF16),
            pltpu.VMEM((CLASSES, INNER, 2 * LANES), F32),
        ],
        compiler_params=params(),
        name="filter_y_forward",
    )(z_index, received, jnp.asarray(forward), jnp.asarray(backward), factors)


def backward_y_kernel(z_ref, m_ref, t_ref, tt_ref, cs_ref, o_ref, x_ref, a_ref):
    step = pl.program_id(0)

    @pl.when(step == 0)
    def _():
        shift = z_ref[0]

        @pl.loop(0, INNER // 8)
        def _(i):
            rows = pl.ds(pl.multiple_of(i * 8, 8), 8)
            blocks = []
            for b in range(16):
                block = lax.rem(shift + b, 16)
                blocks.append(m_ref[lax.rem(block, 8), lax.div(block, 8), rows, :])
            for k, (real, imag) in enumerate(real_dft16(blocks)):
                x_ref[k, rows, :LANES] = real
                x_ref[k, rows, LANES:] = imag

        @pl.loop(0, PLANES)
        def _(p):
            for parity in range(2):
                a_ref[parity, p] = jnp.zeros((INNER, 2 * LANES), F32)

    parity = lax.rem(step, 2)
    high, low = halves(x_ref[step])
    mixed = jnp.dot(
        t_ref[0], jnp.concatenate([high, low, high], axis=0), preferred_element_type=F32
    )
    cosine = mixed[:INNER, :LANES] + mixed[INNER:, LANES:]
    sine = mixed[INNER:, :LANES] - mixed[:INNER, LANES:]
    for p in range(PLANES):
        first = cs_ref[0, :, 2 * p : 2 * p + 1]
        second = cs_ref[0, :, 2 * p + 1 : 2 * p + 2]
        product = jnp.concatenate(
            [
                jnp.concatenate([first * cosine, second * cosine], axis=1),
                jnp.concatenate([first * sine, second * sine], axis=1),
            ],
            axis=0,
        )
        high, low = halves(product)
        a_ref[parity, p] += jnp.dot(
            tt_ref[0], jnp.concatenate([high, low, high], axis=0), preferred_element_type=F32
        )

    @pl.when(step == CLASSES - 1)
    def _():
        @pl.loop(0, PLANES)
        def _(p):
            for core in range(2):
                rows = slice(core * 128, (core + 1) * 128)
                for c in range(2):
                    lanes = slice(c * LANES, (c + 1) * LANES)
                    even, odd = a_ref[0, p, rows, lanes], a_ref[1, p, rows, lanes]
                    o_ref[p * 4 + core, c] = even + odd
                    o_ref[p * 4 + 2 + core, c] = even - odd


def backward_y(z_index, misfit, factors):
    forward, backward = class_tables()
    return pl.pallas_call(
        backward_y_kernel,
        grid=(CLASSES,),
        in_specs=[
            pl.BlockSpec(memory_space=pltpu.SMEM),
            whole((8, 2, INNER, LANES)),
            pl.BlockSpec((1, 512, 768), lambda k: (k, 0, 0)),
            pl.BlockSpec((1, 256, 1536), lambda k: (k, 0, 0)),
            pl.BlockSpec((1, 256, 16), lambda k: (k, 0, 0)),
        ],
        out_specs=whole((32, 2, 128, LANES)),
        out_shape=jax.ShapeDtypeStruct((32, 2, 128, LANES), F32),
        scratch_shapes=[
            pltpu.VMEM((CLASSES, INNER, 2 * LANES), F32),
            pltpu.VMEM((2, PLANES, INNER, 2 * LANES), F32),
        ],
        compiler_params=params(),
        name="filter_y_backward",
    )(z_index, misfit, jnp.asarray(forward), jnp.asarray(backward), factors)


def moved_along(block, axes, distance, size):
    route = [(i - distance, i) for i in range(size) if 0 <= i - distance < size]
    return lax.ppermute(block, axes, route)


def diagonal(block, depth_distance, row_distance):
    route = []
    for depth in range(8):
        for row in range(32):
            from_depth, from_row = depth - depth_distance, row - row_distance
            if 0 <= from_depth < 8 and 0 <= from_row < 32:
                route.append((from_depth * 32 + from_row, depth * 32 + row))
    return lax.ppermute(block, DEPTH + ROW, route)


def flux_of(here, ahead, below, has_ahead, has_below):
    depth_diff = jnp.where(has_ahead, ahead - here, 0.0)
    row_diff = jnp.where(has_below, below - here, 0.0)
    col_diff = jnp.concatenate([here[..., 1:], here[..., -1:]], axis=-1) - here
    magnitude = jnp.sqrt(
        jnp.sum(depth_diff * depth_diff + row_diff * row_diff + col_diff * col_diff, axis=0)
    )
    factor = 1.0 / (1.0 + tv_sharpness * magnitude)
    return depth_diff * factor, row_diff * factor, col_diff * factor


def shrink(moved, depth_index, row_index):
    ahead = moved_along(moved, DEPTH, -1, 8)
    behind = moved_along(moved, DEPTH, 1, 8)
    first, last = moved[:, :1], moved[:, -1:]
    above = moved_along(last, ROW, 1, 32)
    below = moved_along(first, ROW, -1, 32)
    ahead_above = diagonal(last, -1, 1)
    behind_below = diagonal(first, 1, -1)
    has_ahead = depth_index < 7
    has_behind = depth_index > 0
    row_ids = row_index * 128 + jnp.arange(128, dtype=jnp.int32)[None, :, None]
    has_below = row_ids < N - 1
    shifted = jnp.concatenate([moved[:, 1:], below], axis=1)
    flux_z, flux_y, flux_x = flux_of(moved, ahead, shifted, has_ahead, has_below)
    _, above_y, _ = flux_of(above, ahead_above, first, has_ahead, True)
    above_y = jnp.where(row_index > 0, above_y, 0.0)
    behind_shifted = jnp.concatenate([behind[:, 1:], behind_below], axis=1)
    behind_z, _, _ = flux_of(behind, moved, behind_shifted, True, has_below)
    behind_z = jnp.where(has_behind, behind_z, 0.0)
    divergence = (
        flux_z
        - behind_z
        + flux_y
        - jnp.concatenate([above_y, flux_y[:, :-1]], axis=1)
        + flux_x
        - jnp.concatenate([jnp.zeros_like(flux_x[..., :1]), flux_x[..., :-1]], axis=-1)
    )
    return moved + tv_step_size * divergence


def phase_of(depth_values, squares):
    return depth_values * (squares * (math.pi / (N * N)))


def per_device(field, hologram, defocus):
    x_lo, y = lax.axis_index("x_lo"), lax.axis_index("y")
    x_hi, z, core = lax.axis_index("x_hi"), lax.axis_index("z"), lax.axis_index("core")
    depth_index = x_lo * 4 + y
    row_index = x_hi * 16 + z * 2 + core
    z_index = z[None].astype(jnp.int32)
    field = field[:, 0]

    x_freq = RADIX * np.arange(INNER)[None, :] + np.arange(RADIX)[:, None]
    x_phase = phase_of(defocus[0], jnp.asarray(squares_of(x_freq)))
    x_cos, x_sin = jnp.cos(x_phase) / N, jnp.sin(x_phase) / N
    x_forward = jnp.stack([x_cos, -x_sin])
    x_backward = jnp.stack([x_cos, x_sin]) * (-1.0 / PLANES)

    depths = lax.all_gather(defocus, DEPTH, tiled=True)
    y_phase = phase_of(
        depths[None, None, :], jnp.asarray(squares_of(class_frequencies()))[:, :, None]
    )
    weights = np.full((CLASSES, 1, 1), 2.0 / N, np.float32)
    weights[0] = weights[8] = 1.0 / N
    factors = jnp.stack([jnp.cos(y_phase), jnp.sin(y_phase)], axis=-1)
    factors = factors.reshape(CLASSES, INNER, 2 * PLANES) * weights

    hologram_rows = lax.dynamic_slice_in_dim(hologram, depth_index * 16, 16, 0)
    sent = forward_x(field, hologram_rows, x_forward)
    received = lax.all_to_all(sent, LAYER, 0, 0, tiled=True)
    partial = forward_y(z_index, received, factors)
    image = lax.psum_scatter(partial, "z", scatter_dimension=0, tiled=True)
    tile = received[:, 256:, :].reshape(PLANES, 2, 2, 16, LANES)
    tile = jnp.transpose(tile, (1, 2, 0, 3, 4)).reshape(1, 2, INNER, LANES)
    misfit = lax.all_gather(image - tile, "z", axis=0, tiled=True)
    sent = backward_y(z_index, misfit, factors)
    received = lax.all_to_all(sent, LAYER, 0, 0, tiled=True)
    moved = backward_x(received, field, x_backward)
    return shrink(moved, depth_index, row_index)[:, None]


def solution(mesh):
    fine = Mesh(mesh.devices.reshape(2, 4, 2, 8, 2), DEPTH + ROW)
    return jax.shard_map(
        per_device,
        mesh=fine,
        in_specs=(P(None, DEPTH, ROW, None), P(ROW, None), P(DEPTH)),
        out_specs=P(None, DEPTH, ROW, None),
        check_vma=False,
    )
```

time: 1060 us -> 483 us (0.46)
  blocking collectives: 311 us -> 120 us
  waiting for transfers between devices: 325 us -> 171 us
  local copies, waits for them, and re-layouts: 162 us -> 22.1 us
  matrix products: 134 us -> 0 us
  Pallas kernels: 0 us -> 89.1 us
  other arithmetic: 81.5 us -> 36.2 us
    all_to_all x3 -> x1, blocking collectives: 311 us -> 56.9 us  [per_device(): received = lax.all_to_all(sent, LAYER, 0, 0, tiled=True)]
    dot_general x16 -> x0, matrix products: 134 us -> none  [contract(): jnp.einsum(formula, table, data, precision=lax.Precision.HIGHEST, preferr...]
    pallas_call x0 -> x4, Pallas kernels: none -> 89.1 us  [the longest x1 31.2 us: forward_y(): pl.pallas_call(forward_y_kernel, grid=(CLASSES,), in_specs=[pl.BlockSpec(...]
    all_to_all x1, waiting for transfers between devices: 87.1 us -> 0.01 us  [per_device(): received = lax.all_to_all(sent, LAYER, 0, 0, tiled=True)]
    ppermute x4 -> x6, waiting for transfers between devices: 154 us -> 84.5 us  [the longest x2 84.5 us: diagonal(): return lax.ppermute(block, DEPTH + ROW, route)]
    unnamed x0 -> x1, blocking collectives: none -> 63.3 us
    reshape x4 -> x2, local copies, waits for them, and re-layouts: 63.2 us -> 0.47 us  [per_device(): factors = factors.reshape(CLASSES, INNER, 2 * PLANES) * weights]
    reduce_scatter x0 -> x1, waiting for transfers between devices: none -> 46.1 us  [per_device(): image = lax.psum_scatter(partial, 'z', scatter_dimension=0, tiled=True)]
  transfers between devices with their start and end apart: 7 -> 9, of which waited for: 6 -> 3; matrix products, arithmetic and copies ran while one was open for 3% -> 5% of each run, Pallas kernels for 0% -> 0%
where the time goes in v1:
time: 483 us; the launch traced here: 476 us
  waiting for transfers between devices  171 us (35%)
  blocking collectives  120 us (25%)
  Pallas kernels  89.1 us (18%)
  other arithmetic  36.2 us (7%)
  starting transfers between devices  23.6 us (5%)
  local copies, waits for them, and re-layouts  22.1 us (5%)
  between operations  14.5 us (3%)
    ppermute x2, waiting for transfers between devices, diagonal(): return lax.ppermute(block, DEPTH + ROW, route)  84.5 us
    unnamed x1, blocking collectives  63.3 us
    all_to_all x1, blocking collectives, per_device(): received = lax.all_to_all(sent, LAYER, 0, 0, tiled=True)  56.9 us
    reduce_scatter x1, waiting for transfers between devices, per_device(): image = lax.psum_scatter(partial, 'z', scatter_dimension=0, tiled=True)  46.1 us
    all_gather x1, waiting for transfers between devices, per_device(): misfit = lax.all_gather(image - tile, 'z', axis=0, tiled=True)  40.2 us
    pallas_call x1, Pallas kernels, forward_y(): pl.pallas_call(forward_y_kernel, grid=(CLASSES,), in_specs=[pl.BlockSpec(...  31.2 us
    pallas_call x1, Pallas kernels, backward_y(): pl.pallas_call(backward_y_kernel, grid=(CLASSES,), in_specs=[pl.BlockSpec...  30.3 us
    reduce_sum x2, other arithmetic, flux_of(): jnp.sum(depth_diff * depth_diff + row_diff * row_diff + col_diff * col_di...  14.7 us
  transfers between devices with their start and end apart: 9, of which 3 were waited for; matrix products, arithmetic and copies ran while one was open for 5% of the time, Pallas kernels for 0%

profile of v1, /device:TPU:2, one launch (start us, length us, event | category | flops | bytes accessed | tf_op | source)
XLA Modules:
  0.0 476.5 jit_solution(3552814435523487592)
XLA Ops:
  9.5 14.1 %filter_x_forward.1 = f32[32,272,128]{2,1,0:T(8,128)} custom-call(f32[2,128,4096]{2,1,0:T(8,128)} %bitcast.24, f32[16,4096]{1,0:T(8,128)} %constant_dynamic-slice_fusion.hol_ref, f32[2,16,256]{2,1,0:T(8,128)} %constant.77.clone.tw_ref, f32[2,16,256]{2,1,0:T(8,128)} %get-tuple-element.15.d_ref, bf16[1536,512]{1,0:T(8,128)(2,1)} %constant.78.clone.wf_ref, ...), custom_call_target="tpu_custom_call" | custom-call | tf_op jit(solution)/shard_map/filter_x_forward/pallas_call | solution.py:268
  23.7 7.8 %all-to-all-start = ((f32[32,272,128]{2,1,0:T(8,128)}), f32[32,272,128]{2,1,0:T(8,128)}, u32[]{:S(2)}, u32[]{:S(2)}) async-start(f32[32,272,128]{2,1,0:T(8,128)} %filter_x_forward.1), calls=%async_computation | async-start | bytes 8912896 | tf_op jit(solution)/shard_map/all_to_all | solution.py:552
  32.9 63.3 %all-reduce.1 = f32[8]{0:T(128)S(1)} all-reduce(f32[8]{0:T(128)S(1)} %dynamic-update-slice), channel_id=1, replica_groups=mesh['x_lo'=2,'y'=4,'x_hi'=2,'z'=8,'core'=2] {'x_lo','y'}, use_global_device_ids=true, to_apply=%add.1 | all-reduce | flops 8 | bytes 64
  98.3 31.2 %filter_y_forward.1 = f32[8,2,256,128]{3,2,1,0:T(8,128)} custom-call(s32[1]{0:T(128)} %bitcast.z_ref, f32[32,272,128]{2,1,0:T(8,128)} %all-to-all-done.g_ref, bf16[9,512,768]{2,1,0:T(8,128)(2,1)} %constant.80.clone.t_ref, bf16[9,256,1536]{2,1,0:T(8,128)(2,1)} %constant.81.clone.tt_ref, f32[9,256,16]{2,1,0:T(8,128)} %broadcast_multiply_fusion.2.cs_ref), custom_call_target="tpu_custom_call" | custom-call | tf_op jit(solution)/shard_map/filter_y_forward/pallas_call | solution.py:365
  130.6 46.1 %reduce-scatter.2.cloned.1.call-done = f32[1,2,256,128]{3,2,1,0:T(8,128)} async-done(((f32[8,2,256,128]{3,2,1,0:T(8,128)}), f32[1,2,256,128]{3,2,1,0:T(8,128)}) %reduce-scatter.2.cloned.1.call-update) | async-done | bytes 262160 | tf_op jit(solution)/shard_map/reduce_scatter | solution.py:554
  176.7 1.7 sub.39
  178.4 40.2 %all-gather.2.cloned.1.call-done.m_ref = f32[8,2,256,128]{3,2,1,0:T(8,128)} async-done(((f32[1,2,256,128]{3,2,1,0:T(8,128)}), f32[8,2,256,128]{3,2,1,0:T(8,128)}) %all-gather.2.cloned.1.call-update) | async-done | bytes 2097168 | tf_op jit(solution)/shard_map/all_gather | solution.py:557
  218.6 30.3 %filter_y_backward.1 = f32[32,2,128,128]{3,2,1,0:T(8,128)} custom-call(s32[1]{0:T(128)} %bitcast.z_ref, f32[8,2,256,128]{3,2,1,0:T(8,128)} %all-gather.2.cloned.1.call-done.m_ref, bf16[9,512,768]{2,1,0:T(8,128)(2,1)} %constant.80.clone.t_ref, bf16[9,256,1536]{2,1,0:T(8,128)(2,1)} %constant.81.clone.tt_ref, f32[9,256,16]{2,1,0:T(8,128)} %broadcast_multiply_fusion.2.cs_ref), custom_call_target="tpu_custom_call" | custom-call | tf_op jit(solution)/shard_map/filter_y_backward/pallas_call | solution.py:446
  248.9 56.9 %all_to_all.10.g_ref = f32[32,2,128,128]{3,2,1,0:T(8,128)} all-to-all(f32[32,2,128,128]{3,2,1,0:T(8,128)} %filter_y_backward.1), channel_id=1, replica_groups=mesh['x_lo'=2,'y'=4,'x_hi'=2,'z'=8,'core'=2] {'x_lo','y','x_hi','core'}, dimensions={0} | all-to-all | bytes 8388608 | tf_op jit(solution)/shard_map/all_to_all | solution.py:559
  305.8 13.3 %filter_x_backward.1 = f32[2,128,4096]{2,1,0:T(8,128)} custom-call(f32[32,2,128,128]{3,2,1,0:T(8,128)} %all_to_all.10.g_ref, f32[2,128,4096]{2,1,0:T(8,128)} %bitcast.25, f32[2,16,256]{2,1,0:T(8,128)} %constant.77.clone.tw_ref, f32[2,16,256]{2,1,0:T(8,128)} %get-tuple-element.14.d_ref, bf16[1536,512]{1,0:T(8,128)(2,1)} %constant.78.clone.wf_ref, ...), custom_call_target="tpu_custom_call" | custom-call | tf_op jit(solution)/shard_map/filter_x_backward/pallas_call | solution.py:289
  319.2 1.9 collective-permute-start.2
  321.1 6.0 %collective-permute-start = (f32[2,128,4096]{2,1,0:T(8,128)}, f32[2,128,4096]{2,1,0:T(8,128)}, u32[]{:S(2)}, u32[]{:S(2)}) collective-permute-start(f32[2,128,4096]{2,1,0:T(8,128)} %filter_x_backward.1), channel_id=1, source_target_pairs={{32,0},{64,32},{96,64},{128,96},{160,128},{192,160},{224,192},{33,... | collective-permute-start | bytes 12582920 | tf_op jit(solution)/shard_map/ppermute | solution.py:469
  328.1 1.5 collective-permute-start.4
  329.6 3.5 collective-permute-start.5
  333.4 84.5 %collective-permute-done.5 = f32[2,1,4096]{2,1,0:T(1,128)S(1)} collective-permute-done((f32[2,1,4096]{2,1,0:T(1,128)S(1)}, f32[2,1,4096]{2,1,0:T(1,128)S(1)}, u32[]{:S(2)}, u32[]{:S(2)}) %collective-permute-start.5) | collective-permute-done | bytes 32800 | tf_op jit(solution)/shard_map/ppermute | solution.py:479
  420.0 1.3 collective-permute-start.3
  421.3 1.5 collective-permute-start.1
  423.8 3.5 slice.55
  429.0 6.5 %slice.58 = f32[2,128,4095]{2,1,0:T(8,128)} slice(f32[2,128,4096]{2,1,0:T(8,128)} %collective-permute-done.2), slice={[0:2], [0:128], [1:4096]} | slice | bytes 8386560 | tf_op jit(solution)/shard_map/slice | solution.py:485
  435.4 4.6 slice.57
  440.1 13.6 %fusion.5 = (f32[128,4096]{1,0:T(8,128)}, f32[128,4096]{1,0:T(8,128)}, f32[2,128,4096]{2,1,0:T(8,128)}) fusion(f32[2,128,4096]{2,1,0:T(8,128)} %collective-permute-done.2, f32[2,1,4096]{2,1,0:T(1,128)S(1)} %collective-permute-done.3, f32[2,127,4096]{2,1,0:T(8,128)} %slice.57, f32[2,128,1]{2,1,0:T(8,128)S(1)} %slice.59, f32[2,128,4095]{2,1,0:T(8,128)} %slice.58, ...), kind=kLoop, calls=%fused_computation.8 | loop fusion | flops 25165824 | bytes 37748864 | tf_op jit(solution)/shard_map/reduce_sum | solution.py:487
  453.7 5.2 %add_divide_fusion = (f32[128,4096]{1,0:T(8,128)}, f32[128,4096]{1,0:T(8,128)S(1)}) fusion(f32[128,4096]{1,0:T(8,128)} %get-tuple-element.5, f32[128,4096]{1,0:T(8,128)} %get-tuple-element.6), kind=kLoop, calls=%fused_computation.19 | loop fusion | flops 3145728 | bytes 8388608 | tf_op jit(solution)/shard_map/div | solution.py:489
  458.9 2.4 broadcast_multiply_fusion.1
  461.3 8.3 %fusion.11 = f32[2,1,128,4096]{3,2,1,0:T(8,128)} fusion(f32[2,128,4096]{2,1,0:T(8,128)S(1)} %copy-done.2, f32[2,128,4096]{2,1,0:T(8,128)S(1)} %get-tuple-element.9, f32[2,127,4096]{2,1,0:T(8,128)S(1)} %bitcast.22, f32[2,1,4096]{2,1,0:T(1,128)S(1)} %get-tuple-element.10, f32[2,128,4095]{2,1,0:T(8,128)S(1)} %bitcast.23, ...), kind=kLoop, calls=%fused_computation.16 | loop fusion | flops 13631488 | bytes 37747712 | tf_op jit(solution)/shard_map/broadcast_in_dim | solution.py:561
  (56 shorter events, 12.7 us)
Async XLA Ops:
  6.5 1.6 copy-start
  23.7 7.9 %copy-start.10 = (u32[256]{0:T(256)S(1)}, u32[256]{0:T(256)}, u32[]{:S(2)}) copy-start(u32[256]{0:T(256)} %constant.90) | copy-start | bytes 3076
  23.7 72.6 %copy-start.8 = (f32[9,256]{1,0:T(8,128)S(1)}, f32[9,256]{1,0:T(8,128)}, u32[]{:S(2)}) copy-start(f32[9,256]{1,0:T(8,128)} %constant.86) | copy-start | bytes 27652
  23.7 73.5 %copy-start.9 = (f32[9]{0:T(128)S(1)}, f32[9]{0:T(128)}, u32[]{:S(2)}) copy-start(f32[9]{0:T(128)} %constant.87) | copy-start | bytes 112
  23.7 74.7 %all-to-all-start = ((f32[32,272,128]{2,1,0:T(8,128)}), f32[32,272,128]{2,1,0:T(8,128)}, u32[]{:S(2)}, u32[]{:S(2)}) async-start(f32[32,272,128]{2,1,0:T(8,128)} %filter_x_forward.1), calls=%async_computation | async-start | bytes 8912896 | tf_op jit(solution)/shard_map/all_to_all | solution.py:552
  31.5 145.2 %reduce-scatter.2.cloned.1.call-start = ((), (), s32[]{:S(2)}) async-start(), calls=%async_computation.3 | async-start | bytes 2359296 | tf_op jit(solution)/shard_map/reduce_scatter | solution.py:554
  129.6 89.0 %all-gather.2.cloned.1.call-start = ((), (), s32[]{:S(2)}) async-start(), calls=%async_computation.4 | async-start | bytes 2359296 | tf_op jit(solution)/shard_map/all_gather | solution.py:557
  319.2 108.6 %collective-permute-start.2 = (f32[2,128,4096]{2,1,0:T(8,128)}, f32[2,128,4096]{2,1,0:T(8,128)}, u32[]{:S(2)}, u32[]{:S(2)}) collective-permute-start(f32[2,128,4096]{2,1,0:T(8,128)} %filter_x_backward.1), channel_id=1, source_target_pairs={{0,32},{32,64},{64,96},{96,128},{128,160},{160,192},{192,224},{1,3... | collective-permute-start | bytes 12582920 | tf_op jit(solution)/shard_map/ppermute | solution.py:469
  321.1 119.0 %collective-permute-start = (f32[2,128,4096]{2,1,0:T(8,128)}, f32[2,128,4096]{2,1,0:T(8,128)}, u32[]{:S(2)}, u32[]{:S(2)}) collective-permute-start(f32[2,128,4096]{2,1,0:T(8,128)} %filter_x_backward.1), channel_id=1, source_target_pairs={{32,0},{64,32},{96,64},{128,96},{160,128},{192,160},{224,192},{33,... | collective-permute-start | bytes 12582920 | tf_op jit(solution)/shard_map/ppermute | solution.py:469
  328.1 5.0 %collective-permute-start.4 = (f32[2,1,4096]{2,1,0:T(1,128)S(1)}, f32[2,1,4096]{2,1,0:T(1,128)S(1)}, u32[]{:S(2)}, u32[]{:S(2)}) collective-permute-start(f32[2,1,4096]{2,1,0:T(1,128)S(1)} %slice.60), channel_id=1, source_target_pairs={{0,1},{1,2},{2,3},{3,4},{4,5},{5,6},{6,7},{7,8},{8,9},{9,10},{10,1... | collective-permute-start | bytes 98312 | tf_op jit(solution)/shard_map/ppermute | solution.py:469
  329.6 88.3 %collective-permute-start.5 = (f32[2,1,4096]{2,1,0:T(1,128)S(1)}, f32[2,1,4096]{2,1,0:T(1,128)S(1)}, u32[]{:S(2)}, u32[]{:S(2)}) collective-permute-start(f32[2,1,4096]{2,1,0:T(1,128)S(1)} %slice.60), channel_id=1, source_target_pairs={{32,1},{33,2},{34,3},{35,4},{36,5},{37,6},{38,7},{39,8},{40,9},{41... | collective-permute-start | bytes 98312 | tf_op jit(solution)/shard_map/ppermute | solution.py:479
  420.0 20.1 %collective-permute-start.3 = (f32[2,1,4096]{2,1,0:T(1,128)S(1)}, f32[2,1,4096]{2,1,0:T(1,128)S(1)}, u32[]{:S(2)}, u32[]{:S(2)}) collective-permute-start(f32[2,1,4096]{2,1,0:T(1,128)S(1)} %get-tuple-element.11), channel_id=1, source_target_pairs={{1,32},{2,33},{3,34},{4,35},{5,36},{6,37},{7,38},{8,39},{9,40},{10... | collective-permute-start | bytes 98312 | tf_op jit(solution)/shard_map/ppermute | solution.py:479
  421.3 18.8 %collective-permute-start.1 = (f32[2,1,4096]{2,1,0:T(1,128)S(1)}, f32[2,1,4096]{2,1,0:T(1,128)S(1)}, u32[]{:S(2)}, u32[]{:S(2)}) collective-permute-start(f32[2,1,4096]{2,1,0:T(1,128)S(1)} %get-tuple-element.11), channel_id=1, source_target_pairs={{1,0},{2,1},{3,2},{4,3},{5,4},{6,5},{7,6},{8,7},{9,8},{10,9},{11,1... | collective-permute-start | bytes 98312 | tf_op jit(solution)/shard_map/ppermute | solution.py:469
  423.8 3.5 copy-start.2
  427.3 12.8 %copy-start.3 = (f32[2,128,4095]{2,1,0:T(8,128)}, f32[2,128,4095]{2,1,0:T(8,128)S(1)}, u32[]{:S(2)}) copy-start(f32[2,128,4095]{2,1,0:T(8,128)S(1)} %slice.55) | copy-start | bytes 12579844
  427.8 12.3 %copy-start.5 = (f32[2,127,4096]{2,1,0:T(8,128)}, f32[2,127,4096]{2,1,0:T(8,128)S(1)}, u32[]{:S(2)}) copy-start(f32[2,127,4096]{2,1,0:T(8,128)S(1)} %slice.53) | copy-start | bytes 12484612
  453.7 5.2 %copy-start.4 = (f32[2,128,4095]{2,1,0:T(8,128)S(1)}, f32[2,128,4095]{2,1,0:T(8,128)}, u32[]{:S(2)}) copy-start(f32[2,128,4095]{2,1,0:T(8,128)} %copy-done.3) | copy-start | bytes 12579844
  453.7 5.2 %copy-start.6 = (f32[2,127,4096]{2,1,0:T(8,128)S(1)}, f32[2,127,4096]{2,1,0:T(8,128)}, u32[]{:S(2)}) copy-start(f32[2,127,4096]{2,1,0:T(8,128)} %copy-done.5) | copy-start | bytes 12484612
  458.9 2.4 copy-start.7
  461.3 8.3 %copy-start.1 = (f32[128,4096]{1,0:T(8,128)S(1)}, f32[128,4096]{1,0:T(8,128)}, u32[]{:S(2)}) copy-start(f32[128,4096]{1,0:T(8,128)} %param.17) | copy-start | bytes 6291460
Sparse Core Ops, SparseCore 0:
  129.7 46.9 reduce-scatter.1
  178.5 40.0 all-gather.1

commit v2 on v1

v2 whole, which is shorter than its diff:
```python
import functools
import math

import jax
import jax.numpy as jnp
import ml_dtypes
import numpy as np
from jax import lax
from jax.experimental import pallas as pl
from jax.experimental.pallas import tpu as pltpu
from jax.sharding import Mesh
from jax.sharding import PartitionSpec as P

tv_step_size = 1.0 / 12.0
tv_sharpness = 0.25

N = 4096
RADIX = 16
INNER = 256
CLASSES = 9
PLANES = 8
LANES = 128
HALF = 64
F32 = jnp.float32
BF16 = jnp.bfloat16

DEPTH = ("x_lo", "y")
ROW = ("x_hi", "z", "core")
LAYER = ("x_lo", "y", "x_hi", "core")


def split_table(table):
    high = table.astype(ml_dtypes.bfloat16)
    low = (table - high.astype(np.float64)).astype(ml_dtypes.bfloat16)
    return high, low


def inner_tables():
    index = np.arange(INNER)
    angle = 2.0 * np.pi * (np.outer(index, index) % INNER) / INNER
    cosine, sine = np.cos(angle), np.sin(angle)
    tables = []
    for sign in (1.0, -1.0):
        whole = np.block([[cosine, -sign * sine], [sign * sine, cosine]])
        high, low = split_table(whole)
        tables.append(np.concatenate([high, high, low], axis=0))
    return tables


def twiddles():
    angle = 2.0 * np.pi * np.outer(np.arange(RADIX), np.arange(INNER)) / N
    return np.stack([np.cos(angle), np.sin(angle)]).astype(np.float32)


def class_frequencies():
    return (RADIX * np.arange(INNER)[None, :] + np.arange(CLASSES)[:, None]) % N


def class_tables():
    freq = class_frequencies()
    angle = 2.0 * np.pi * ((freq[:, None, :] * np.arange(INNER)[None, :, None]) % N) / N
    table = np.concatenate([np.cos(angle), np.sin(angle)], axis=2)
    tables = []
    for each in (table, np.swapaxes(table, 1, 2)):
        high, low = split_table(each)
        tables.append(np.concatenate([high, high, low], axis=1))
    return tables


def squares_of(index):
    centred = np.where(index < N // 2, index, index - N)
    return (centred * centred).astype(np.float32)


def dft4(values, inverse):
    (ar, ai), (br, bi), (cr, ci), (dr, di) = values
    s0r, s0i, s1r, s1i = ar + cr, ai + ci, ar - cr, ai - ci
    s2r, s2i, s3r, s3i = br + dr, bi + di, br - dr, bi - di
    plus = (s1r - s3i, s1i + s3r)
    minus = (s1r + s3i, s1i - s3r)
    first, third = (plus, minus) if inverse else (minus, plus)
    return [(s0r + s2r, s0i + s2i), first, (s0r - s2r, s0i - s2i), third]


def times_constant(value, cosine, sine):
    real, imag = value
    if abs(sine) < 1e-9 and abs(cosine - 1.0) < 1e-9:
        return value
    if abs(cosine) < 1e-9 and abs(sine - 1.0) < 1e-9:
        return (-imag, real)
    if abs(cosine) < 1e-9 and abs(sine + 1.0) < 1e-9:
        return (imag, -real)
    if abs(abs(cosine) - abs(sine)) < 1e-9:
        root = math.sqrt(0.5)
        sc, ss = math.copysign(1.0, cosine), math.copysign(1.0, sine)
        first = (real if sc > 0 else -real) - (imag if ss > 0 else -imag)
        second = (imag if sc > 0 else -imag) + (real if ss > 0 else -real)
        return (first * root, second * root)
    return (real * cosine - imag * sine, imag * cosine + real * sine)


def dft16(values, inverse):
    direction = 1.0 if inverse else -1.0
    stage = [dft4([values[4 * n1 + n2] for n1 in range(4)], inverse) for n2 in range(4)]
    result = [None] * 16
    for k1 in range(4):
        column = []
        for n2 in range(4):
            angle = direction * 2.0 * math.pi * n2 * k1 / 16
            column.append(times_constant(stage[n2][k1], math.cos(angle), math.sin(angle)))
        for k2, value in enumerate(dft4(column, inverse)):
            result[k1 + 4 * k2] = value
    return result


def weighted_sum(terms):
    total = None
    for coefficient, value in terms:
        if abs(coefficient) < 1e-9:
            continue
        if abs(coefficient - 1.0) < 1e-9:
            total = value if total is None else total + value
        elif abs(coefficient + 1.0) < 1e-9:
            total = -value if total is None else total - value
        else:
            piece = value * float(np.float32(coefficient))
            total = piece if total is None else total + piece
    return total


def real_dft16(blocks):
    sums = [blocks[0]] + [blocks[b] + blocks[16 - b] for b in range(1, 8)] + [blocks[8]]
    diffs = [None] + [blocks[b] - blocks[16 - b] for b in range(1, 8)]
    result = []
    for k in range(CLASSES):
        real = weighted_sum([(math.cos(2 * math.pi * k * b / 16), sums[b]) for b in range(9)])
        if k in (0, 8):
            imag = jnp.zeros_like(real)
        else:
            imag = weighted_sum(
                [(-math.sin(2 * math.pi * k * b / 16), diffs[b]) for b in range(1, 8)]
            )
        result.append((real, imag))
    return result


def real_inverse16(values):
    result = [None] * 16
    for b in range(9):
        even = weighted_sum([(math.cos(2 * math.pi * k * b / 16), values[k][0]) for k in range(9)])
        if b in (0, 8):
            result[b] = even
        else:
            odd = weighted_sum(
                [(math.sin(2 * math.pi * k * b / 16), values[k][1]) for k in range(1, 8)]
            )
            result[b] = even - odd
            result[16 - b] = even + odd
    return result


def halves(value):
    high = value.astype(BF16)
    low = (value - high.astype(F32)).astype(BF16)
    return high, low


STEP_ROWS = 32
CHUNK_CLASSES = 16


def filter_rows(load, store, tw_ref, d_ref, wf_ref, wi_ref, x_ref):
    groups = [(r, h) for r in range(STEP_ROWS // 8) for h in range(INNER // LANES)]
    for r, h in groups:
        values = [load(r, b * (INNER // LANES) + h) for b in range(RADIX)]
        lanes = slice(h * LANES, (h + 1) * LANES)
        for k, (real, imag) in enumerate(dft16(values, False)):
            if k:
                cosine, sine = tw_ref[0, k : k + 1, lanes], tw_ref[1, k : k + 1, lanes]
                real, imag = real * cosine + imag * sine, imag * cosine - real * sine
            rows = slice(k * STEP_ROWS + 8 * r, k * STEP_ROWS + 8 * r + 8)
            x_ref[rows, lanes] = real
            x_ref[rows, INNER + h * LANES : INNER + (h + 1) * LANES] = imag
    for chunk in range(RADIX // CHUNK_CLASSES):
        base = chunk * CHUNK_CLASSES * STEP_ROWS
        rows = slice(base, base + CHUNK_CLASSES * STEP_ROWS)
        high, low = halves(x_ref[rows, :])
        spectrum = jnp.dot(
            jnp.concatenate([high, low, high], axis=1), wf_ref[...], preferred_element_type=F32
        )
        pieces = []
        for kk in range(CHUNK_CLASSES):
            k = chunk * CHUNK_CLASSES + kk
            cosine, sine = per_row(d_ref[0, k]), per_row(d_ref[1, k])
            real = spectrum[kk * STEP_ROWS : (kk + 1) * STEP_ROWS, :INNER]
            imag = spectrum[kk * STEP_ROWS : (kk + 1) * STEP_ROWS, INNER:]
            pieces.append(
                jnp.concatenate(
                    [real * cosine - imag * sine, imag * cosine + real * sine], axis=1
                )
            )
        high, low = halves(jnp.concatenate(pieces, axis=0))
        x_ref[rows, :] = jnp.dot(
            jnp.concatenate([high, low, high], axis=1), wi_ref[...], preferred_element_type=F32
        )
    for r, h in groups:
        lanes = slice(h * LANES, (h + 1) * LANES)
        values = []
        for k in range(RADIX):
            rows = slice(k * STEP_ROWS + 8 * r, k * STEP_ROWS + 8 * r + 8)
            real = x_ref[rows, lanes]
            imag = x_ref[rows, INNER + h * LANES : INNER + (h + 1) * LANES]
            if k:
                cosine, sine = tw_ref[0, k : k + 1, lanes], tw_ref[1, k : k + 1, lanes]
                real, imag = real * cosine - imag * sine, imag * cosine + real * sine
            values.append((real, imag))
        for b, value in enumerate(dft16(values, True)):
            store(r, b * (INNER // LANES) + h, value)


def per_row(factor):
    if factor.shape[0] == 1:
        return factor
    return jnp.concatenate([factor] * (STEP_ROWS // factor.shape[0]), axis=0)


def low_lanes(shape):
    return lax.broadcasted_iota(jnp.int32, shape, len(shape) - 1) < HALF


def exchange_halves(first, second):
    low = low_lanes(first.shape)
    axis = first.ndim - 1
    return (
        jnp.where(low, first, pltpu.roll(second, HALF, axis)),
        jnp.where(low, pltpu.roll(first, HALF, axis), second),
    )


def forward_x_kernel(f_ref, hol_ref, tw_ref, d_ref, wf_ref, wi_ref, a_ref, b_ref, x_ref):
    step = pl.program_id(0)

    @pl.when(step == 0)
    def _():
        for j in range(32):
            lanes = slice(j * LANES, (j + 1) * LANES)
            first, second = exchange_halves(hol_ref[0, :, lanes], hol_ref[1, :, lanes])
            a_ref[j, 128:136, :] = first
            b_ref[j, 128:136, :] = second

    def load(r, j):
        rows, lanes = slice(8 * r, 8 * r + 8), slice(j * LANES, (j + 1) * LANES)
        return f_ref[0, rows, lanes], f_ref[1, rows, lanes]

    def store(r, j, value):
        rows = pl.ds(pl.multiple_of(step * STEP_ROWS + 8 * r, 8), 8)
        first, second = exchange_halves(*value)
        a_ref[j, rows, :] = first
        b_ref[j, rows, :] = second

    filter_rows(load, store, tw_ref, d_ref, wf_ref, wi_ref, x_ref)


def backward_x_kernel(ga_ref, gb_ref, fr_ref, fi_ref, tw_ref, d_ref, wf_ref, wi_ref, o_ref, x_ref, f_ref):
    step = pl.program_id(0)

    @pl.when(step == 0)
    def _():
        for c, source in ((0, fr_ref), (1, fi_ref)):
            for p in range(PLANES):
                for j in range(N // LANES):
                    f_ref[c, j, pl.ds(p, 16, stride=PLANES), :] = source[
                        p, :, j * LANES : (j + 1) * LANES
                    ]

    def load(r, j):
        rows = slice(8 * r, 8 * r + 8)
        return exchange_halves(ga_ref[j, rows, :], gb_ref[j, rows, :])

    def store(r, j, value):
        rows, lanes = slice(8 * r, 8 * r + 8), slice(j * LANES, (j + 1) * LANES)
        held = pl.ds(pl.multiple_of(step * STEP_ROWS + 8 * r, 8), 8)
        for c in range(2):
            o_ref[c, rows, lanes] = f_ref[c, j, held, :] + value[c]

    filter_rows(load, store, tw_ref, d_ref, wf_ref, wi_ref, x_ref)


def whole(shape):
    return pl.BlockSpec(shape, lambda *_: (0,) * len(shape))


def params():
    return pltpu.CompilerParams(vmem_limit_bytes=56 << 20)


def x_tables():
    forward, inverse = inner_tables()
    return jnp.asarray(twiddles()), jnp.asarray(forward), jnp.asarray(inverse)


def forward_x(field, hologram_rows, transfer):
    tw, wf, wi = x_tables()
    return pl.pallas_call(
        forward_x_kernel,
        grid=(128 // STEP_ROWS,),
        in_specs=[
            pl.BlockSpec((2, STEP_ROWS, N), lambda i: (0, i, 0)),
            whole((2, 8, N)),
            whole((2, RADIX, INNER)),
            whole((2, RADIX, 1, INNER)),
            whole((1536, 512)),
            whole((1536, 512)),
        ],
        out_specs=[whole((32, 136, LANES))] * 2,
        out_shape=[jax.ShapeDtypeStruct((32, 136, LANES), F32)] * 2,
        scratch_shapes=[pltpu.VMEM((RADIX * STEP_ROWS, 2 * INNER), F32)],
        compiler_params=params(),
        name="filter_x_forward",
    )(field, hologram_rows, tw, transfer, wf, wi)


def backward_x(first, second, field_real, field_imag, transfer):
    tw, wf, wi = x_tables()
    return pl.pallas_call(
        backward_x_kernel,
        grid=(128 // STEP_ROWS,),
        in_specs=[
            pl.BlockSpec((32, STEP_ROWS, LANES), lambda i: (0, i, 0)),
            pl.BlockSpec((32, STEP_ROWS, LANES), lambda i: (0, i, 0)),
            whole((PLANES, 16, N)),
            whole((PLANES, 16, N)),
            whole((2, RADIX, INNER)),
            whole((2, RADIX, PLANES, INNER)),
            whole((1536, 512)),
            whole((1536, 512)),
        ],
        out_specs=pl.BlockSpec((2, STEP_ROWS, N), lambda i: (0, i, 0)),
        out_shape=jax.ShapeDtypeStruct((2, 128, N), F32),
        scratch_shapes=[
            pltpu.VMEM((RADIX * STEP_ROWS, 2 * INNER), F32),
            pltpu.VMEM((2, N // LANES, 128, LANES), F32),
        ],
        compiler_params=params(),
        name="filter_x_backward",
    )(first, second, field_real, field_imag, tw, transfer, wf, wi)


DOT_PLANES = 4


def forward_y_kernel(z_ref, g_ref, t_ref, tt_ref, cs_ref, o_ref, h_ref, u_ref, s_ref):
    step = pl.program_id(0)

    @pl.when(step == 0)
    def _():
        @pl.loop(0, PLANES)
        def _(p):
            held = pl.ds(pl.multiple_of(p * LANES, LANES), LANES)
            for core in range(2):
                upper = g_ref[p * 4 + core, :128, :].T
                lower = g_ref[p * 4 + 2 + core, :128, :].T
                for parity, value in ((0, upper + lower), (1, upper - lower)):
                    high, low = halves(value)
                    for part, piece in ((0, high), (1, low), (2, high)):
                        start = part * INNER + core * 128
                        u_ref[parity, held, start : start + 128] = piece

        for upper in range(2):
            for core in range(2):
                rows = [g_ref[p * 4 + upper * 2 + core, 128:, :] for p in range(PLANES)]
                block = jnp.concatenate(rows, axis=0).T
                block = jnp.concatenate([block[:HALF], block[HALF:]], axis=1)
                h_ref[0, upper, :, core * 128 : (core + 1) * 128] = block

    parity = lax.rem(step, 2)
    total = None
    for chunk in range(PLANES // DOT_PLANES):
        rows = slice(chunk * DOT_PLANES * LANES, (chunk + 1) * DOT_PLANES * LANES)
        result = jnp.dot(u_ref[parity, rows, :], t_ref[0], preferred_element_type=F32)
        for i in range(DOT_PLANES):
            p = chunk * DOT_PLANES + i
            piece = (
                cs_ref[0, 2 * p : 2 * p + 1, :] * result[i * LANES : i * LANES + HALF]
                + cs_ref[0, 2 * p + 1 : 2 * p + 2, :] * result[i * LANES + HALF : (i + 1) * LANES]
            )
            total = piece if total is None else total + piece
    turned = jnp.concatenate([-total[:, INNER:], total[:, :INNER]], axis=1)
    high, low = halves(jnp.concatenate([total, turned], axis=0))
    s_ref[step] = jnp.dot(
        jnp.concatenate([high, low, high], axis=1), tt_ref[0], preferred_element_type=F32
    )

    @pl.when(step == CLASSES - 1)
    def _():
        shift = z_ref[0]

        @pl.loop(0, HALF // 8)
        def _(i):
            rows = pl.ds(pl.multiple_of(i * 8, 8), 8)
            other = pl.ds(pl.multiple_of(HALF + i * 8, 8), 8)
            for half in range(2):
                lanes = slice(half * LANES, (half + 1) * LANES)
                values = [(s_ref[k, rows, lanes], s_ref[k, other, lanes]) for k in range(CLASSES)]
                for b, value in enumerate(real_inverse16(values)):
                    block = lax.rem(shift + b, 16)
                    o_ref[lax.rem(block, 8), lax.div(block, 8), rows, lanes] = value


def forward_y(z_index, received, factors):
    forward, backward = class_tables()
    return pl.pallas_call(
        forward_y_kernel,
        grid=(CLASSES,),
        in_specs=[
            pl.BlockSpec(memory_space=pltpu.SMEM),
            whole((32, 136, LANES)),
            pl.BlockSpec((1, 768, 512), lambda k: (k, 0, 0)),
            pl.BlockSpec((1, 1536, 256), lambda k: (k, 0, 0)),
            pl.BlockSpec((1, 16, 512), lambda k: (k, 0, 0)),
        ],
        out_specs=[whole((8, 2, HALF, INNER)), whole((1, 2, HALF, INNER))],
        out_shape=[
            jax.ShapeDtypeStruct((8, 2, HALF, INNER), F32),
            jax.ShapeDtypeStruct((1, 2, HALF, INNER), F32),
        ],
        scratch_shapes=[
            pltpu.VMEM((2, PLANES * LANES, 768), BF16),
            pltpu.VMEM((CLASSES, LANES, INNER), F32),
        ],
        compiler_params=params(),
        name="filter_y_forward",
    )(z_index, received, jnp.asarray(forward), jnp.asarray(backward), factors)


def backward_y_kernel(z_ref, m_ref, t_ref, tt_ref, cs_ref, o_ref, x_ref, a_ref):
    step = pl.program_id(0)

    @pl.when(step == 0)
    def _():
        shift = z_ref[0]

        @pl.loop(0, HALF // 8)
        def _(i):
            rows = pl.ds(pl.multiple_of(i * 8, 8), 8)
            other = pl.ds(pl.multiple_of(HALF + i * 8, 8), 8)
            for half in range(2):
                lanes = slice(half * LANES, (half + 1) * LANES)
                blocks = []
                for b in range(16):
                    block = lax.rem(shift + b, 16)
                    blocks.append(m_ref[lax.rem(block, 8), lax.div(block, 8), rows, lanes])
                for k, (real, imag) in enumerate(real_dft16(blocks)):
                    x_ref[k, rows, lanes] = real
                    x_ref[k, other, lanes] = imag

        @pl.loop(0, PLANES)
        def _(p):
            held = pl.ds(pl.multiple_of(p * LANES, LANES), LANES)
            for parity in range(2):
                a_ref[parity, held, :] = jnp.zeros((LANES, INNER), F32)

    parity = lax.rem(step, 2)
    high, low = halves(x_ref[step])
    mixed = jnp.dot(
        jnp.concatenate([high, low, high], axis=1), t_ref[0], preferred_element_type=F32
    )
    cosine = mixed[:HALF, :INNER] + mixed[HALF:, INNER:]
    sine = mixed[:HALF, INNER:] - mixed[HALF:, :INNER]
    spectrum = jnp.concatenate([cosine, sine], axis=1)
    for chunk in range(PLANES // DOT_PLANES):
        rows = slice(chunk * DOT_PLANES * LANES, (chunk + 1) * DOT_PLANES * LANES)
        pieces = []
        for row in range(2 * DOT_PLANES * chunk, 2 * DOT_PLANES * (chunk + 1)):
            pieces.append(cs_ref[0, row : row + 1, :] * spectrum)
        high, low = halves(jnp.concatenate(pieces, axis=0))
        a_ref[parity, rows, :] += jnp.dot(
            jnp.concatenate([high, low, high], axis=1), tt_ref[0], preferred_element_type=F32
        )

    @pl.when(step == CLASSES - 1)
    def _():
        @pl.loop(0, PLANES)
        def _(p):
            rows = pl.ds(pl.multiple_of(p * LANES, LANES), LANES)
            for core in range(2):
                lanes = slice(core * 128, (core + 1) * 128)
                even, odd = a_ref[0, rows, lanes], a_ref[1, rows, lanes]
                upper, lower = (even + odd).T, (even - odd).T
                for owner in range(PLANES):
                    part = slice(owner * 16, owner * 16 + 16)
                    held = pl.ds(p, 16, stride=PLANES)
                    o_ref[owner * 4 + core, held, :] = upper[part]
                    o_ref[owner * 4 + 2 + core, held, :] = lower[part]


def backward_y(z_index, misfit, factors):
    forward, backward = class_tables()
    return pl.pallas_call(
        backward_y_kernel,
        grid=(CLASSES,),
        in_specs=[
            pl.BlockSpec(memory_space=pltpu.SMEM),
            whole((8, 2, HALF, INNER)),
            pl.BlockSpec((1, 768, 512), lambda k: (k, 0, 0)),
            pl.BlockSpec((1, 1536, 256), lambda k: (k, 0, 0)),
            pl.BlockSpec((1, 16, 512), lambda k: (k, 0, 0)),
        ],
        out_specs=whole((32, 128, LANES)),
        out_shape=jax.ShapeDtypeStruct((32, 128, LANES), F32),
        scratch_shapes=[
            pltpu.VMEM((CLASSES, LANES, INNER), F32),
            pltpu.VMEM((2, PLANES * LANES, INNER), F32),
        ],
        compiler_params=params(),
        name="filter_y_backward",
    )(z_index, misfit, jnp.asarray(forward), jnp.asarray(backward), factors)


TV_ROWS = 8


def shrink_kernel(edge_ref, m_ref, next_ref, above_ref, below_ref, o_ref, e_ref, prior_ref):
    step = pl.program_id(0)
    plane = lax.broadcasted_iota(jnp.int32, (PLANES, N), 0)
    column = lax.broadcasted_iota(jnp.int32, (PLANES, N), 1)
    last_plane, first_plane = plane == PLANES - 1, plane == 0
    last_column, first_column = column == N - 1, column == 0

    def flux(here, below):
        squares = None
        diffs = []
        for c in range(2):
            depth = jnp.where(last_plane, 0.0, pltpu.roll(here[c], PLANES - 1, 0) - here[c])
            row = below[c] - here[c]
            col = jnp.where(last_column, 0.0, pltpu.roll(here[c], N - 1, 1) - here[c])
            diffs.append((depth, row, col))
            term = depth * depth + row * row + col * col
            squares = term if squares is None else squares + term
        factor = 1.0 / (1.0 + tv_sharpness * jnp.sqrt(squares))
        return [tuple(d * factor for d in triple) for triple in diffs]

    @pl.when(step == 0)
    def _():
        above = [above_ref[c] for c in range(2)]
        first = [m_ref[c, :PLANES, :] for c in range(2)]
        terms = flux(above, first)
        for c in range(2):
            prior_ref[c] = jnp.where(edge_ref[0] > 0, terms[c][1], 0.0)

    def row_at(t):
        rows = pl.ds(pl.multiple_of(t * PLANES, PLANES), PLANES)
        return [m_ref[c, rows, :] for c in range(2)]

    def emit(t, here, below):
        terms = flux(here, below)
        rows = pl.ds(pl.multiple_of(t * PLANES, PLANES), PLANES)
        for c in range(2):
            depth, row, col = terms[c]
            divergence = (
                (depth - jnp.where(first_plane, 0.0, pltpu.roll(depth, 1, 0)))
                + (row - prior_ref[c])
                + (col - jnp.where(first_column, 0.0, pltpu.roll(col, 1, 1)))
            )
            prior_ref[c] = row
            estimate = here[c] + tv_step_size * divergence
            for j in range(N // LANES):
                e_ref[c, j, rows, :] = estimate[:, j * LANES : (j + 1) * LANES]

    @pl.loop(0, TV_ROWS - 1)
    def _(t):
        emit(t, row_at(t), row_at(t + 1))

    here = row_at(TV_ROWS - 1)
    final = step == 16 // TV_ROWS - 1
    below = []
    for c in range(2):
        beyond = jnp.where(edge_ref[1] > 0, below_ref[c], here[c])
        below.append(jnp.where(final, beyond, next_ref[c]))
    emit(TV_ROWS - 1, here, below)
    for p in range(PLANES):
        for c in range(2):
            for j in range(N // LANES):
                held = pl.ds(p, TV_ROWS, stride=PLANES)
                o_ref[p, c, :, j * LANES : (j + 1) * LANES] = e_ref[c, j, held, :]


def shrink(edges, moved, above, below):
    steps = 16 // TV_ROWS
    return pl.pallas_call(
        shrink_kernel,
        grid=(steps,),
        in_specs=[
            pl.BlockSpec(memory_space=pltpu.SMEM),
            pl.BlockSpec((2, TV_ROWS * PLANES, N), lambda i: (0, i, 0)),
            pl.BlockSpec((2, PLANES, N), lambda i: (0, jnp.minimum((i + 1) * TV_ROWS, 15), 0)),
            whole((2, PLANES, N)),
            whole((2, PLANES, N)),
        ],
        out_specs=pl.BlockSpec((PLANES, 2, TV_ROWS, N), lambda i: (0, 0, i, 0)),
        out_shape=jax.ShapeDtypeStruct((PLANES, 2, 16, N), F32),
        scratch_shapes=[
            pltpu.VMEM((2, N // LANES, TV_ROWS * PLANES, LANES), F32),
            pltpu.VMEM((2, PLANES, N), F32),
        ],
        compiler_params=params(),
        name="tv_shrink",
    )(edges, moved, moved, above, below)


def along_rows(block, distance):
    place = lambda line: (line % 8) * 32 + line // 8
    route = [
        (place(line - distance), place(line)) for line in range(256) if 0 <= line - distance < 256
    ]
    return lax.ppermute(block, DEPTH + ROW, route)


def phase_of(depth_values, squares):
    return depth_values * (squares * (math.pi / (N * N)))


def per_device(field, hologram, defocus):
    x_lo, y = lax.axis_index("x_lo"), lax.axis_index("y")
    x_hi, z, core = lax.axis_index("x_hi"), lax.axis_index("z"), lax.axis_index("core")
    depth_index = x_lo * 4 + y
    row_index = x_hi * 16 + z * 2 + core
    z_index = z[None].astype(jnp.int32)
    field = field[:, 0]

    x_freq = RADIX * np.arange(INNER)[None, :] + np.arange(RADIX)[:, None]
    x_squares = jnp.asarray(squares_of(x_freq))[:, None, :]
    x_phase = phase_of(defocus[0], x_squares)
    x_forward = jnp.stack([jnp.cos(x_phase) / N, -jnp.sin(x_phase) / N])

    depths = lax.all_gather(defocus, DEPTH, tiled=True)
    x_phase = phase_of(depths[None, :, None], x_squares)
    x_backward = jnp.stack([jnp.cos(x_phase), jnp.sin(x_phase)]) * (-1.0 / (PLANES * N))
    y_squares = jnp.asarray(squares_of(class_frequencies()))[:, None, None, :]
    y_phase = phase_of(depths[None, :, None, None], y_squares)
    weights = np.full((CLASSES, 1, 1, 1), 2.0 / N, np.float32)
    weights[0] = weights[8] = 1.0 / N
    factors = jnp.concatenate([jnp.cos(y_phase), jnp.sin(y_phase)], axis=2) * weights
    factors = factors.reshape(CLASSES, 2 * PLANES, INNER)
    factors = jnp.concatenate([factors, factors], axis=2)

    hologram_rows = lax.dynamic_slice_in_dim(
        hologram.reshape(2, HALF, N), depth_index * 8, 8, axis=1
    )
    sent = forward_x(field, hologram_rows, x_forward)
    first = lax.all_to_all(sent[0], LAYER, 0, 0, tiled=True)
    first, later = lax.optimization_barrier((first, sent[1]))
    second = lax.all_to_all(later, LAYER, 0, 0, tiled=True)
    second, field = lax.optimization_barrier((second, field))
    held = [
        lax.all_to_all(field[c].reshape(PLANES, 16, N), DEPTH, 0, 0, tiled=True) for c in range(2)
    ]
    returned = []
    for received in (first, second):
        partial, tile = forward_y(z_index, received, factors)
        image = lax.psum_scatter(partial, "z", scatter_dimension=0, tiled=True)
        misfit = lax.all_gather(image - tile, "z", axis=0, tiled=True)
        sent = backward_y(z_index, misfit, factors)
        returned.append(lax.all_to_all(sent, LAYER, 0, 0, tiled=True))
    moved = backward_x(returned[0], returned[1], held[0], held[1], x_backward)
    above = along_rows(moved[:, 120:], 1)
    below = along_rows(moved[:, :8], -1)
    line = row_index * 8 + depth_index
    edges = jnp.stack([line > 0, line < 255]).astype(jnp.int32)
    estimate = shrink(edges, moved, above, below)
    estimate = lax.all_to_all(estimate, DEPTH, 0, 0, tiled=True)
    return jnp.transpose(estimate, (1, 0, 2, 3)).reshape(2, 1, 128, N)


def solution(mesh):
    fine = Mesh(mesh.devices.reshape(2, 4, 2, 8, 2), DEPTH + ROW)
    return jax.shard_map(
        per_device,
        mesh=fine,
        in_specs=(P(None, DEPTH, ROW, None), P(ROW, None), P(DEPTH)),
        out_specs=P(None, DEPTH, ROW, None),
        check_vma=False,
    )
```

time: 483 us -> 420 us (0.87)
  waiting for transfers between devices: 171 us -> 132 us
  blocking collectives: 120 us -> 88.8 us
  other arithmetic: 36.2 us -> 7.71 us
  Pallas kernels: 89.1 us -> 114 us
  starting transfers between devices: 23.6 us -> 43.8 us
  local copies, waits for them, and re-layouts: 22.1 us -> 13.8 us
    ppermute x6 -> x2, waiting for transfers between devices: 84.5 us -> 9.68 us  [along_rows(): return lax.ppermute(block, DEPTH + ROW, route)]
    all_to_all x1 -> x6, waiting for transfers between devices: 0.01 us -> 33.4 us  [the longest x2 26.3 us: per_device(): returned.append(lax.all_to_all(sent, LAYER, 0, 0, tiled=True))]
    all_to_all x1 -> x6, starting transfers between devices: 7.82 us -> 37.9 us  [the longest x2 13.4 us: per_device(): returned.append(lax.all_to_all(sent, LAYER, 0, 0, tiled=True))]
    unnamed x1, blocking collectives: 63.3 us -> 37.5 us
    reduce_sum x2 -> x0, other arithmetic: 14.7 us -> none  [flux_of(): jnp.sum(depth_diff * depth_diff + row_diff * row_diff + col_diff * col_di...]
    slice x10 -> x2, local copies, waits for them, and re-layouts: 19.4 us -> 5.75 us  [the longest x1 4.69 us: per_device(): field[c].reshape(PLANES, 16, N)]
    ppermute x6 -> x2, starting transfers between devices: 15.7 us -> 5.84 us  [along_rows(): return lax.ppermute(block, DEPTH + ROW, route)]
    pallas_call x0 -> x1, Pallas kernels: none -> 9 us  [shrink(): pl.pallas_call(shrink_kernel, grid=(steps,), in_specs=[pl.BlockSpec(memor...]
  transfers between devices with their start and end apart: 9 -> 12, of which waited for: 3 -> 9; matrix products, arithmetic and copies ran while one was open for 5% -> 3% of each run, Pallas kernels for 0% -> 18%
where the time goes in v2:
time: 420 us; the launch traced here: 415 us
  waiting for transfers between devices  132 us (31%)
  Pallas kernels  114 us (27%)
  blocking collectives  88.8 us (21%)
  starting transfers between devices  43.8 us (10%)
  between operations  14.1 us (3%)
  local copies, waits for them, and re-layouts  13.8 us (3%)
  other arithmetic  7.71 us (2%)
    all_to_all x1, blocking collectives, per_device(): estimate = lax.all_to_all(estimate, DEPTH, 0, 0, tiled=True)  51.3 us
    reduce_scatter x2, waiting for transfers between devices, per_device(): image = lax.psum_scatter(partial, 'z', scatter_dimension=0, tiled=True)  50.9 us
    all_gather x2, waiting for transfers between devices, per_device(): misfit = lax.all_gather(image - tile, 'z', axis=0, tiled=True)  38.1 us
    pallas_call x2, Pallas kernels, backward_y(): pl.pallas_call(backward_y_kernel, grid=(CLASSES,), in_specs=[pl.BlockSpec...  37.8 us
    unnamed x1, blocking collectives  37.5 us
    pallas_call x2, Pallas kernels, forward_y(): pl.pallas_call(forward_y_kernel, grid=(CLASSES,), in_specs=[pl.BlockSpec(...  37.3 us
    all_to_all x2, waiting for transfers between devices, per_device(): returned.append(lax.all_to_all(sent, LAYER, 0, 0, tiled=True))  26.3 us
    pallas_call x1, Pallas kernels, backward_x(): pl.pallas_call(backward_x_kernel, grid=(128 // STEP_ROWS,), in_specs=[pl....  15.9 us
  transfers between devices with their start and end apart: 12, of which 9 were waited for; matrix products, arithmetic and copies ran while one was open for 3% of the time, Pallas kernels for 18%

profile of v2, /device:TPU:2, one launch (start us, length us, event | category | flops | bytes accessed | tf_op | source)
XLA Modules:
  0.0 414.9 jit_solution(5675173316324583543)
XLA Ops:
  9.6 14.4 %filter_x_forward.1 = (f32[32,136,128]{2,1,0:T(8,128)}, f32[32,136,128]{2,1,0:T(8,128)}) custom-call(f32[2,128,4096]{2,1,0:T(8,128)} %bitcast.16, f32[2,8,4096]{2,1,0:T(8,128)} %constant_dynamic-slice_fusion.hol_ref, f32[2,16,256]{2,1,0:T(8,128)} %constant.65.clone.tw_ref, f32[2,16,1,256]{3,2,1,0:T(1,128)} %pad_maximum_fusion.2.d_ref, ...), custom_call_target="tpu_custom_call" | custom-call | tf_op jit(solution)/shard_map/filter_x_forward/pallas_call | solution.py:304
  24.0 7.8 %all-to-all-start = ((f32[32,136,128]{2,1,0:T(8,128)}), f32[32,136,128]{2,1,0:T(8,128)}, u32[]{:S(2)}, u32[]{:S(2)}) async-start(f32[32,136,128]{2,1,0:T(8,128)} %get-tuple-element.15), calls=%async_computation | async-start | bytes 4456448 | tf_op jit(solution)/shard_map/all_to_all | solution.py:651
  33.1 37.5 %all-reduce = f32[8]{0:T(128)S(1)} all-reduce(f32[8]{0:T(128)S(1)} %dynamic-update-slice), channel_id=1, replica_groups=mesh['x_lo'=2,'y'=4,'x_hi'=2,'z'=8,'core'=2] {'x_lo','y'}, use_global_device_ids=true, to_apply=%add | all-reduce | flops 8 | bytes 64
  71.2 6.0 %all-to-all-start.2 = ((f32[32,136,128]{2,1,0:T(8,128)}), f32[32,136,128]{2,1,0:T(8,128)}, u32[]{:S(2)}, u32[]{:S(2)}) async-start(f32[32,136,128]{2,1,0:T(8,128)} %get-tuple-element.20), calls=%async_computation.3 | async-start | bytes 4456448 | tf_op jit(solution)/shard_map/all_to_all | solution.py:653
  78.1 18.6 %filter_y_forward.2 = (f32[8,2,64,256]{3,2,1,0:T(8,128)}, f32[1,2,64,256]{3,2,1,0:T(8,128)}) custom-call(s32[1]{0:T(128)} %bitcast.2.z_ref, f32[32,136,128]{2,1,0:T(8,128)} %all-to-all-done.g_ref, bf16[9,768,512]{2,1,0:T(8,128)(2,1)} %constant.68.clone.t_ref, bf16[9,1536,256]{2,1,0:T(8,128)(2,1)} %constant.69.clone.tt_ref, f32[9,16,512]{2,1,0:T(8,128)} %pad_maximum_fusion.cs_ref), custom_call_target="tpu_custom_call" | custom-call | tf_op jit(solution)/shard_map/filter_y_forward/pallas_call | solution.py:412
  96.8 41.3 %reduce-scatter.3.cloned.1.call-done = f32[1,2,64,256]{3,2,1,0:T(8,128)} async-done(((f32[8,2,64,256]{3,2,1,0:T(8,128)}), f32[1,2,64,256]{3,2,1,0:T(8,128)}) %reduce-scatter.3.cloned.1.call-update) | async-done | bytes 131088 | tf_op jit(solution)/shard_map/reduce_scatter | solution.py:661
  139.8 4.7 %fusion.5 = (f32[1,128,4096]{2,1,0:T(8,128)}, f32[1,128,4096]{2,1,0:T(8,128)}) fusion(f32[2,128,4096]{2,1,0:T(8,128)} %bitcast.17), kind=kLoop, calls=%fused_computation.18 | loop fusion | bytes 8388608 | tf_op jit(solution)/shard_map/slice | solution.py:656
  144.5 5.8 %all-to-all-start.4 = ((f32[8,16,4096]{2,1,0:T(8,128)}), f32[8,16,4096]{2,1,0:T(8,128)S(1)}, u32[]{:S(2)}, u32[]{:S(2)}) async-start(f32[8,16,4096]{2,1,0:T(8,128)} %bitcast.20), calls=%async_computation.6 | async-start | bytes 4194304 | tf_op jit(solution)/shard_map/all_to_all | solution.py:656
  150.3 18.7 %filter_y_forward.3 = (f32[8,2,64,256]{3,2,1,0:T(8,128)}, f32[1,2,64,256]{3,2,1,0:T(8,128)}) custom-call(s32[1]{0:T(128)} %bitcast.2.z_ref, f32[32,136,128]{2,1,0:T(8,128)} %all-to-all-done.2.g_ref, bf16[9,768,512]{2,1,0:T(8,128)(2,1)} %constant.68.clone.t_ref, bf16[9,1536,256]{2,1,0:T(8,128)(2,1)} %constant.69.clone.tt_ref, ...), custom_call_target="tpu_custom_call" | custom-call | tf_op jit(solution)/shard_map/filter_y_forward/pallas_call | solution.py:412
  172.2 4.8 %all-to-all-start.5 = ((f32[8,16,4096]{2,1,0:T(8,128)}), f32[8,16,4096]{2,1,0:T(8,128)}, u32[]{:S(2)}, u32[]{:S(2)}) async-start(f32[8,16,4096]{2,1,0:T(8,128)} %bitcast.19), calls=%async_computation.7 | async-start | bytes 4194304 | tf_op jit(solution)/shard_map/all_to_all | solution.py:656
  177.5 18.9 %filter_y_backward.2 = f32[32,128,128]{2,1,0:T(8,128)} custom-call(s32[1]{0:T(128)} %bitcast.2.z_ref, f32[8,2,64,256]{3,2,1,0:T(8,128)} %all-gather.3.cloned.1.call-done.m_ref, bf16[9,768,512]{2,1,0:T(8,128)(2,1)} %constant.68.clone.t_ref, bf16[9,1536,256]{2,1,0:T(8,128)(2,1)} %constant.69.clone.tt_ref, f32[9,16,512]{2,1,0:T(8,128)} %pad_maximum_fusion.cs_ref), custom_call_target="tpu_custom_call" | custom-call | tf_op jit(solution)/shard_map/filter_y_backward/pallas_call | solution.py:499
  196.4 5.2 %all-to-all-done.5.fi_ref = f32[8,16,4096]{2,1,0:T(8,128)} async-done(((f32[8,16,4096]{2,1,0:T(8,128)}), f32[8,16,4096]{2,1,0:T(8,128)}, u32[]{:S(2)}, u32[]{:S(2)}) %all-to-all-start.5) | async-done | bytes 2097184 | tf_op jit(solution)/shard_map/all_to_all | solution.py:656
  201.6 5.9 %all-to-all-start.1 = ((f32[32,128,128]{2,1,0:T(8,128)}), f32[32,128,128]{2,1,0:T(8,128)S(1)}, u32[]{:S(2)}, u32[]{:S(2)}) async-start(f32[32,128,128]{2,1,0:T(8,128)} %filter_y_backward.2), calls=%async_computation.2 | async-start | bytes 4194304 | tf_op jit(solution)/shard_map/all_to_all | solution.py:664
  207.6 9.6 %reduce-scatter.5.cloned.1.call-done = f32[1,2,64,256]{3,2,1,0:T(8,128)} async-done(((f32[8,2,64,256]{3,2,1,0:T(8,128)}), f32[1,2,64,256]{3,2,1,0:T(8,128)}) %reduce-scatter.5.cloned.1.call-update) | async-done | bytes 131088 | tf_op jit(solution)/shard_map/reduce_scatter | solution.py:661
  218.8 37.6 %all-gather.5.cloned.1.call-done.m_ref = f32[8,2,64,256]{3,2,1,0:T(8,128)} async-done(((f32[1,2,64,256]{3,2,1,0:T(8,128)}), f32[8,2,64,256]{3,2,1,0:T(8,128)}) %all-gather.5.cloned.1.call-update) | async-done | bytes 1048592 | tf_op jit(solution)/shard_map/all_gather | solution.py:662
  256.4 18.9 %filter_y_backward.3 = f32[32,128,128]{2,1,0:T(8,128)} custom-call(s32[1]{0:T(128)} %bitcast.2.z_ref, f32[8,2,64,256]{3,2,1,0:T(8,128)} %all-gather.5.cloned.1.call-done.m_ref, bf16[9,768,512]{2,1,0:T(8,128)(2,1)} %constant.68.clone.t_ref, bf16[9,1536,256]{2,1,0:T(8,128)(2,1)} %constant.69.clone.tt_ref, f32[9,16,512]{2,1,0:T(8,128)} %pad_maximum_fusion.cs_ref), custom_call_target="tpu_custom_call" | custom-call | tf_op jit(solution)/shard_map/filter_y_backward/pallas_call | solution.py:499
  276.7 7.5 %all-to-all-start.3 = ((f32[32,128,128]{2,1,0:T(8,128)}), f32[32,128,128]{2,1,0:T(8,128)}, u32[]{:S(2)}, u32[]{:S(2)}) async-start(f32[32,128,128]{2,1,0:T(8,128)} %filter_y_backward.3), calls=%async_computation.5 | async-start | bytes 4194304 | tf_op jit(solution)/shard_map/all_to_all | solution.py:664
  285.5 26.3 %all-to-all-done.3.gb_ref = f32[32,128,128]{2,1,0:T(8,128)} async-done(((f32[32,128,128]{2,1,0:T(8,128)}), f32[32,128,128]{2,1,0:T(8,128)}, u32[]{:S(2)}, u32[]{:S(2)}) %all-to-all-start.3) | async-done | bytes 2097184 | tf_op jit(solution)/shard_map/all_to_all | solution.py:664
  311.7 15.9 %filter_x_backward.1.m_ref.next_ref = f32[2,128,4096]{2,1,0:T(8,128)} custom-call(f32[32,128,128]{2,1,0:T(8,128)} %copy-done.3, f32[32,128,128]{2,1,0:T(8,128)} %all-to-all-done.3.gb_ref, f32[8,16,4096]{2,1,0:T(8,128)} %copy-done.2, f32[8,16,4096]{2,1,0:T(8,128)} %all-to-all-done.5.fi_ref, f32[2,16,256]{2,1,0:T(8,128)} %constant.65.clone.tw_ref, ...), custom_call_target="tpu_custom_call" | custom-call | tf_op jit(solution)/shard_map/filter_x_backward/pallas_call | solution.py:325
  328.7 3.5 collective-permute-start.1
  335.2 3.5 collective-permute-done.1.below_ref
  338.7 6.2 %collective-permute-done.above_ref = f32[2,8,4096]{2,1,0:T(8,128)S(1)} collective-permute-done((f32[2,8,4096]{2,1,0:T(8,128)S(1)}, f32[2,8,4096]{2,1,0:T(8,128)S(1)}, u32[]{:S(2)}, u32[]{:S(2)}) %collective-permute-start) | collective-permute-done | bytes 262176 | tf_op jit(solution)/shard_map/ppermute | solution.py:616
  345.6 9.0 %tv_shrink.1 = f32[8,2,16,4096]{3,2,1,0:T(8,128)} custom-call(s32[2]{0:T(128)} %add_convert_fusion.edge_ref, f32[2,128,4096]{2,1,0:T(8,128)} %filter_x_backward.1.m_ref.next_ref, f32[2,128,4096]{2,1,0:T(8,128)} %filter_x_backward.1.m_ref.next_ref, f32[2,8,4096]{2,1,0:T(8,128)} %copy-done.5, f32[2,8,4096]{2,1,0:T(8,128)} %copy-done.4), custom_call_target="tpu_custom_call" | custom-call | tf_op jit(solution)/shard_map/tv_shrink/pallas_call | solution.py:590
  354.6 51.3 %all_to_all.35 = f32[8,2,16,4096]{3,2,1,0:T(8,128)S(1)} all-to-all(f32[8,2,16,4096]{3,2,1,0:T(8,128)} %tv_shrink.1), channel_id=1, replica_groups=mesh['x_lo'=2,'y'=4,'x_hi'=2,'z'=8,'core'=2] {'x_lo','y'}, dimensions={0} | all-to-all | bytes 8388608 | tf_op jit(solution)/shard_map/all_to_all | solution.py:671
  (57 shorter events, 21.8 us)
Async XLA Ops:
  6.5 2.3 copy-start
  23.9 7.9 %copy-start.10 = (u32[256]{0:T(256)S(1)}, u32[256]{0:T(256)}, u32[]{:S(2)}) copy-start(u32[256]{0:T(256)} %constant.77) | copy-start | bytes 3076
  24.0 46.6 %copy-start.8 = (f32[9,256]{1,0:T(8,128)S(1)}, f32[9,256]{1,0:T(8,128)}, u32[]{:S(2)}) copy-start(f32[9,256]{1,0:T(8,128)} %constant.72) | copy-start | bytes 27652
  24.0 47.2 %copy-start.9 = (f32[9]{0:T(128)S(1)}, f32[9]{0:T(128)}, u32[]{:S(2)}) copy-start(f32[9]{0:T(128)} %constant.73) | copy-start | bytes 112
  24.0 47.3 %all-to-all-start = ((f32[32,136,128]{2,1,0:T(8,128)}), f32[32,136,128]{2,1,0:T(8,128)}, u32[]{:S(2)}, u32[]{:S(2)}) async-start(f32[32,136,128]{2,1,0:T(8,128)} %get-tuple-element.15), calls=%async_computation | async-start | bytes 4456448 | tf_op jit(solution)/shard_map/all_to_all | solution.py:651
  71.2 68.5 %all-to-all-start.2 = ((f32[32,136,128]{2,1,0:T(8,128)}), f32[32,136,128]{2,1,0:T(8,128)}, u32[]{:S(2)}, u32[]{:S(2)}) async-start(f32[32,136,128]{2,1,0:T(8,128)} %get-tuple-element.20), calls=%async_computation.3 | async-start | bytes 4456448 | tf_op jit(solution)/shard_map/all_to_all | solution.py:653
  77.3 60.8 %reduce-scatter.3.cloned.1.call-start = ((), (), s32[]{:S(2)}) async-start(), calls=%async_computation.9 | async-start | bytes 1179648 | tf_op jit(solution)/shard_map/reduce_scatter | solution.py:661
  96.7 80.8 %all-gather.3.cloned.1.call-start = ((), (), s32[]{:S(2)}) async-start(), calls=%async_computation.10 | async-start | bytes 1179648 | tf_op jit(solution)/shard_map/all_gather | solution.py:662
  144.5 26.4 %all-to-all-start.4 = ((f32[8,16,4096]{2,1,0:T(8,128)}), f32[8,16,4096]{2,1,0:T(8,128)S(1)}, u32[]{:S(2)}, u32[]{:S(2)}) async-start(f32[8,16,4096]{2,1,0:T(8,128)} %bitcast.20), calls=%async_computation.6 | async-start | bytes 4194304 | tf_op jit(solution)/shard_map/all_to_all | solution.py:656
  150.3 66.9 %reduce-scatter.5.cloned.1.call-start = ((), (), s32[]{:S(2)}) async-start(), calls=%async_computation.11 | async-start | bytes 1179648 | tf_op jit(solution)/shard_map/reduce_scatter | solution.py:661
  170.9 1.3 copy-start.2
  172.2 29.3 %all-to-all-start.5 = ((f32[8,16,4096]{2,1,0:T(8,128)}), f32[8,16,4096]{2,1,0:T(8,128)}, u32[]{:S(2)}, u32[]{:S(2)}) async-start(f32[8,16,4096]{2,1,0:T(8,128)} %bitcast.19), calls=%async_computation.7 | async-start | bytes 4194304 | tf_op jit(solution)/shard_map/all_to_all | solution.py:656
  196.4 20.8 %copy-start.6 = (f32[1,2,64,256]{3,2,1,0:T(8,128)S(1)}, f32[1,2,64,256]{3,2,1,0:T(8,128)}, u32[]{:S(2)}) copy-start(f32[1,2,64,256]{3,2,1,0:T(8,128)} %get-tuple-element.23) | copy-start | bytes 393220
  201.6 73.7 %all-to-all-start.1 = ((f32[32,128,128]{2,1,0:T(8,128)}), f32[32,128,128]{2,1,0:T(8,128)S(1)}, u32[]{:S(2)}, u32[]{:S(2)}) async-start(f32[32,128,128]{2,1,0:T(8,128)} %filter_y_backward.2), calls=%async_computation.2 | async-start | bytes 4194304 | tf_op jit(solution)/shard_map/all_to_all | solution.py:664
  207.5 48.8 %all-gather.5.cloned.1.call-start = ((), (), s32[]{:S(2)}) async-start(), calls=%async_computation.12 | async-start | bytes 1179648 | tf_op jit(solution)/shard_map/all_gather | solution.py:662
  275.3 8.9 %copy-start.7 = (f32[16,256]{1,0:T(8,128)S(1)}, f32[16,256]{1,0:T(8,128)}, u32[]{:S(2)}) copy-start(f32[16,256]{1,0:T(8,128)} %constant.74) | copy-start | bytes 49156
  275.3 1.4 copy-start.3
  276.7 35.0 %all-to-all-start.3 = ((f32[32,128,128]{2,1,0:T(8,128)}), f32[32,128,128]{2,1,0:T(8,128)}, u32[]{:S(2)}, u32[]{:S(2)}) async-start(f32[32,128,128]{2,1,0:T(8,128)} %filter_y_backward.3), calls=%async_computation.5 | async-start | bytes 4194304 | tf_op jit(solution)/shard_map/all_to_all | solution.py:664
  328.7 9.9 %collective-permute-start.1 = (f32[2,8,4096]{2,1,0:T(8,128)S(1)}, f32[2,8,4096]{2,1,0:T(8,128)S(1)}, u32[]{:S(2)}, u32[]{:S(2)}) collective-permute-start(f32[2,8,4096]{2,1,0:T(8,128)S(1)} %get-tuple-element.25), channel_id=1, source_target_pairs={{32,0},{64,32},{96,64},{128,96},{160,128},{192,160},{224,192},{1,2... | collective-permute-start | bytes 786440 | tf_op jit(solution)/shard_map/ppermute | solution.py:616
  332.2 12.7 %collective-permute-start = (f32[2,8,4096]{2,1,0:T(8,128)S(1)}, f32[2,8,4096]{2,1,0:T(8,128)S(1)}, u32[]{:S(2)}, u32[]{:S(2)}) collective-permute-start(f32[2,8,4096]{2,1,0:T(8,128)S(1)} %get-tuple-element.26), channel_id=1, source_target_pairs={{0,32},{32,64},{64,96},{96,128},{128,160},{160,192},{192,224},{224... | collective-permute-start | bytes 786440 | tf_op jit(solution)/shard_map/ppermute | solution.py:616
  338.7 6.2 %copy-start.4 = (f32[2,8,4096]{2,1,0:T(8,128)}, f32[2,8,4096]{2,1,0:T(8,128)S(1)}, u32[]{:S(2)}) copy-start(f32[2,8,4096]{2,1,0:T(8,128)S(1)} %collective-permute-done.1.below_ref) | copy-start | bytes 786436
  344.9 0.7 copy-start.5
  406.0 2.4 copy-start.1
Sparse Core Ops, SparseCore 0:
  96.8 41.2 reduce-scatter.2
  139.9 37.5 all-gather.2
  180.0 37.0 reduce-scatter.4
  218.9 37.4 all-gather.4

commit v3 on v2

--- a/solution.py
+++ b/solution.py
@@ -20,7 +20,6 @@
 CLASSES = 9
 PLANES = 8
 LANES = 128
-HALF = 64
 F32 = jnp.float32
 BF16 = jnp.bfloat16
 
@@ -224,58 +223,41 @@
     return jnp.concatenate([factor] * (STEP_ROWS // factor.shape[0]), axis=0)
 
 
-def low_lanes(shape):
-    return lax.broadcasted_iota(jnp.int32, shape, len(shape) - 1) < HALF
-
-
-def exchange_halves(first, second):
-    low = low_lanes(first.shape)
-    axis = first.ndim - 1
-    return (
-        jnp.where(low, first, pltpu.roll(second, HALF, axis)),
-        jnp.where(low, pltpu.roll(first, HALF, axis), second),
-    )
-
-
-def forward_x_kernel(f_ref, hol_ref, tw_ref, d_ref, wf_ref, wi_ref, a_ref, b_ref, x_ref):
+def forward_x_kernel(f_ref, hol_ref, tw_ref, d_ref, wf_ref, wi_ref, o_ref, x_ref):
     step = pl.program_id(0)
 
     @pl.when(step == 0)
     def _():
         for j in range(32):
-            lanes = slice(j * LANES, (j + 1) * LANES)
-            first, second = exchange_halves(hol_ref[0, :, lanes], hol_ref[1, :, lanes])
-            a_ref[j, 128:136, :] = first
-            b_ref[j, 128:136, :] = second
+            o_ref[j, 256:272, :] = hol_ref[:, j * LANES : (j + 1) * LANES]
 
     def load(r, j):
         rows, lanes = slice(8 * r, 8 * r + 8), slice(j * LANES, (j + 1) * LANES)
         return f_ref[0, rows, lanes], f_ref[1, rows, lanes]
 
     def store(r, j, value):
-        rows = pl.ds(pl.multiple_of(step * STEP_ROWS + 8 * r, 8), 8)
-        first, second = exchange_halves(*value)
-        a_ref[j, rows, :] = first
-        b_ref[j, rows, :] = second
+        for c in range(2):
+            start = pl.multiple_of(step * STEP_ROWS + 128 * c + 8 * r, 8)
+            o_ref[j, pl.ds(start, 8), :] = value[c]
 
     filter_rows(load, store, tw_ref, d_ref, wf_ref, wi_ref, x_ref)
 
 
-def backward_x_kernel(ga_ref, gb_ref, fr_ref, fi_ref, tw_ref, d_ref, wf_ref, wi_ref, o_ref, x_ref, f_ref):
+def backward_x_kernel(g_ref, held_ref, tw_ref, d_ref, wf_ref, wi_ref, o_ref, x_ref, f_ref):
     step = pl.program_id(0)
 
     @pl.when(step == 0)
     def _():
-        for c, source in ((0, fr_ref), (1, fi_ref)):
+        for c in range(2):
             for p in range(PLANES):
                 for j in range(N // LANES):
-                    f_ref[c, j, pl.ds(p, 16, stride=PLANES), :] = source[
-                        p, :, j * LANES : (j + 1) * LANES
+                    f_ref[c, j, pl.ds(p, 16, stride=PLANES), :] = held_ref[
+                        p, c, :, j * LANES : (j + 1) * LANES
                     ]
 
     def load(r, j):
         rows = slice(8 * r, 8 * r + 8)
-        return exchange_halves(ga_ref[j, rows, :], gb_ref[j, rows, :])
+        return g_ref[j, 0, rows, :], g_ref[j, 1, rows, :]
 
     def store(r, j, value):
         rows, lanes = slice(8 * r, 8 * r + 8), slice(j * LANES, (j + 1) * LANES)
@@ -288,6 +270,10 @@
 
 def whole(shape):
     return pl.BlockSpec(shape, lambda *_: (0,) * len(shape))
+
+
+def cost_of(microseconds):
+    return pl.CostEstimate(flops=0, bytes_accessed=microseconds * 3_000_000, transcendentals=0)
 
 
 def params():
@@ -306,30 +292,29 @@
         grid=(128 // STEP_ROWS,),
         in_specs=[
             pl.BlockSpec((2, STEP_ROWS, N), lambda i: (0, i, 0)),
-            whole((2, 8, N)),
+            whole((16, N)),
             whole((2, RADIX, INNER)),
             whole((2, RADIX, 1, INNER)),
             whole((1536, 512)),
             whole((1536, 512)),
         ],
-        out_specs=[whole((32, 136, LANES))] * 2,
-        out_shape=[jax.ShapeDtypeStruct((32, 136, LANES), F32)] * 2,
+        out_specs=whole((32, 272, LANES)),
+        out_shape=jax.ShapeDtypeStruct((32, 272, LANES), F32),
         scratch_shapes=[pltpu.VMEM((RADIX * STEP_ROWS, 2 * INNER), F32)],
         compiler_params=params(),
+        cost_estimate=cost_of(14),
         name="filter_x_forward",
     )(field, hologram_rows, tw, transfer, wf, wi)
 
 
-def backward_x(first, second, field_real, field_imag, transfer):
+def backward_x(gradient, held, transfer):
     tw, wf, wi = x_tables()
     return pl.pallas_call(
         backward_x_kernel,
         grid=(128 // STEP_ROWS,),
         in_specs=[
-            pl.BlockSpec((32, STEP_ROWS, LANES), lambda i: (0, i, 0)),
-            pl.BlockSpec((32, STEP_ROWS, LANES), lambda i: (0, i, 0)),
-            whole((PLANES, 16, N)),
-            whole((PLANES, 16, N)),
+            pl.BlockSpec((32, 2, STEP_ROWS, LANES), lambda i: (0, 0, i, 0)),
+            whole((PLANES, 2, 16, N)),
             whole((2, RADIX, INNER)),
             whole((2, RADIX, PLANES, INNER)),
             whole((1536, 512)),
@@ -342,11 +327,9 @@
             pltpu.VMEM((2, N // LANES, 128, LANES), F32),
         ],
         compiler_params=params(),
+        cost_estimate=cost_of(16),
         name="filter_x_backward",
-    )(first, second, field_real, field_imag, tw, transfer, wf, wi)
-
-
-DOT_PLANES = 4
+    )(gradient, held, tw, transfer, wf, wi)
 
 
 def forward_y_kernel(z_ref, g_ref, t_ref, tt_ref, cs_ref, o_ref, h_ref, u_ref, s_ref):
@@ -356,35 +339,34 @@
     def _():
         @pl.loop(0, PLANES)
         def _(p):
-            held = pl.ds(pl.multiple_of(p * LANES, LANES), LANES)
             for core in range(2):
-                upper = g_ref[p * 4 + core, :128, :].T
-                lower = g_ref[p * 4 + 2 + core, :128, :].T
-                for parity, value in ((0, upper + lower), (1, upper - lower)):
-                    high, low = halves(value)
-                    for part, piece in ((0, high), (1, low), (2, high)):
-                        start = part * INNER + core * 128
-                        u_ref[parity, held, start : start + 128] = piece
+                for c in range(2):
+                    rows = slice(c * 128, (c + 1) * 128)
+                    upper = g_ref[p * 4 + core, rows, :].T
+                    lower = g_ref[p * 4 + 2 + core, rows, :].T
+                    for parity, value in ((0, upper + lower), (1, upper - lower)):
+                        high, low = halves(value)
+                        for part, piece in ((0, high), (1, low), (2, high)):
+                            start = part * INNER + core * 128
+                            u_ref[parity, p, c * LANES : (c + 1) * LANES, start : start + 128] = (
+                                piece
+                            )
 
         for upper in range(2):
             for core in range(2):
-                rows = [g_ref[p * 4 + upper * 2 + core, 128:, :] for p in range(PLANES)]
+                rows = [g_ref[p * 4 + upper * 2 + core, 256:, :] for p in range(PLANES)]
                 block = jnp.concatenate(rows, axis=0).T
-                block = jnp.concatenate([block[:HALF], block[HALF:]], axis=1)
                 h_ref[0, upper, :, core * 128 : (core + 1) * 128] = block
 
     parity = lax.rem(step, 2)
     total = None
-    for chunk in range(PLANES // DOT_PLANES):
-        rows = slice(chunk * DOT_PLANES * LANES, (chunk + 1) * DOT_PLANES * LANES)
-        result = jnp.dot(u_ref[parity, rows, :], t_ref[0], preferred_element_type=F32)
-        for i in range(DOT_PLANES):
-            p = chunk * DOT_PLANES + i
-            piece = (
-                cs_ref[0, 2 * p : 2 * p + 1, :] * result[i * LANES : i * LANES + HALF]
-                + cs_ref[0, 2 * p + 1 : 2 * p + 2, :] * result[i * LANES + HALF : (i + 1) * LANES]
-            )
-            total = piece if total is None else total + piece
+    for p in range(PLANES):
+        result = jnp.dot(u_ref[parity, p], t_ref[0], preferred_element_type=F32)
+        piece = (
+            cs_ref[0, 2 * p : 2 * p + 1, :] * result[:LANES]
+            + cs_ref[0, 2 * p + 1 : 2 * p + 2, :] * result[LANES:]
+        )
+        total = piece if total is None else total + piece
     turned = jnp.concatenate([-total[:, INNER:], total[:, :INNER]], axis=1)
     high, low = halves(jnp.concatenate([total, turned], axis=0))
     s_ref[step] = jnp.dot(
@@ -395,10 +377,10 @@
     def _():
         shift = z_ref[0]
 
-        @pl.loop(0, HALF // 8)
+        @pl.loop(0, LANES // 8)
         def _(i):
             rows = pl.ds(pl.multiple_of(i * 8, 8), 8)
-            other = pl.ds(pl.multiple_of(HALF + i * 8, 8), 8)
+            other = pl.ds(pl.multiple_of(LANES + i * 8, 8), 8)
             for half in range(2):
                 lanes = slice(half * LANES, (half + 1) * LANES)
                 values = [(s_ref[k, rows, lanes], s_ref[k, other, lanes]) for k in range(CLASSES)]
@@ -414,21 +396,22 @@
         grid=(CLASSES,),
         in_specs=[
             pl.BlockSpec(memory_space=pltpu.SMEM),
-            whole((32, 136, LANES)),
+            whole((32, 272, LANES)),
             pl.BlockSpec((1, 768, 512), lambda k: (k, 0, 0)),
             pl.BlockSpec((1, 1536, 256), lambda k: (k, 0, 0)),
             pl.BlockSpec((1, 16, 512), lambda k: (k, 0, 0)),
         ],
-        out_specs=[whole((8, 2, HALF, INNER)), whole((1, 2, HALF, INNER))],
+        out_specs=[whole((8, 2, LANES, INNER)), whole((1, 2, LANES, INNER))],
         out_shape=[
-            jax.ShapeDtypeStruct((8, 2, HALF, INNER), F32),
-            jax.ShapeDtypeStruct((1, 2, HALF, INNER), F32),
+            jax.ShapeDtypeStruct((8, 2, LANES, INNER), F32),
+            jax.ShapeDtypeStruct((1, 2, LANES, INNER), F32),
         ],
         scratch_shapes=[
-            pltpu.VMEM((2, PLANES * LANES, 768), BF16),
-            pltpu.VMEM((CLASSES, LANES, INNER), F32),
+            pltpu.VMEM((2, PLANES, 2 * LANES, 768), BF16),
+            pltpu.VMEM((CLASSES, 2 * LANES, INNER), F32),
         ],
         compiler_params=params(),
+        cost_estimate=cost_of(32),
         name="filter_y_forward",
     )(z_index, received, jnp.asarray(forward), jnp.asarray(backward), factors)
 
@@ -440,10 +423,10 @@
     def _():
         shift = z_ref[0]
 
-        @pl.loop(0, HALF // 8)
+        @pl.loop(0, LANES // 8)
         def _(i):
             rows = pl.ds(pl.multiple_of(i * 8, 8), 8)
-            other = pl.ds(pl.multiple_of(HALF + i * 8, 8), 8)
+            other = pl.ds(pl.multiple_of(LANES + i * 8, 8), 8)
             for half in range(2):
                 lanes = slice(half * LANES, (half + 1) * LANES)
                 blocks = []
@@ -456,25 +439,27 @@
 
         @pl.loop(0, PLANES)
         def _(p):
-            held = pl.ds(pl.multiple_of(p * LANES, LANES), LANES)
             for parity in range(2):
-                a_ref[parity, held, :] = jnp.zeros((LANES, INNER), F32)
+                a_ref[parity, p] = jnp.zeros((2 * LANES, INNER), F32)
 
     parity = lax.rem(step, 2)
     high, low = halves(x_ref[step])
     mixed = jnp.dot(
         jnp.concatenate([high, low, high], axis=1), t_ref[0], preferred_element_type=F32
     )
-    cosine = mixed[:HALF, :INNER] + mixed[HALF:, INNER:]
-    sine = mixed[:HALF, INNER:] - mixed[HALF:, :INNER]
+    cosine = mixed[:LANES, :INNER] + mixed[LANES:, INNER:]
+    sine = mixed[:LANES, INNER:] - mixed[LANES:, :INNER]
     spectrum = jnp.concatenate([cosine, sine], axis=1)
-    for chunk in range(PLANES // DOT_PLANES):
-        rows = slice(chunk * DOT_PLANES * LANES, (chunk + 1) * DOT_PLANES * LANES)
-        pieces = []
-        for row in range(2 * DOT_PLANES * chunk, 2 * DOT_PLANES * (chunk + 1)):
-            pieces.append(cs_ref[0, row : row + 1, :] * spectrum)
-        high, low = halves(jnp.concatenate(pieces, axis=0))
-        a_ref[parity, rows, :] += jnp.dot(
+    for p in range(PLANES):
+        product = jnp.concatenate(
+            [
+                cs_ref[0, 2 * p : 2 * p + 1, :] * spectrum,
+                cs_ref[0, 2 * p + 1 : 2 * p + 2, :] * spectrum,
+            ],
+            axis=0,
+        )
+        high, low = halves(product)
+        a_ref[parity, p] += jnp.dot(
             jnp.concatenate([high, low, high], axis=1), tt_ref[0], preferred_element_type=F32
         )
 
@@ -482,16 +467,17 @@
     def _():
         @pl.loop(0, PLANES)
         def _(p):
-            rows = pl.ds(pl.multiple_of(p * LANES, LANES), LANES)
             for core in range(2):
                 lanes = slice(core * 128, (core + 1) * 128)
-                even, odd = a_ref[0, rows, lanes], a_ref[1, rows, lanes]
-                upper, lower = (even + odd).T, (even - odd).T
-                for owner in range(PLANES):
-                    part = slice(owner * 16, owner * 16 + 16)
-                    held = pl.ds(p, 16, stride=PLANES)
-                    o_ref[owner * 4 + core, held, :] = upper[part]
-                    o_ref[owner * 4 + 2 + core, held, :] = lower[part]
+                for c in range(2):
+                    rows = slice(c * LANES, (c + 1) * LANES)
+                    even, odd = a_ref[0, p, rows, lanes], a_ref[1, p, rows, lanes]
+                    upper, lower = (even + odd).T, (even - odd).T
+                    for owner in range(PLANES):
+                        part = slice(owner * 16, owner * 16 + 16)
+                        held = pl.ds(p, 16, stride=PLANES)
+                        o_ref[owner * 4 + core, c, held, :] = upper[part]
+                        o_ref[owner * 4 + 2 + core, c, held, :] = lower[part]
 
 
 def backward_y(z_index, misfit, factors):
@@ -501,20 +487,125 @@
         grid=(CLASSES,),
         in_specs=[
             pl.BlockSpec(memory_space=pltpu.SMEM),
-            whole((8, 2, HALF, INNER)),
+            whole((8, 2, LANES, INNER)),
             pl.BlockSpec((1, 768, 512), lambda k: (k, 0, 0)),
             pl.BlockSpec((1, 1536, 256), lambda k: (k, 0, 0)),
             pl.BlockSpec((1, 16, 512), lambda k: (k, 0, 0)),
         ],
-        out_specs=whole((32, 128, LANES)),
-        out_shape=jax.ShapeDtypeStruct((32, 128, LANES), F32),
+        out_specs=whole((32, 2, 128, LANES)),
+        out_shape=jax.ShapeDtypeStruct((32, 2, 128, LANES), F32),
         scratch_shapes=[
-            pltpu.VMEM((CLASSES, LANES, INNER), F32),
-            pltpu.VMEM((2, PLANES * LANES, INNER), F32),
+            pltpu.VMEM((CLASSES, 2 * LANES, INNER), F32),
+            pltpu.VMEM((2, PLANES, 2 * LANES, INNER), F32),
         ],
         compiler_params=params(),
+        cost_estimate=cost_of(30),
         name="filter_y_backward",
     )(z_index, misfit, jnp.asarray(forward), jnp.asarray(backward), factors)
+
+
+SUBS = 2
+LAYERS = 8
+
+
+def z_exchange_kernel(p_ref, h_ref, o_ref, r_ref, sum_send, sum_recv, all_send, all_recv):
+    me = lax.axis_index("z")
+    at = lambda distance: lax.rem(me + distance + 2 * LAYERS, LAYERS)
+    right, left = at(1), at(-1)
+    barrier = pltpu.get_barrier_semaphore()
+    for neighbour in (left, right):
+        pl.semaphore_signal(
+            barrier,
+            inc=1,
+            device_id={"z": neighbour},
+            device_id_type=pl.DeviceIdType.MESH,
+        )
+    pl.semaphore_wait(barrier, 2)
+
+    size = LANES // SUBS
+    rings = [(way, sub) for sub in range(SUBS) for way in range(2)]
+
+    def send(source, target, send_sem, recv_sem, way):
+        return pltpu.make_async_remote_copy(
+            src_ref=source,
+            dst_ref=target,
+            send_sem=send_sem,
+            recv_sem=recv_sem,
+            device_id={"z": (right, left)[way]},
+            device_id_type=pl.DeviceIdType.MESH,
+        )
+
+    started, arrived = [], {}
+    for step in range(LAYERS):
+        for way, sub in rings:
+            rows = slice(sub * size, (sub + 1) * size)
+            block = at((-1 - step) if way == 0 else (1 + step))
+            slot = r_ref.at[way, sub]
+            if step:
+                arrived[way, sub].wait_recv()
+                if step < LAYERS - 1:
+                    r_ref[way, sub, step - 1] += p_ref[block, way, rows, :]
+                else:
+                    o_ref[me, way, rows, :] = (
+                        r_ref[way, sub, step - 1] + p_ref[me, way, rows, :]
+                    ) - h_ref[0, way, rows, :]
+            if step < LAYERS - 1:
+                source = p_ref.at[block, way, rows, :] if step == 0 else slot.at[step - 1]
+                copy = send(
+                    source,
+                    slot.at[step],
+                    sum_send.at[way, sub, step],
+                    sum_recv.at[way, sub, step],
+                    way,
+                )
+                copy.start()
+                started.append(copy)
+                arrived[way, sub] = copy
+            else:
+                place = o_ref.at[me, way, rows, :]
+                copy = send(
+                    place, place, all_send.at[way, sub, 0], all_recv.at[way, sub, 0], way
+                )
+                copy.start()
+                started.append(copy)
+                arrived[way, sub] = copy
+    for step in range(1, LAYERS):
+        for way, sub in rings:
+            rows = slice(sub * size, (sub + 1) * size)
+            arrived[way, sub].wait_recv()
+            if step < LAYERS - 1:
+                place = o_ref.at[at(-step if way == 0 else step), way, rows, :]
+                copy = send(
+                    place, place, all_send.at[way, sub, step], all_recv.at[way, sub, step], way
+                )
+                copy.start()
+                started.append(copy)
+                arrived[way, sub] = copy
+    for copy in started:
+        copy.wait_send()
+
+
+def z_exchange(partial, tile):
+    steps = LAYERS - 1
+    vmem = pl.BlockSpec(memory_space=pltpu.VMEM)
+    return pl.pallas_call(
+        z_exchange_kernel,
+        in_specs=[vmem, vmem],
+        out_specs=vmem,
+        out_shape=jax.ShapeDtypeStruct((LAYERS, 2, LANES, INNER), F32),
+        scratch_shapes=[
+            pltpu.VMEM((2, SUBS, steps, LANES // SUBS, INNER), F32),
+            pltpu.SemaphoreType.DMA((2, SUBS, steps)),
+            pltpu.SemaphoreType.DMA((2, SUBS, steps)),
+            pltpu.SemaphoreType.DMA((2, SUBS, steps)),
+            pltpu.SemaphoreType.DMA((2, SUBS, steps)),
+        ],
+        compiler_params=pltpu.CompilerParams(
+            collective_id=0, has_side_effects=True, vmem_limit_bytes=32 << 20
+        ),
+        cost_estimate=cost_of(50),
+        name="z_exchange",
+    )(partial, tile)
 
 
 TV_ROWS = 8
@@ -604,6 +695,7 @@
             pltpu.VMEM((2, PLANES, N), F32),
         ],
         compiler_params=params(),
+        cost_estimate=cost_of(9),
         name="tv_shrink",
     )(edges, moved, moved, above, below)
 
@@ -644,25 +736,17 @@
     factors = factors.reshape(CLASSES, 2 * PLANES, INNER)
     factors = jnp.concatenate([factors, factors], axis=2)
 
-    hologram_rows = lax.dynamic_slice_in_dim(
-        hologram.reshape(2, HALF, N), depth_index * 8, 8, axis=1
-    )
+    hologram_rows = lax.dynamic_slice_in_dim(hologram, depth_index * 16, 16, 0)
     sent = forward_x(field, hologram_rows, x_forward)
-    first = lax.all_to_all(sent[0], LAYER, 0, 0, tiled=True)
-    first, later = lax.optimization_barrier((first, sent[1]))
-    second = lax.all_to_all(later, LAYER, 0, 0, tiled=True)
-    second, field = lax.optimization_barrier((second, field))
-    held = [
-        lax.all_to_all(field[c].reshape(PLANES, 16, N), DEPTH, 0, 0, tiled=True) for c in range(2)
-    ]
-    returned = []
-    for received in (first, second):
-        partial, tile = forward_y(z_index, received, factors)
-        image = lax.psum_scatter(partial, "z", scatter_dimension=0, tiled=True)
-        misfit = lax.all_gather(image - tile, "z", axis=0, tiled=True)
-        sent = backward_y(z_index, misfit, factors)
-        returned.append(lax.all_to_all(sent, LAYER, 0, 0, tiled=True))
-    moved = backward_x(returned[0], returned[1], held[0], held[1], x_backward)
+    received = lax.all_to_all(sent, LAYER, 0, 0, tiled=True)
+    partial, tile = forward_y(z_index, received, factors)
+    field, partial = lax.optimization_barrier((field, partial))
+    held = jnp.transpose(field.reshape(2, PLANES, 16, N), (1, 0, 2, 3))
+    held = lax.all_to_all(held, DEPTH, 0, 0, tiled=True)
+    misfit = z_exchange(partial, tile)
+    sent = backward_y(z_index, misfit, factors)
+    received = lax.all_to_all(sent, LAYER, 0, 0, tiled=True)
+    moved = backward_x(received, held, x_backward)
     above = along_rows(moved[:, 120:], 1)
     below = along_rows(moved[:, :8], -1)
     line = row_index * 8 + depth_index

time: 420 us -> 383 us (0.912)
  waiting for transfers between devices: 132 us -> 55.5 us
  Pallas kernels: 114 us -> 157 us
  blocking collectives: 88.8 us -> 120 us
  between operations: 14.1 us -> 0.98 us
  starting transfers between devices: 43.8 us -> 33.5 us
    pallas_call x0 -> x1, Pallas kernels: none -> 60.2 us  [z_exchange(): pl.pallas_call(z_exchange_kernel, in_specs=[vmem, vmem], out_specs=vmem,...]
    reduce_scatter x2 -> x0, waiting for transfers between devices: 50.9 us -> none  [per_device(): image = lax.psum_scatter(partial, 'z', scatter_dimension=0, tiled=True)]
    all_gather x2 -> x0, waiting for transfers between devices: 38.1 us -> none  [per_device(): misfit = lax.all_gather(image - tile, 'z', axis=0, tiled=True)]
    unnamed x1, blocking collectives: 37.5 us -> 63.4 us
    all_to_all x6 -> x3, waiting for transfers between devices: 33.4 us -> 50.5 us  [the longest x2 50.5 us: per_device(): received = lax.all_to_all(sent, LAYER, 0, 0, tiled=True)]
    all_to_all x6 -> x3, starting transfers between devices: 37.9 us -> 25.6 us  [the longest x2 20.8 us: per_device(): received = lax.all_to_all(sent, LAYER, 0, 0, tiled=True)]
    pallas_call x2 -> x1, Pallas kernels: 37.8 us -> 28.7 us  [backward_y(): pl.pallas_call(backward_y_kernel, grid=(CLASSES,), in_specs=[pl.BlockSpec...]
    pallas_call x2 -> x1, Pallas kernels: 37.3 us -> 31.1 us  [forward_y(): pl.pallas_call(forward_y_kernel, grid=(CLASSES,), in_specs=[pl.BlockSpec(...]
  transfers between devices with their start and end apart: 12 -> 5, of which waited for: 9 -> 3; matrix products, arithmetic and copies ran while one was open for 3% -> 1% of each run, Pallas kernels for 18% -> 23%
where the time goes in v3:
time: 383 us; the launch traced here: 382 us
  Pallas kernels  157 us (41%)
  blocking collectives  120 us (31%)
  waiting for transfers between devices  55.5 us (14%)
  starting transfers between devices  33.5 us (9%)
  local copies, waits for them, and re-layouts  10.3 us (3%)
  other arithmetic  4.48 us (1%)
    unnamed x1, blocking collectives  63.4 us
    pallas_call x1, Pallas kernels, z_exchange(): pl.pallas_call(z_exchange_kernel, in_specs=[vmem, vmem], out_specs=vmem,...  60.2 us
    all_to_all x1, blocking collectives, per_device(): estimate = lax.all_to_all(estimate, DEPTH, 0, 0, tiled=True)  56.6 us
    all_to_all x2, waiting for transfers between devices, per_device(): received = lax.all_to_all(sent, LAYER, 0, 0, tiled=True)  50.5 us
    pallas_call x1, Pallas kernels, forward_y(): pl.pallas_call(forward_y_kernel, grid=(CLASSES,), in_specs=[pl.BlockSpec(...  31.1 us
    pallas_call x1, Pallas kernels, backward_y(): pl.pallas_call(backward_y_kernel, grid=(CLASSES,), in_specs=[pl.BlockSpec...  28.7 us
    all_to_all x2, starting transfers between devices, per_device(): received = lax.all_to_all(sent, LAYER, 0, 0, tiled=True)  20.8 us
    pallas_call x1, Pallas kernels, backward_x(): pl.pallas_call(backward_x_kernel, grid=(128 // STEP_ROWS,), in_specs=[pl....  14.8 us
  transfers between devices with their start and end apart: 5, of which 3 were waited for; matrix products, arithmetic and copies ran while one was open for 1% of the time, Pallas kernels for 23%

profile of v3, /device:TPU:2, one launch (start us, length us, event | category | flops | bytes accessed | tf_op | source)
XLA Modules:
  0.0 382.0 jit_solution(1950359632790178881)
XLA Ops:
  0.8 0.8 fusion.1
  3.0 13.4 %filter_x_forward.1 = f32[32,272,128]{2,1,0:T(8,128)} custom-call(f32[2,128,4096]{2,1,0:T(8,128)} %bitcast.16, f32[16,4096]{1,0:T(8,128)} %constant_dynamic-slice_fusion.hol_ref, f32[2,16,256]{2,1,0:T(8,128)} %constant.65.clone.tw_ref, f32[2,16,1,256]{3,2,1,0:T(1,128)} %pad_maximum_fusion.2.d_ref, bf16[1536,512]{1,0:T(8,128)(2,1)} %constant.66.clone.wf_ref, ...), custom_call_target="tpu_custom_call" | custom-call | bytes 42000000 | tf_op jit(solution)/shard_map/filter_x_forward/pallas_call | solution.py:290
  16.4 7.8 %all-to-all-start = ((f32[32,272,128]{2,1,0:T(8,128)}), f32[32,272,128]{2,1,0:T(8,128)}, u32[]{:S(2)}, u32[]{:S(2)}) async-start(f32[32,272,128]{2,1,0:T(8,128)} %filter_x_forward.1), calls=%async_computation | async-start | bytes 8912896 | tf_op jit(solution)/shard_map/all_to_all | solution.py:741
  24.8 0.8 dynamic-update-slice
  25.6 63.4 %all-reduce = f32[8]{0:T(128)S(1)} all-reduce(f32[8]{0:T(128)S(1)} %dynamic-update-slice), channel_id=1, replica_groups=mesh['x_lo'=2,'y'=4,'x_hi'=2,'z'=8,'core'=2] {'x_lo','y'}, use_global_device_ids=true, to_apply=%add | all-reduce | flops 8 | bytes 64
  89.6 0.7 pad_maximum_fusion.cs_ref
  90.3 31.1 %filter_y_forward.1 = (f32[8,2,128,256]{3,2,1,0:T(8,128)}, f32[1,2,128,256]{3,2,1,0:T(8,128)}) custom-call(s32[1]{0:T(128)} %bitcast.2.z_ref, f32[32,272,128]{2,1,0:T(8,128)} %all-to-all-done.g_ref, bf16[9,768,512]{2,1,0:T(8,128)(2,1)} %constant.68.clone.t_ref, bf16[9,1536,256]{2,1,0:T(8,128)(2,1)} %constant.69.clone.tt_ref, ...), custom_call_target="tpu_custom_call" | custom-call | bytes 96000000 | tf_op jit(solution)/shard_map/filter_y_forward/pallas_call | solution.py:394
  121.4 2.5 copy.28
  123.9 4.8 %all-to-all-start.2 = ((f32[8,2,16,4096]{3,2,1,0:T(8,128)}), f32[8,2,16,4096]{3,2,1,0:T(8,128)}, u32[]{:S(2)}, u32[]{:S(2)}) async-start(f32[8,2,16,4096]{3,2,1,0:T(8,128)} %bitcast.18), calls=%async_computation.2 | async-start | bytes 8388608 | tf_op jit(solution)/shard_map/all_to_all | solution.py:745
  128.7 60.2 %z_exchange.1.m_ref = f32[8,2,128,256]{3,2,1,0:T(8,128)S(1)} custom-call(f32[8,2,128,256]{3,2,1,0:T(8,128)S(1)} %copy-done.3, f32[1,2,128,256]{3,2,1,0:T(8,128)S(1)} %copy-done.4), custom_call_target="tpu_custom_call" | custom-call | bytes 150000000 | tf_op jit(solution)/shard_map/z_exchange/pallas_call | solution.py:591
  189.0 1.4 copy-done.2
  190.3 28.7 %filter_y_backward.1 = f32[32,2,128,128]{3,2,1,0:T(8,128)} custom-call(s32[1]{0:T(128)} %bitcast.2.z_ref, f32[8,2,128,256]{3,2,1,0:T(8,128)} %copy-done.2, bf16[9,768,512]{2,1,0:T(8,128)(2,1)} %constant.68.clone.t_ref, bf16[9,1536,256]{2,1,0:T(8,128)(2,1)} %constant.69.clone.tt_ref, f32[9,16,512]{2,1,0:T(8,128)} %pad_maximum_fusion.cs_ref), custom_call_target="tpu_custom_call" | custom-call | bytes 90000000 | tf_op jit(solution)/shard_map/filter_y_backward/pallas_call | solution.py:485
  219.1 13.0 %all-to-all-start.1 = ((f32[32,2,128,128]{3,2,1,0:T(8,128)}), f32[32,2,128,128]{3,2,1,0:T(8,128)}, u32[]{:S(2)}, u32[]{:S(2)}) async-start(f32[32,2,128,128]{3,2,1,0:T(8,128)} %filter_y_backward.1), calls=%async_computation.1 | async-start | bytes 8388608 | tf_op jit(solution)/shard_map/all_to_all | solution.py:748
  232.6 0.7 maximum_multiply_fusion.d_ref
  233.3 50.5 %all-to-all-done.1.g_ref = f32[32,2,128,128]{3,2,1,0:T(8,128)} async-done(((f32[32,2,128,128]{3,2,1,0:T(8,128)}), f32[32,2,128,128]{3,2,1,0:T(8,128)}, u32[]{:S(2)}, u32[]{:S(2)}) %all-to-all-start.1) | async-done | bytes 4194336 | tf_op jit(solution)/shard_map/all_to_all | solution.py:748
  283.8 14.8 %filter_x_backward.1.m_ref.next_ref = f32[2,128,4096]{2,1,0:T(8,128)} custom-call(f32[32,2,128,128]{3,2,1,0:T(8,128)} %all-to-all-done.1.g_ref, f32[8,2,16,4096]{3,2,1,0:T(8,128)} %all-to-all-done.2.held_ref, f32[2,16,256]{2,1,0:T(8,128)} %constant.65.clone.tw_ref, f32[2,16,8,256]{3,2,1,0:T(8,128)} %maximum_multiply_fusion.d_ref, ...), custom_call_target="tpu_custom_call" | custom-call | bytes 48000000 | tf_op jit(solution)/shard_map/filter_x_backward/pallas_call | solution.py:312
  298.7 1.1 fusion.4
  299.7 1.9 collective-permute-start
  301.7 6.0 %collective-permute-start.1 = (f32[2,8,4096]{2,1,0:T(8,128)S(1)}, f32[2,8,4096]{2,1,0:T(8,128)S(1)}, u32[]{:S(2)}, u32[]{:S(2)}) collective-permute-start(f32[2,8,4096]{2,1,0:T(8,128)S(1)} %get-tuple-element.13), channel_id=1, source_target_pairs={{32,0},{64,32},{96,64},{128,96},{160,128},{192,160},{224,192},{1,2... | collective-permute-start | bytes 786440 | tf_op jit(solution)/shard_map/ppermute | solution.py:708
  308.3 3.8 collective-permute-done.above_ref
  312.1 1.2 collective-permute-done.1.below_ref
  314.1 9.0 %tv_shrink.1 = f32[8,2,16,4096]{3,2,1,0:T(8,128)} custom-call(s32[2]{0:T(128)} %add_convert_fusion.edge_ref, f32[2,128,4096]{2,1,0:T(8,128)} %filter_x_backward.1.m_ref.next_ref, f32[2,128,4096]{2,1,0:T(8,128)} %filter_x_backward.1.m_ref.next_ref, f32[2,8,4096]{2,1,0:T(8,128)} %copy-done.6, f32[2,8,4096]{2,1,0:T(8,128)} %copy-done.7), custom_call_target="tpu_custom_call" | custom-call | bytes 27000000 | tf_op jit(solution)/shard_map/tv_shrink/pallas_call | solution.py:681
  323.0 56.6 %all_to_all.20 = f32[8,2,16,4096]{3,2,1,0:T(8,128)S(1)} all-to-all(f32[8,2,16,4096]{3,2,1,0:T(8,128)} %tv_shrink.1), channel_id=1, replica_groups=mesh['x_lo'=2,'y'=4,'x_hi'=2,'z'=8,'core'=2] {'x_lo','y'}, dimensions={0} | all-to-all | bytes 8388608 | tf_op jit(solution)/shard_map/all_to_all | solution.py:755
  379.6 2.3 copy.25
  (38 shorter events, 4.6 us)
Async XLA Ops:
  0.0 1.7 copy-start
  16.4 7.8 %copy-start.11 = (u32[256]{0:T(256)S(1)}, u32[256]{0:T(256)}, u32[]{:S(2)}) copy-start(u32[256]{0:T(256)} %constant.77) | copy-start | bytes 3076
  16.4 72.6 %copy-start.9 = (f32[9,256]{1,0:T(8,128)S(1)}, f32[9,256]{1,0:T(8,128)}, u32[]{:S(2)}) copy-start(f32[9,256]{1,0:T(8,128)} %constant.72) | copy-start | bytes 27652
  16.4 73.1 %copy-start.10 = (f32[9]{0:T(128)S(1)}, f32[9]{0:T(128)}, u32[]{:S(2)}) copy-start(f32[9]{0:T(128)} %constant.73) | copy-start | bytes 112
  16.4 74.0 %all-to-all-start = ((f32[32,272,128]{2,1,0:T(8,128)}), f32[32,272,128]{2,1,0:T(8,128)}, u32[]{:S(2)}, u32[]{:S(2)}) async-start(f32[32,272,128]{2,1,0:T(8,128)} %filter_x_forward.1), calls=%async_computation | async-start | bytes 8912896 | tf_op jit(solution)/shard_map/all_to_all | solution.py:741
  90.3 31.1 %copy-start.5 = (f32[2,1,128,4096]{3,2,1,0:T(8,128)S(1)}, f32[2,1,128,4096]{3,2,1,0:T(8,128)}, u32[]{:S(2)}) copy-start(f32[2,1,128,4096]{3,2,1,0:T(8,128)} %param.16) | copy-start | bytes 12582916
  123.9 4.8 %copy-start.3 = (f32[8,2,128,256]{3,2,1,0:T(8,128)S(1)}, f32[8,2,128,256]{3,2,1,0:T(8,128)}, u32[]{:S(2)}) copy-start(f32[8,2,128,256]{3,2,1,0:T(8,128)} %get-tuple-element.10.p_ref) | copy-start | bytes 6291460
  123.9 4.8 %copy-start.4 = (f32[1,2,128,256]{3,2,1,0:T(8,128)S(1)}, f32[1,2,128,256]{3,2,1,0:T(8,128)}, u32[]{:S(2)}) copy-start(f32[1,2,128,256]{3,2,1,0:T(8,128)} %get-tuple-element.11.h_ref) | copy-start | bytes 786436
  123.9 95.2 %all-to-all-start.2 = ((f32[8,2,16,4096]{3,2,1,0:T(8,128)}), f32[8,2,16,4096]{3,2,1,0:T(8,128)}, u32[]{:S(2)}, u32[]{:S(2)}) async-start(f32[8,2,16,4096]{3,2,1,0:T(8,128)} %bitcast.18), calls=%async_computation.2 | async-start | bytes 8388608 | tf_op jit(solution)/shard_map/all_to_all | solution.py:745
  188.9 1.4 copy-start.2
  219.1 13.0 %copy-start.8 = (f32[16,256]{1,0:T(8,128)S(1)}, f32[16,256]{1,0:T(8,128)}, u32[]{:S(2)}) copy-start(f32[16,256]{1,0:T(8,128)} %constant.74) | copy-start | bytes 49156
  219.1 64.8 %all-to-all-start.1 = ((f32[32,2,128,128]{3,2,1,0:T(8,128)}), f32[32,2,128,128]{3,2,1,0:T(8,128)}, u32[]{:S(2)}, u32[]{:S(2)}) async-start(f32[32,2,128,128]{3,2,1,0:T(8,128)} %filter_y_backward.1), calls=%async_computation.1 | async-start | bytes 8388608 | tf_op jit(solution)/shard_map/all_to_all | solution.py:748
  299.7 12.4 %collective-permute-start = (f32[2,8,4096]{2,1,0:T(8,128)S(1)}, f32[2,8,4096]{2,1,0:T(8,128)S(1)}, u32[]{:S(2)}, u32[]{:S(2)}) collective-permute-start(f32[2,8,4096]{2,1,0:T(8,128)S(1)} %get-tuple-element.14), channel_id=1, source_target_pairs={{0,32},{32,64},{64,96},{96,128},{128,160},{160,192},{192,224},{224... | collective-permute-start | bytes 786440 | tf_op jit(solution)/shard_map/ppermute | solution.py:708
  301.7 11.7 %collective-permute-start.1 = (f32[2,8,4096]{2,1,0:T(8,128)S(1)}, f32[2,8,4096]{2,1,0:T(8,128)S(1)}, u32[]{:S(2)}, u32[]{:S(2)}) collective-permute-start(f32[2,8,4096]{2,1,0:T(8,128)S(1)} %get-tuple-element.13), channel_id=1, source_target_pairs={{32,0},{64,32},{96,64},{128,96},{160,128},{192,160},{224,192},{1,2... | collective-permute-start | bytes 786440 | tf_op jit(solution)/shard_map/ppermute | solution.py:708
  312.1 1.2 copy-start.6
  313.3 0.7 copy-start.7
  379.6 2.4 copy-start.1

commit v4 on v3

--- a/solution.py
+++ b/solution.py
@@ -332,11 +332,91 @@
     )(gradient, held, tw, transfer, wf, wi)
 
 
-def forward_y_kernel(z_ref, g_ref, t_ref, tt_ref, cs_ref, o_ref, h_ref, u_ref, s_ref):
+LAYERS = 8
+PART = LANES // LAYERS
+REDUCE_HOPS = LAYERS - 1
+HOPS = 2 * (LAYERS - 1)
+
+
+def filter_y_kernel(
+    rot_ref, g_ref, t_ref, tt_ref, cs_ref, o_ref, u_ref, s_ref, h_ref, r_ref, a_ref, send_sem, recv_sem
+):
     step = pl.program_id(0)
+    me = lax.axis_index("z")
+
+    def hop(k, h):
+        odd = lax.rem(k, 2)
+        sign = 1 - 2 * odd
+
+        def block(distance):
+            index = lax.rem(me + sign * distance + 2 * LAYERS, LAYERS)
+            return pl.ds(pl.multiple_of(index * PART, PART), PART)
+
+        def copy(source, target, h):
+            return pltpu.make_async_remote_copy(
+                src_ref=source,
+                dst_ref=target,
+                send_sem=send_sem.at[k],
+                recv_sem=recv_sem.at[k, h],
+                device_id={"z": lax.rem(me + sign + LAYERS, LAYERS)},
+                device_id_type=pl.DeviceIdType.MESH,
+            )
+
+        own = block(0)
+
+        @pl.when(h > 0)
+        def _():
+            last = copy(s_ref.at[k, own, :], r_ref.at[k, 0], h - 1)
+            last.wait_send()
+            last.wait_recv()
+
+        @pl.when(h < REDUCE_HOPS)
+        def _():
+            rows = block(-1 - h)
+
+            @pl.when(h > 0)
+            def _():
+                s_ref[k, rows, :] += r_ref[k, h - 1]
+
+            copy(s_ref.at[k, rows, :], r_ref.at[k, h], h).start()
+
+        @pl.when(h == REDUCE_HOPS)
+        def _():
+            h_ref[k, own, :] = s_ref[k, own, :] + r_ref[k, REDUCE_HOPS - 1]
+
+        @pl.when((h >= REDUCE_HOPS) & (h < HOPS))
+        def _():
+            rows = block(REDUCE_HOPS - h)
+            copy(h_ref.at[k, rows, :], h_ref.at[k, rows, :], h).start()
+
+    def progress(slot):
+        @pl.loop(0, CLASSES)
+        def _(k):
+            h = slot - (2 * k + 1)
+
+            @pl.when((h >= 0) & (h <= HOPS))
+            def _():
+                hop(k, h)
 
     @pl.when(step == 0)
     def _():
+        barrier = pltpu.get_barrier_semaphore()
+        for distance in (1, LAYERS - 1):
+            pl.semaphore_signal(
+                barrier,
+                inc=1,
+                device_id={"z": lax.rem(me + distance, LAYERS)},
+                device_id_type=pl.DeviceIdType.MESH,
+            )
+        pl.semaphore_wait(barrier, 2)
+
+        def place(p, lanes, core, upper, lower):
+            for parity, value in ((0, upper + lower), (1, upper - lower)):
+                high, low = halves(value)
+                for part, piece in ((0, high), (1, low), (2, high)):
+                    start = part * INNER + core * 128
+                    u_ref[parity, p, lanes, start : start + 128] = piece
+
         @pl.loop(0, PLANES)
         def _(p):
             for core in range(2):
@@ -344,126 +424,72 @@
                     rows = slice(c * 128, (c + 1) * 128)
                     upper = g_ref[p * 4 + core, rows, :].T
                     lower = g_ref[p * 4 + 2 + core, rows, :].T
-                    for parity, value in ((0, upper + lower), (1, upper - lower)):
-                        high, low = halves(value)
-                        for part, piece in ((0, high), (1, low), (2, high)):
-                            start = part * INNER + core * 128
-                            u_ref[parity, p, c * LANES : (c + 1) * LANES, start : start + 128] = (
-                                piece
-                            )
-
-        for upper in range(2):
-            for core in range(2):
+                    place(p, slice(c * LANES, (c + 1) * LANES), core, upper, lower)
+
+        for core in range(2):
+            tiles = []
+            for upper in range(2):
                 rows = [g_ref[p * 4 + upper * 2 + core, 256:, :] for p in range(PLANES)]
-                block = jnp.concatenate(rows, axis=0).T
-                h_ref[0, upper, :, core * 128 : (core + 1) * 128] = block
-
-    parity = lax.rem(step, 2)
-    total = None
-    for p in range(PLANES):
-        result = jnp.dot(u_ref[parity, p], t_ref[0], preferred_element_type=F32)
-        piece = (
-            cs_ref[0, 2 * p : 2 * p + 1, :] * result[:LANES]
-            + cs_ref[0, 2 * p + 1 : 2 * p + 2, :] * result[LANES:]
+                tiles.append(jnp.concatenate(rows, axis=0).T)
+            place(PLANES, slice(0, LANES), core, tiles[0], tiles[1])
+
+    @pl.when(step < CLASSES)
+    def _():
+        parity = lax.rem(step, 2)
+
+        def planes(first, total):
+            for p in range(first, first + PLANES // 2):
+                result = jnp.dot(u_ref[parity, p], t_ref[0], preferred_element_type=F32)
+                total = (
+                    total
+                    + cs_ref[0, 2 * p : 2 * p + 1, :] * result[:LANES]
+                    + cs_ref[0, 2 * p + 1 : 2 * p + 2, :] * result[LANES:]
+                )
+            return total
+
+        minus = jnp.dot(u_ref[parity, PLANES, :LANES, :], t_ref[0], preferred_element_type=F32)
+        s_ref[step] = planes(0, -minus)
+        progress(2 * step)
+        total = planes(PLANES // 2, s_ref[step])
+        cosine, sine = rot_ref[step, 0], rot_ref[step, 1]
+        real, imag = total[:, :INNER], total[:, INNER:]
+        s_ref[step, :, :INNER] = cosine * real - sine * imag
+        s_ref[step, :, INNER:] = cosine * imag + sine * real
+        progress(2 * step + 1)
+
+    @pl.when(step >= CLASSES)
+    def _():
+        k = step - CLASSES
+        parity = lax.rem(k, 2)
+        cosine, sine = rot_ref[k, 2], rot_ref[k, 3]
+        real, imag = h_ref[k, :, :INNER], h_ref[k, :, INNER:]
+        spectrum = jnp.concatenate(
+            [cosine * real + sine * imag, cosine * imag - sine * real], axis=1
         )
-        total = piece if total is None else total + piece
-    turned = jnp.concatenate([-total[:, INNER:], total[:, :INNER]], axis=1)
-    high, low = halves(jnp.concatenate([total, turned], axis=0))
-    s_ref[step] = jnp.dot(
-        jnp.concatenate([high, low, high], axis=1), tt_ref[0], preferred_element_type=F32
-    )
-
-    @pl.when(step == CLASSES - 1)
-    def _():
-        shift = z_ref[0]
-
-        @pl.loop(0, LANES // 8)
-        def _(i):
-            rows = pl.ds(pl.multiple_of(i * 8, 8), 8)
-            other = pl.ds(pl.multiple_of(LANES + i * 8, 8), 8)
-            for half in range(2):
-                lanes = slice(half * LANES, (half + 1) * LANES)
-                values = [(s_ref[k, rows, lanes], s_ref[k, other, lanes]) for k in range(CLASSES)]
-                for b, value in enumerate(real_inverse16(values)):
-                    block = lax.rem(shift + b, 16)
-                    o_ref[lax.rem(block, 8), lax.div(block, 8), rows, lanes] = value
-
-
-def forward_y(z_index, received, factors):
-    forward, backward = class_tables()
-    return pl.pallas_call(
-        forward_y_kernel,
-        grid=(CLASSES,),
-        in_specs=[
-            pl.BlockSpec(memory_space=pltpu.SMEM),
-            whole((32, 272, LANES)),
-            pl.BlockSpec((1, 768, 512), lambda k: (k, 0, 0)),
-            pl.BlockSpec((1, 1536, 256), lambda k: (k, 0, 0)),
-            pl.BlockSpec((1, 16, 512), lambda k: (k, 0, 0)),
-        ],
-        out_specs=[whole((8, 2, LANES, INNER)), whole((1, 2, LANES, INNER))],
-        out_shape=[
-            jax.ShapeDtypeStruct((8, 2, LANES, INNER), F32),
-            jax.ShapeDtypeStruct((1, 2, LANES, INNER), F32),
-        ],
-        scratch_shapes=[
-            pltpu.VMEM((2, PLANES, 2 * LANES, 768), BF16),
-            pltpu.VMEM((CLASSES, 2 * LANES, INNER), F32),
-        ],
-        compiler_params=params(),
-        cost_estimate=cost_of(32),
-        name="filter_y_forward",
-    )(z_index, received, jnp.asarray(forward), jnp.asarray(backward), factors)
-
-
-def backward_y_kernel(z_ref, m_ref, t_ref, tt_ref, cs_ref, o_ref, x_ref, a_ref):
-    step = pl.program_id(0)
-
-    @pl.when(step == 0)
-    def _():
-        shift = z_ref[0]
-
-        @pl.loop(0, LANES // 8)
-        def _(i):
-            rows = pl.ds(pl.multiple_of(i * 8, 8), 8)
-            other = pl.ds(pl.multiple_of(LANES + i * 8, 8), 8)
-            for half in range(2):
-                lanes = slice(half * LANES, (half + 1) * LANES)
-                blocks = []
-                for b in range(16):
-                    block = lax.rem(shift + b, 16)
-                    blocks.append(m_ref[lax.rem(block, 8), lax.div(block, 8), rows, lanes])
-                for k, (real, imag) in enumerate(real_dft16(blocks)):
-                    x_ref[k, rows, lanes] = real
-                    x_ref[k, other, lanes] = imag
-
-        @pl.loop(0, PLANES)
-        def _(p):
-            for parity in range(2):
-                a_ref[parity, p] = jnp.zeros((2 * LANES, INNER), F32)
-
-    parity = lax.rem(step, 2)
-    high, low = halves(x_ref[step])
-    mixed = jnp.dot(
-        jnp.concatenate([high, low, high], axis=1), t_ref[0], preferred_element_type=F32
-    )
-    cosine = mixed[:LANES, :INNER] + mixed[LANES:, INNER:]
-    sine = mixed[:LANES, INNER:] - mixed[LANES:, :INNER]
-    spectrum = jnp.concatenate([cosine, sine], axis=1)
-    for p in range(PLANES):
-        product = jnp.concatenate(
-            [
-                cs_ref[0, 2 * p : 2 * p + 1, :] * spectrum,
-                cs_ref[0, 2 * p + 1 : 2 * p + 2, :] * spectrum,
-            ],
-            axis=0,
-        )
-        high, low = halves(product)
-        a_ref[parity, p] += jnp.dot(
-            jnp.concatenate([high, low, high], axis=1), tt_ref[0], preferred_element_type=F32
-        )
-
-    @pl.when(step == CLASSES - 1)
+
+        def planes(first):
+            for p in range(first, first + PLANES // 2):
+                product = jnp.concatenate(
+                    [
+                        cs_ref[0, 2 * p : 2 * p + 1, :] * spectrum,
+                        cs_ref[0, 2 * p + 1 : 2 * p + 2, :] * spectrum,
+                    ],
+                    axis=0,
+                )
+                high, low = halves(product)
+                value = jnp.dot(
+                    jnp.concatenate([high, low, high], axis=1),
+                    tt_ref[0],
+                    preferred_element_type=F32,
+                )
+                a_ref[parity, p] = jnp.where(k < 2, value, a_ref[parity, p] + value)
+
+        planes(0)
+        progress(2 * step)
+        planes(PLANES // 2)
+        progress(2 * step + 1)
+
+    @pl.when(step == 2 * CLASSES - 1)
     def _():
         @pl.loop(0, PLANES)
         def _(p):
@@ -480,132 +506,36 @@
                         o_ref[owner * 4 + 2 + core, c, held, :] = lower[part]
 
 
-def backward_y(z_index, misfit, factors):
+def filter_y(rotations, received, factors):
     forward, backward = class_tables()
+    last = CLASSES - 1
     return pl.pallas_call(
-        backward_y_kernel,
-        grid=(CLASSES,),
+        filter_y_kernel,
+        grid=(2 * CLASSES,),
         in_specs=[
             pl.BlockSpec(memory_space=pltpu.SMEM),
-            whole((8, 2, LANES, INNER)),
-            pl.BlockSpec((1, 768, 512), lambda k: (k, 0, 0)),
-            pl.BlockSpec((1, 1536, 256), lambda k: (k, 0, 0)),
-            pl.BlockSpec((1, 16, 512), lambda k: (k, 0, 0)),
+            whole((32, 272, LANES)),
+            pl.BlockSpec((1, 768, 512), lambda i: (jnp.minimum(i, last), 0, 0)),
+            pl.BlockSpec((1, 1536, 256), lambda i: (jnp.maximum(i - CLASSES, 0), 0, 0)),
+            pl.BlockSpec((1, 16, 512), lambda i: (lax.rem(i, CLASSES), 0, 0)),
         ],
         out_specs=whole((32, 2, 128, LANES)),
         out_shape=jax.ShapeDtypeStruct((32, 2, 128, LANES), F32),
         scratch_shapes=[
-            pltpu.VMEM((CLASSES, 2 * LANES, INNER), F32),
+            pltpu.VMEM((2, PLANES + 1, 2 * LANES, 768), BF16),
+            pltpu.VMEM((CLASSES, LANES, 2 * INNER), F32),
+            pltpu.VMEM((CLASSES, LANES, 2 * INNER), F32),
+            pltpu.VMEM((CLASSES, REDUCE_HOPS, PART, 2 * INNER), F32),
             pltpu.VMEM((2, PLANES, 2 * LANES, INNER), F32),
-        ],
-        compiler_params=params(),
-        cost_estimate=cost_of(30),
-        name="filter_y_backward",
-    )(z_index, misfit, jnp.asarray(forward), jnp.asarray(backward), factors)
-
-
-SUBS = 2
-LAYERS = 8
-
-
-def z_exchange_kernel(p_ref, h_ref, o_ref, r_ref, sum_send, sum_recv, all_send, all_recv):
-    me = lax.axis_index("z")
-    at = lambda distance: lax.rem(me + distance + 2 * LAYERS, LAYERS)
-    right, left = at(1), at(-1)
-    barrier = pltpu.get_barrier_semaphore()
-    for neighbour in (left, right):
-        pl.semaphore_signal(
-            barrier,
-            inc=1,
-            device_id={"z": neighbour},
-            device_id_type=pl.DeviceIdType.MESH,
-        )
-    pl.semaphore_wait(barrier, 2)
-
-    size = LANES // SUBS
-    rings = [(way, sub) for sub in range(SUBS) for way in range(2)]
-
-    def send(source, target, send_sem, recv_sem, way):
-        return pltpu.make_async_remote_copy(
-            src_ref=source,
-            dst_ref=target,
-            send_sem=send_sem,
-            recv_sem=recv_sem,
-            device_id={"z": (right, left)[way]},
-            device_id_type=pl.DeviceIdType.MESH,
-        )
-
-    started, arrived = [], {}
-    for step in range(LAYERS):
-        for way, sub in rings:
-            rows = slice(sub * size, (sub + 1) * size)
-            block = at((-1 - step) if way == 0 else (1 + step))
-            slot = r_ref.at[way, sub]
-            if step:
-                arrived[way, sub].wait_recv()
-                if step < LAYERS - 1:
-                    r_ref[way, sub, step - 1] += p_ref[block, way, rows, :]
-                else:
-                    o_ref[me, way, rows, :] = (
-                        r_ref[way, sub, step - 1] + p_ref[me, way, rows, :]
-                    ) - h_ref[0, way, rows, :]
-            if step < LAYERS - 1:
-                source = p_ref.at[block, way, rows, :] if step == 0 else slot.at[step - 1]
-                copy = send(
-                    source,
-                    slot.at[step],
-                    sum_send.at[way, sub, step],
-                    sum_recv.at[way, sub, step],
-                    way,
-                )
-                copy.start()
-                started.append(copy)
-                arrived[way, sub] = copy
-            else:
-                place = o_ref.at[me, way, rows, :]
-                copy = send(
-                    place, place, all_send.at[way, sub, 0], all_recv.at[way, sub, 0], way
-                )
-                copy.start()
-                started.append(copy)
-                arrived[way, sub] = copy
-    for step in range(1, LAYERS):
-        for way, sub in rings:
-            rows = slice(sub * size, (sub + 1) * size)
-            arrived[way, sub].wait_recv()
-            if step < LAYERS - 1:
-                place = o_ref.at[at(-step if way == 0 else step), way, rows, :]
-                copy = send(
-                    place, place, all_send.at[way, sub, step], all_recv.at[way, sub, step], way
-                )
-                copy.start()
-                started.append(copy)
-                arrived[way, sub] = copy
-    for copy in started:
-        copy.wait_send()
-
-
-def z_exchange(partial, tile):
-    steps = LAYERS - 1
-    vmem = pl.BlockSpec(memory_space=pltpu.VMEM)
-    return pl.pallas_call(
-        z_exchange_kernel,
-        in_specs=[vmem, vmem],
-        out_specs=vmem,
-        out_shape=jax.ShapeDtypeStruct((LAYERS, 2, LANES, INNER), F32),
-        scratch_shapes=[
-            pltpu.VMEM((2, SUBS, steps, LANES // SUBS, INNER), F32),
-            pltpu.SemaphoreType.DMA((2, SUBS, steps)),
-            pltpu.SemaphoreType.DMA((2, SUBS, steps)),
-            pltpu.SemaphoreType.DMA((2, SUBS, steps)),
-            pltpu.SemaphoreType.DMA((2, SUBS, steps)),
+            pltpu.SemaphoreType.DMA((CLASSES,)),
+            pltpu.SemaphoreType.DMA((CLASSES, HOPS)),
         ],
         compiler_params=pltpu.CompilerParams(
-            collective_id=0, has_side_effects=True, vmem_limit_bytes=32 << 20
+            collective_id=0, has_side_effects=True, vmem_limit_bytes=56 << 20
         ),
-        cost_estimate=cost_of(50),
-        name="z_exchange",
-    )(partial, tile)
+        cost_estimate=cost_of(90),
+        name="filter_y",
+    )(rotations, received, jnp.asarray(forward), jnp.asarray(backward), factors)
 
 
 TV_ROWS = 8
@@ -717,7 +647,6 @@
     x_hi, z, core = lax.axis_index("x_hi"), lax.axis_index("z"), lax.axis_index("core")
     depth_index = x_lo * 4 + y
     row_index = x_hi * 16 + z * 2 + core
-    z_index = z[None].astype(jnp.int32)
     field = field[:, 0]
 
     x_freq = RADIX * np.arange(INNER)[None, :] + np.arange(RADIX)[:, None]
@@ -730,21 +659,24 @@
     x_backward = jnp.stack([jnp.cos(x_phase), jnp.sin(x_phase)]) * (-1.0 / (PLANES * N))
     y_squares = jnp.asarray(squares_of(class_frequencies()))[:, None, None, :]
     y_phase = phase_of(depths[None, :, None, None], y_squares)
-    weights = np.full((CLASSES, 1, 1, 1), 2.0 / N, np.float32)
-    weights[0] = weights[8] = 1.0 / N
-    factors = jnp.concatenate([jnp.cos(y_phase), jnp.sin(y_phase)], axis=2) * weights
+    factors = jnp.concatenate([jnp.cos(y_phase), jnp.sin(y_phase)], axis=2)
     factors = factors.reshape(CLASSES, 2 * PLANES, INNER)
     factors = jnp.concatenate([factors, factors], axis=2)
+
+    weights = np.full((CLASSES,), 2.0 / N, np.float32)
+    weights[0] = weights[8] = 1.0 / N
+    turns = lax.rem(z * np.arange(CLASSES, dtype=np.int32), RADIX).astype(F32)
+    turns = turns * (2.0 * math.pi / RADIX)
+    cosine, sine = jnp.cos(turns), jnp.sin(turns)
+    rotations = jnp.stack([weights * cosine, weights * sine, cosine, sine], axis=1)
 
     hologram_rows = lax.dynamic_slice_in_dim(hologram, depth_index * 16, 16, 0)
     sent = forward_x(field, hologram_rows, x_forward)
     received = lax.all_to_all(sent, LAYER, 0, 0, tiled=True)
-    partial, tile = forward_y(z_index, received, factors)
-    field, partial = lax.optimization_barrier((field, partial))
+    field, received = lax.optimization_barrier((field, received))
     held = jnp.transpose(field.reshape(2, PLANES, 16, N), (1, 0, 2, 3))
     held = lax.all_to_all(held, DEPTH, 0, 0, tiled=True)
-    misfit = z_exchange(partial, tile)
-    sent = backward_y(z_index, misfit, factors)
+    sent = filter_y(rotations, received, factors)
     received = lax.all_to_all(sent, LAYER, 0, 0, tiled=True)
     moved = backward_x(received, held, x_backward)
     above = along_rows(moved[:, 120:], 1)

time: 383 us -> 425 us (1.11)
  blocking collectives: 120 us -> 176 us
  starting transfers between devices: 33.5 us -> 19.8 us
    all_to_all x0 -> x1, blocking collectives: none -> 60.7 us  [per_device(): received = lax.all_to_all(sent, LAYER, 0, 0, tiled=True)]
    all_to_all x2 -> x1, starting transfers between devices: 20.8 us -> 5.81 us  [per_device(): received = lax.all_to_all(sent, LAYER, 0, 0, tiled=True)]
    unnamed x1, blocking collectives: 63.4 us -> 57.7 us
    pallas_call x3 -> x1, Pallas kernels: 120 us -> 121 us  [filter_y(): pl.pallas_call(filter_y_kernel, grid=(2 * CLASSES,), in_specs=[pl.BlockSp...]
    all_to_all x2 -> x1, waiting for transfers between devices: 50.5 us -> 50.5 us  [per_device(): received = lax.all_to_all(sent, LAYER, 0, 0, tiled=True)]
  transfers between devices with their start and end apart: 5 -> 4, of which waited for: 3 -> 3; matrix products, arithmetic and copies ran while one was open for 1% -> 1% of each run, Pallas kernels for 23% -> 29%
where the time goes in v4:
time: 425 us; the launch traced here: 424 us
  blocking collectives  176 us (41%)
  Pallas kernels  158 us (37%)
  waiting for transfers between devices  55.6 us (13%)
  starting transfers between devices  19.8 us (5%)
  local copies, waits for them, and re-layouts  9.38 us (2%)
  other arithmetic  4.5 us (1%)
    pallas_call x1, Pallas kernels, filter_y(): pl.pallas_call(filter_y_kernel, grid=(2 * CLASSES,), in_specs=[pl.BlockSp...  121 us
    all_to_all x1, blocking collectives, per_device(): received = lax.all_to_all(sent, LAYER, 0, 0, tiled=True)  60.7 us
    unnamed x1, blocking collectives  57.7 us
    all_to_all x1, blocking collectives, per_device(): estimate = lax.all_to_all(estimate, DEPTH, 0, 0, tiled=True)  57.2 us
    all_to_all x1, waiting for transfers between devices, per_device(): received = lax.all_to_all(sent, LAYER, 0, 0, tiled=True)  50.5 us
    pallas_call x1, Pallas kernels, backward_x(): pl.pallas_call(backward_x_kernel, grid=(128 // STEP_ROWS,), in_specs=[pl....  14.8 us
    pallas_call x1, Pallas kernels, forward_x(): pl.pallas_call(forward_x_kernel, grid=(128 // STEP_ROWS,), in_specs=[pl.B...  13.4 us
    pallas_call x1, Pallas kernels, shrink(): pl.pallas_call(shrink_kernel, grid=(steps,), in_specs=[pl.BlockSpec(memor...  8.96 us
  transfers between devices with their start and end apart: 4, of which 3 were waited for; matrix products, arithmetic and copies ran while one was open for 1% of the time, Pallas kernels for 29%

profile of v4, /device:TPU:2, one launch (start us, length us, event | category | flops | bytes accessed | tf_op | source)
XLA Modules:
  0.0 424.2 jit_solution(13002993297370440257)
XLA Ops:
  0.8 0.8 fusion.1
  1.7 0.7 constant_dynamic-slice_fusion.hol_ref
  3.0 13.4 %filter_x_forward.1 = f32[32,272,128]{2,1,0:T(8,128)} custom-call(f32[2,128,4096]{2,1,0:T(8,128)} %bitcast.23, f32[16,4096]{1,0:T(8,128)} %constant_dynamic-slice_fusion.hol_ref, f32[2,16,256]{2,1,0:T(8,128)} %constant.73.clone.tw_ref, f32[2,16,1,256]{3,2,1,0:T(1,128)} %pad_maximum_fusion.2.d_ref, bf16[1536,512]{1,0:T(8,128)(2,1)} %constant.74.clone.wf_ref, ...), custom_call_target="tpu_custom_call" | custom-call | bytes 42000000 | tf_op jit(solution)/shard_map/filter_x_forward/pallas_call | solution.py:290
  16.4 60.7 %all_to_all.20.g_ref = f32[32,272,128]{2,1,0:T(8,128)} all-to-all(f32[32,272,128]{2,1,0:T(8,128)} %filter_x_forward.1), channel_id=1, replica_groups=mesh['x_lo'=2,'y'=4,'x_hi'=2,'z'=8,'core'=2] {'x_lo','y','x_hi','core'}, dimensions={0} | all-to-all | bytes 8912896 | tf_op jit(solution)/shard_map/all_to_all | solution.py:675
  77.1 2.3 copy.41
  79.4 6.0 %all-to-all-start.2 = ((f32[8,2,16,4096]{3,2,1,0:T(8,128)}), f32[8,2,16,4096]{3,2,1,0:T(8,128)}, u32[]{:S(2)}, u32[]{:S(2)}) async-start(f32[8,2,16,4096]{3,2,1,0:T(8,128)} %bitcast.25), calls=%async_computation.2 | async-start | bytes 8388608 | tf_op jit(solution)/shard_map/all_to_all | solution.py:678
  86.1 0.7 dynamic-update-slice
  86.7 57.7 %all-reduce = f32[8]{0:T(128)S(1)} all-reduce(f32[8]{0:T(128)S(1)} %dynamic-update-slice), channel_id=1, replica_groups=mesh['x_lo'=2,'y'=4,'x_hi'=2,'z'=8,'core'=2] {'x_lo','y'}, use_global_device_ids=true, to_apply=%add | all-reduce | flops 8 | bytes 64
  144.6 0.7 copy.36.rot_ref
  145.8 0.8 pad_maximum_fusion.cs_ref
  146.6 121.2 %filter_y.1 = f32[32,2,128,128]{3,2,1,0:T(8,128)} custom-call(f32[9,4]{1,0:T(8,128)} %copy.36.rot_ref, f32[32,272,128]{2,1,0:T(8,128)} %all_to_all.20.g_ref, bf16[9,768,512]{2,1,0:T(8,128)(2,1)} %constant.76.clone.t_ref, bf16[9,1536,256]{2,1,0:T(8,128)(2,1)} %constant.77.clone.tt_ref, f32[9,16,512]{2,1,0:T(8,128)} %pad_maximum_fusion.cs_ref), custom_call_target="tpu_custom_call" | custom-call | bytes 270000000 | tf_op jit(solution)/shard_map/filter_y/pallas_call | solution.py:512
  267.8 5.8 %all-to-all-start.1 = ((f32[32,2,128,128]{3,2,1,0:T(8,128)}), f32[32,2,128,128]{3,2,1,0:T(8,128)}, u32[]{:S(2)}, u32[]{:S(2)}) async-start(f32[32,2,128,128]{3,2,1,0:T(8,128)} %filter_y.1), calls=%async_computation.1 | async-start | bytes 8388608 | tf_op jit(solution)/shard_map/all_to_all | solution.py:680
  274.2 0.7 maximum_multiply_fusion.d_ref
  274.9 50.5 %all-to-all-done.1.g_ref = f32[32,2,128,128]{3,2,1,0:T(8,128)} async-done(((f32[32,2,128,128]{3,2,1,0:T(8,128)}), f32[32,2,128,128]{3,2,1,0:T(8,128)}, u32[]{:S(2)}, u32[]{:S(2)}) %all-to-all-start.1) | async-done | bytes 4194336 | tf_op jit(solution)/shard_map/all_to_all | solution.py:680
  325.4 14.8 %filter_x_backward.1.m_ref.next_ref = f32[2,128,4096]{2,1,0:T(8,128)} custom-call(f32[32,2,128,128]{3,2,1,0:T(8,128)} %all-to-all-done.1.g_ref, f32[8,2,16,4096]{3,2,1,0:T(8,128)} %all-to-all-done.2.held_ref, f32[2,16,256]{2,1,0:T(8,128)} %constant.73.clone.tw_ref, f32[2,16,8,256]{3,2,1,0:T(8,128)} %maximum_multiply_fusion.d_ref, ...), custom_call_target="tpu_custom_call" | custom-call | bytes 48000000 | tf_op jit(solution)/shard_map/filter_x_backward/pallas_call | solution.py:312
  340.2 1.1 fusion.11
  341.2 1.9 collective-permute-start
  343.2 6.1 %collective-permute-start.1 = (f32[2,8,4096]{2,1,0:T(8,128)S(1)}, f32[2,8,4096]{2,1,0:T(8,128)S(1)}, u32[]{:S(2)}, u32[]{:S(2)}) collective-permute-start(f32[2,8,4096]{2,1,0:T(8,128)S(1)} %get-tuple-element.9), channel_id=1, source_target_pairs={{32,0},{64,32},{96,64},{128,96},{160,128},{192,160},{224,192},{1,2... | collective-permute-start | bytes 786440 | tf_op jit(solution)/shard_map/ppermute | solution.py:638
  349.9 3.9 collective-permute-done.above_ref
  353.8 1.2 collective-permute-done.1.below_ref
  355.0 0.7 copy-done.4
  355.7 9.0 %tv_shrink.1 = f32[8,2,16,4096]{3,2,1,0:T(8,128)} custom-call(s32[2]{0:T(128)} %add_convert_fusion.edge_ref, f32[2,128,4096]{2,1,0:T(8,128)} %filter_x_backward.1.m_ref.next_ref, f32[2,128,4096]{2,1,0:T(8,128)} %filter_x_backward.1.m_ref.next_ref, f32[2,8,4096]{2,1,0:T(8,128)} %copy-done.3, f32[2,8,4096]{2,1,0:T(8,128)} %copy-done.4), custom_call_target="tpu_custom_call" | custom-call | bytes 27000000 | tf_op jit(solution)/shard_map/tv_shrink/pallas_call | solution.py:611
  364.6 57.2 %all_to_all.21 = f32[8,2,16,4096]{3,2,1,0:T(8,128)S(1)} all-to-all(f32[8,2,16,4096]{3,2,1,0:T(8,128)} %tv_shrink.1), channel_id=1, replica_groups=mesh['x_lo'=2,'y'=4,'x_hi'=2,'z'=8,'core'=2] {'x_lo','y'}, dimensions={0} | all-to-all | bytes 8388608 | tf_op jit(solution)/shard_map/all_to_all | solution.py:687
  421.8 2.3 copy.38
  (32 shorter events, 3.1 us)
Async XLA Ops:
  0.0 1.7 copy-start
  16.4 60.7 %copy-start.2 = (f32[2,1,128,4096]{3,2,1,0:T(8,128)S(1)}, f32[2,1,128,4096]{3,2,1,0:T(8,128)}, u32[]{:S(2)}) copy-start(f32[2,1,128,4096]{3,2,1,0:T(8,128)} %param.15) | copy-start | bytes 12582916
  79.4 6.0 %copy-start.8 = (u32[256]{0:T(256)S(1)}, u32[256]{0:T(256)}, u32[]{:S(2)}) copy-start(u32[256]{0:T(256)} %constant.84) | copy-start | bytes 3076
  79.4 65.1 %copy-start.7 = (f32[9]{0:T(128)S(1)}, f32[9]{0:T(128)}, u32[]{:S(2)}) copy-start(f32[9]{0:T(128)} %constant.72.clone) | copy-start | bytes 112
  79.4 65.9 %copy-start.6 = (f32[9,256]{1,0:T(8,128)S(1)}, f32[9,256]{1,0:T(8,128)}, u32[]{:S(2)}) copy-start(f32[9,256]{1,0:T(8,128)} %constant.80) | copy-start | bytes 27652
  79.4 188.4 %all-to-all-start.2 = ((f32[8,2,16,4096]{3,2,1,0:T(8,128)}), f32[8,2,16,4096]{3,2,1,0:T(8,128)}, u32[]{:S(2)}, u32[]{:S(2)}) async-start(f32[8,2,16,4096]{3,2,1,0:T(8,128)} %bitcast.25), calls=%async_computation.2 | async-start | bytes 8388608 | tf_op jit(solution)/shard_map/all_to_all | solution.py:678
  267.8 5.8 %copy-start.5 = (f32[16,256]{1,0:T(8,128)S(1)}, f32[16,256]{1,0:T(8,128)}, u32[]{:S(2)}) copy-start(f32[16,256]{1,0:T(8,128)} %constant.81) | copy-start | bytes 49156
  267.8 57.6 %all-to-all-start.1 = ((f32[32,2,128,128]{3,2,1,0:T(8,128)}), f32[32,2,128,128]{3,2,1,0:T(8,128)}, u32[]{:S(2)}, u32[]{:S(2)}) async-start(f32[32,2,128,128]{3,2,1,0:T(8,128)} %filter_y.1), calls=%async_computation.1 | async-start | bytes 8388608 | tf_op jit(solution)/shard_map/all_to_all | solution.py:680
  341.2 12.5 %collective-permute-start = (f32[2,8,4096]{2,1,0:T(8,128)S(1)}, f32[2,8,4096]{2,1,0:T(8,128)S(1)}, u32[]{:S(2)}, u32[]{:S(2)}) collective-permute-start(f32[2,8,4096]{2,1,0:T(8,128)S(1)} %get-tuple-element.10), channel_id=1, source_target_pairs={{0,32},{32,64},{64,96},{96,128},{128,160},{160,192},{192,224},{224... | collective-permute-start | bytes 786440 | tf_op jit(solution)/shard_map/ppermute | solution.py:638
  343.2 11.8 %collective-permute-start.1 = (f32[2,8,4096]{2,1,0:T(8,128)S(1)}, f32[2,8,4096]{2,1,0:T(8,128)S(1)}, u32[]{:S(2)}, u32[]{:S(2)}) collective-permute-start(f32[2,8,4096]{2,1,0:T(8,128)S(1)} %get-tuple-element.9), channel_id=1, source_target_pairs={{32,0},{64,32},{96,64},{128,96},{160,128},{192,160},{224,192},{1,2... | collective-permute-start | bytes 786440 | tf_op jit(solution)/shard_map/ppermute | solution.py:638
  353.8 1.2 copy-start.3
  355.0 0.7 copy-start.4
  421.8 2.4 copy-start.1

commit v5 on v4

--- a/solution.py
+++ b/solution.py
@@ -334,8 +334,9 @@
 
 LAYERS = 8
 PART = LANES // LAYERS
-REDUCE_HOPS = LAYERS - 1
-HOPS = 2 * (LAYERS - 1)
+LONG = LAYERS // 2
+SHORT = LAYERS - 1 - LONG
+HOPS = 2 * LONG
 
 
 def filter_y_kernel(
@@ -345,54 +346,68 @@
     me = lax.axis_index("z")
 
     def hop(k, h):
-        odd = lax.rem(k, 2)
-        sign = 1 - 2 * odd
+        sign = 1 - 2 * lax.rem(k, 2)
 
         def block(distance):
-            index = lax.rem(me + sign * distance + 2 * LAYERS, LAYERS)
+            index = lax.rem(me + sign * distance + LAYERS, LAYERS)
             return pl.ds(pl.multiple_of(index * PART, PART), PART)
 
-        def copy(source, target, h):
+        def copy(source, target, way, h):
+            onward = sign if way == 0 else -sign
             return pltpu.make_async_remote_copy(
                 src_ref=source,
                 dst_ref=target,
-                send_sem=send_sem.at[k],
-                recv_sem=recv_sem.at[k, h],
-                device_id={"z": lax.rem(me + sign + LAYERS, LAYERS)},
+                send_sem=send_sem.at[k, way],
+                recv_sem=recv_sem.at[k, way, h],
+                device_id={"z": lax.rem(me + onward + LAYERS, LAYERS)},
                 device_id_type=pl.DeviceIdType.MESH,
             )
 
         own = block(0)
 
+        def finish(way):
+            last = copy(s_ref.at[k, own, :], r_ref.at[k, 0], way, h - 1)
+            last.wait_send()
+            last.wait_recv()
+
         @pl.when(h > 0)
         def _():
-            last = copy(s_ref.at[k, own, :], r_ref.at[k, 0], h - 1)
-            last.wait_send()
-            last.wait_recv()
-
-        @pl.when(h < REDUCE_HOPS)
+            finish(0)
+
+        @pl.when((h > 0) & (h != LONG) & (h != 2 * LONG))
         def _():
-            rows = block(-1 - h)
-
-            @pl.when(h > 0)
+            finish(1)
+
+        def reduce(way, length, first_slot, rows):
+            @pl.when(h < length)
             def _():
-                s_ref[k, rows, :] += r_ref[k, h - 1]
-
-            copy(s_ref.at[k, rows, :], r_ref.at[k, h], h).start()
-
-        @pl.when(h == REDUCE_HOPS)
+                @pl.when(h > 0)
+                def _():
+                    s_ref[k, rows, :] += r_ref[k, first_slot + h - 1]
+
+                copy(s_ref.at[k, rows, :], r_ref.at[k, first_slot + h], way, h).start()
+
+        reduce(0, LONG, 0, block(LONG - h))
+        reduce(1, SHORT, LONG, block(h - SHORT))
+
+        @pl.when(h == LONG)
         def _():
-            h_ref[k, own, :] = s_ref[k, own, :] + r_ref[k, REDUCE_HOPS - 1]
-
-        @pl.when((h >= REDUCE_HOPS) & (h < HOPS))
-        def _():
-            rows = block(REDUCE_HOPS - h)
-            copy(h_ref.at[k, rows, :], h_ref.at[k, rows, :], h).start()
+            h_ref[k, own, :] = (
+                s_ref[k, own, :] + r_ref[k, LONG - 1] + r_ref[k, LONG + SHORT - 1]
+            )
+
+        def gather(way, length, rows):
+            @pl.when((h >= LONG) & (h < LONG + length))
+            def _():
+                copy(h_ref.at[k, rows, :], h_ref.at[k, rows, :], way, h).start()
+
+        gather(0, LONG, block(LONG - h))
+        gather(1, SHORT, block(h - LONG))
 
     def progress(slot):
         @pl.loop(0, CLASSES)
         def _(k):
-            h = slot - (2 * k + 1)
+            h = slot - k
 
             @pl.when((h >= 0) & (h <= HOPS))
             def _():
@@ -448,14 +463,11 @@
             return total
 
         minus = jnp.dot(u_ref[parity, PLANES, :LANES, :], t_ref[0], preferred_element_type=F32)
-        s_ref[step] = planes(0, -minus)
-        progress(2 * step)
-        total = planes(PLANES // 2, s_ref[step])
+        total = planes(PLANES // 2, planes(0, -minus))
         cosine, sine = rot_ref[step, 0], rot_ref[step, 1]
         real, imag = total[:, :INNER], total[:, INNER:]
         s_ref[step, :, :INNER] = cosine * real - sine * imag
         s_ref[step, :, INNER:] = cosine * imag + sine * real
-        progress(2 * step + 1)
 
     @pl.when(step >= CLASSES)
     def _():
@@ -485,9 +497,9 @@
                 a_ref[parity, p] = jnp.where(k < 2, value, a_ref[parity, p] + value)
 
         planes(0)
-        progress(2 * step)
         planes(PLANES // 2)
-        progress(2 * step + 1)
+
+    progress(step)
 
     @pl.when(step == 2 * CLASSES - 1)
     def _():
@@ -525,10 +537,10 @@
             pltpu.VMEM((2, PLANES + 1, 2 * LANES, 768), BF16),
             pltpu.VMEM((CLASSES, LANES, 2 * INNER), F32),
             pltpu.VMEM((CLASSES, LANES, 2 * INNER), F32),
-            pltpu.VMEM((CLASSES, REDUCE_HOPS, PART, 2 * INNER), F32),
+            pltpu.VMEM((CLASSES, LONG + SHORT, PART, 2 * INNER), F32),
             pltpu.VMEM((2, PLANES, 2 * LANES, INNER), F32),
-            pltpu.SemaphoreType.DMA((CLASSES,)),
-            pltpu.SemaphoreType.DMA((CLASSES, HOPS)),
+            pltpu.SemaphoreType.DMA((CLASSES, 2)),
+            pltpu.SemaphoreType.DMA((CLASSES, 2, HOPS)),
         ],
         compiler_params=pltpu.CompilerParams(
             collective_id=0, has_side_effects=True, vmem_limit_bytes=56 << 20
@@ -654,6 +666,16 @@
     x_phase = phase_of(defocus[0], x_squares)
     x_forward = jnp.stack([jnp.cos(x_phase) / N, -jnp.sin(x_phase) / N])
 
+    weights = np.full((CLASSES,), 2.0 / N, np.float32)
+    weights[0] = weights[8] = 1.0 / N
+    turns = lax.rem(z * np.arange(CLASSES, dtype=np.int32), RADIX).astype(F32)
+    turns = turns * (2.0 * math.pi / RADIX)
+    cosine, sine = jnp.cos(turns), jnp.sin(turns)
+    rotations = jnp.stack([weights * cosine, weights * sine, cosine, sine], axis=1)
+
+    hologram_rows = lax.dynamic_slice_in_dim(hologram, depth_index * 16, 16, 0)
+    sent = forward_x(field, hologram_rows, x_forward)
+    defocus, sent = lax.optimization_barrier((defocus, sent))
     depths = lax.all_gather(defocus, DEPTH, tiled=True)
     x_phase = phase_of(depths[None, :, None], x_squares)
     x_backward = jnp.stack([jnp.cos(x_phase), jnp.sin(x_phase)]) * (-1.0 / (PLANES * N))
@@ -662,18 +684,8 @@
     factors = jnp.concatenate([jnp.cos(y_phase), jnp.sin(y_phase)], axis=2)
     factors = factors.reshape(CLASSES, 2 * PLANES, INNER)
     factors = jnp.concatenate([factors, factors], axis=2)
-
-    weights = np.full((CLASSES,), 2.0 / N, np.float32)
-    weights[0] = weights[8] = 1.0 / N
-    turns = lax.rem(z * np.arange(CLASSES, dtype=np.int32), RADIX).astype(F32)
-    turns = turns * (2.0 * math.pi / RADIX)
-    cosine, sine = jnp.cos(turns), jnp.sin(turns)
-    rotations = jnp.stack([weights * cosine, weights * sine, cosine, sine], axis=1)
-
-    hologram_rows = lax.dynamic_slice_in_dim(hologram, depth_index * 16, 16, 0)
-    sent = forward_x(field, hologram_rows, x_forward)
     received = lax.all_to_all(sent, LAYER, 0, 0, tiled=True)
-    field, received = lax.optimization_barrier((field, received))
+    field, received, factors = lax.optimization_barrier((field, received, factors))
     held = jnp.transpose(field.reshape(2, PLANES, 16, N), (1, 0, 2, 3))
     held = lax.all_to_all(held, DEPTH, 0, 0, tiled=True)
     sent = filter_y(rotations, received, factors)

time: 425 us -> 349 us (0.82)
  blocking collectives: 176 us -> 120 us
  Pallas kernels: 158 us -> 123 us
  starting transfers between devices: 19.8 us -> 32.7 us
    all_to_all x1 -> x0, blocking collectives: 60.7 us -> none  [per_device(): received = lax.all_to_all(sent, LAYER, 0, 0, tiled=True)]
    pallas_call x1, Pallas kernels: 121 us -> 86 us  [filter_y(): pl.pallas_call(filter_y_kernel, grid=(2 * CLASSES,), in_specs=[pl.BlockSp...]
    all_to_all x1 -> x2, starting transfers between devices: 5.81 us -> 19.9 us  [per_device(): received = lax.all_to_all(sent, LAYER, 0, 0, tiled=True)]
    unnamed x1, blocking collectives: 57.7 us -> 63.4 us
    all_to_all x1 -> x2, waiting for transfers between devices: 50.5 us -> 50.5 us  [per_device(): received = lax.all_to_all(sent, LAYER, 0, 0, tiled=True)]
  transfers between devices with their start and end apart: 4 -> 5, of which waited for: 3 -> 3; matrix products, arithmetic and copies ran while one was open for 1% -> 2% of each run, Pallas kernels for 29% -> 25%
where the time goes in v5:
time: 349 us
  Pallas kernels  123 us (35%)
  blocking collectives  120 us (34%)
  waiting for transfers between devices  55.5 us (16%)
  starting transfers between devices  32.7 us (9%)
  local copies, waits for them, and re-layouts  11.8 us (3%)
  other arithmetic  4.5 us (1%)
    pallas_call x1, Pallas kernels, filter_y(): pl.pallas_call(filter_y_kernel, grid=(2 * CLASSES,), in_specs=[pl.BlockSp...  86 us
    unnamed x1, blocking collectives  63.4 us
    all_to_all x1, blocking collectives, per_device(): estimate = lax.all_to_all(estimate, DEPTH, 0, 0, tiled=True)  56.5 us
    all_to_all x2, waiting for transfers between devices, per_device(): received = lax.all_to_all(sent, LAYER, 0, 0, tiled=True)  50.5 us
    all_to_all x2, starting transfers between devices, per_device(): received = lax.all_to_all(sent, LAYER, 0, 0, tiled=True)  19.9 us
    pallas_call x1, Pallas kernels, backward_x(): pl.pallas_call(backward_x_kernel, grid=(128 // STEP_ROWS,), in_specs=[pl....  14.8 us
    pallas_call x1, Pallas kernels, forward_x(): pl.pallas_call(forward_x_kernel, grid=(128 // STEP_ROWS,), in_specs=[pl.B...  13.4 us
    pallas_call x1, Pallas kernels, shrink(): pl.pallas_call(shrink_kernel, grid=(steps,), in_specs=[pl.BlockSpec(memor...  9 us
  transfers between devices with their start and end apart: 5, of which 3 were waited for; matrix products, arithmetic and copies ran while one was open for 2% of the time, Pallas kernels for 25%

profile of v5, /device:TPU:2, one launch (start us, length us, event | category | flops | bytes accessed | tf_op | source)
XLA Modules:
  0.0 348.5 jit_solution(10126475421920847132)
XLA Ops:
  0.8 0.8 fusion.1
  1.7 0.7 constant_dynamic-slice_fusion.hol_ref
  3.0 13.4 %filter_x_forward.1 = f32[32,272,128]{2,1,0:T(8,128)} custom-call(f32[2,128,4096]{2,1,0:T(8,128)} %bitcast.23, f32[16,4096]{1,0:T(8,128)} %constant_dynamic-slice_fusion.hol_ref, f32[2,16,256]{2,1,0:T(8,128)} %constant.72.clone.tw_ref, f32[2,16,1,256]{3,2,1,0:T(1,128)} %pad_maximum_fusion.2.d_ref, bf16[1536,512]{1,0:T(8,128)(2,1)} %constant.73.clone.wf_ref, ...), custom_call_target="tpu_custom_call" | custom-call | bytes 42000000 | tf_op jit(solution)/shard_map/filter_x_forward/pallas_call | solution.py:290
  16.4 7.8 %all-to-all-start = ((f32[32,272,128]{2,1,0:T(8,128)}), f32[32,272,128]{2,1,0:T(8,128)}, u32[]{:S(2)}, u32[]{:S(2)}) async-start(f32[32,272,128]{2,1,0:T(8,128)} %filter_x_forward.1), calls=%async_computation | async-start | bytes 8912896 | tf_op jit(solution)/shard_map/all_to_all | solution.py:687
  24.8 0.8 dynamic-update-slice
  25.6 63.4 %all-reduce = f32[8]{0:T(128)S(1)} all-reduce(f32[8]{0:T(128)S(1)} %dynamic-update-slice), channel_id=1, replica_groups=mesh['x_lo'=2,'y'=4,'x_hi'=2,'z'=8,'core'=2] {'x_lo','y'}, use_global_device_ids=true, to_apply=%add | all-reduce | flops 8 | bytes 64
  89.5 0.8 pad_maximum_fusion.cs_ref
  90.3 4.7 %copy.41 = f32[2,8,16,4096]{3,2,0,1:T(8,128)} copy(f32[2,8,16,4096]{3,2,1,0:T(8,128)} %bitcast.24) | data formatting | bytes 8388608 | tf_op jit(solution)/shard_map/reshape | solution.py:689
  94.9 4.8 %all-to-all-start.2 = ((f32[8,2,16,4096]{3,2,1,0:T(8,128)}), f32[8,2,16,4096]{3,2,1,0:T(8,128)}, u32[]{:S(2)}, u32[]{:S(2)}) async-start(f32[8,2,16,4096]{3,2,1,0:T(8,128)} %bitcast.25), calls=%async_computation.2 | async-start | bytes 8388608 | tf_op jit(solution)/shard_map/all_to_all | solution.py:690
  99.8 0.7 copy.36.rot_ref
  100.5 86.0 %filter_y.1 = f32[32,2,128,128]{3,2,1,0:T(8,128)} custom-call(f32[9,4]{1,0:T(8,128)} %copy.36.rot_ref, f32[32,272,128]{2,1,0:T(8,128)} %all-to-all-done.g_ref, bf16[9,768,512]{2,1,0:T(8,128)(2,1)} %constant.76.clone.t_ref, bf16[9,1536,256]{2,1,0:T(8,128)(2,1)} %constant.77.clone.tt_ref, f32[9,16,512]{2,1,0:T(8,128)} %pad_maximum_fusion.cs_ref), custom_call_target="tpu_custom_call" | custom-call | bytes 270000000 | tf_op jit(solution)/shard_map/filter_y/pallas_call | solution.py:524
  186.5 12.1 %all-to-all-start.1 = ((f32[32,2,128,128]{3,2,1,0:T(8,128)}), f32[32,2,128,128]{3,2,1,0:T(8,128)}, u32[]{:S(2)}, u32[]{:S(2)}) async-start(f32[32,2,128,128]{3,2,1,0:T(8,128)} %filter_y.1), calls=%async_computation.1 | async-start | bytes 8388608 | tf_op jit(solution)/shard_map/all_to_all | solution.py:692
  199.2 0.7 maximum_multiply_fusion.d_ref
  200.0 50.5 %all-to-all-done.1.g_ref = f32[32,2,128,128]{3,2,1,0:T(8,128)} async-done(((f32[32,2,128,128]{3,2,1,0:T(8,128)}), f32[32,2,128,128]{3,2,1,0:T(8,128)}, u32[]{:S(2)}, u32[]{:S(2)}) %all-to-all-start.1) | async-done | bytes 4194336 | tf_op jit(solution)/shard_map/all_to_all | solution.py:692
  250.5 14.8 %filter_x_backward.1.m_ref.next_ref = f32[2,128,4096]{2,1,0:T(8,128)} custom-call(f32[32,2,128,128]{3,2,1,0:T(8,128)} %all-to-all-done.1.g_ref, f32[8,2,16,4096]{3,2,1,0:T(8,128)} %all-to-all-done.2.held_ref, f32[2,16,256]{2,1,0:T(8,128)} %constant.72.clone.tw_ref, f32[2,16,8,256]{3,2,1,0:T(8,128)} %maximum_multiply_fusion.d_ref, ...), custom_call_target="tpu_custom_call" | custom-call | bytes 48000000 | tf_op jit(solution)/shard_map/filter_x_backward/pallas_call | solution.py:312
  265.3 1.1 fusion.11
  266.3 1.9 collective-permute-start
  268.3 6.0 %collective-permute-start.1 = (f32[2,8,4096]{2,1,0:T(8,128)S(1)}, f32[2,8,4096]{2,1,0:T(8,128)S(1)}, u32[]{:S(2)}, u32[]{:S(2)}) collective-permute-start(f32[2,8,4096]{2,1,0:T(8,128)S(1)} %get-tuple-element.15), channel_id=1, source_target_pairs={{32,0},{64,32},{96,64},{128,96},{160,128},{192,160},{224,192},{1,2... | collective-permute-start | bytes 786440 | tf_op jit(solution)/shard_map/ppermute | solution.py:650
  274.9 3.8 %collective-permute-done.above_ref = f32[2,8,4096]{2,1,0:T(8,128)S(1)} collective-permute-done((f32[2,8,4096]{2,1,0:T(8,128)S(1)}, f32[2,8,4096]{2,1,0:T(8,128)S(1)}, u32[]{:S(2)}, u32[]{:S(2)}) %collective-permute-start) | collective-permute-done | bytes 262176 | tf_op jit(solution)/shard_map/ppermute | solution.py:650
  278.8 1.2 collective-permute-done.1.below_ref
  280.0 0.7 copy-done.3
  280.6 9.0 %tv_shrink.1 = f32[8,2,16,4096]{3,2,1,0:T(8,128)} custom-call(s32[2]{0:T(128)} %add_convert_fusion.edge_ref, f32[2,128,4096]{2,1,0:T(8,128)} %filter_x_backward.1.m_ref.next_ref, f32[2,128,4096]{2,1,0:T(8,128)} %filter_x_backward.1.m_ref.next_ref, f32[2,8,4096]{2,1,0:T(8,128)} %copy-done.2, f32[2,8,4096]{2,1,0:T(8,128)} %copy-done.3), custom_call_target="tpu_custom_call" | custom-call | bytes 27000000 | tf_op jit(solution)/shard_map/tv_shrink/pallas_call | solution.py:623
  289.6 56.5 %all_to_all.20 = f32[8,2,16,4096]{3,2,1,0:T(8,128)S(1)} all-to-all(f32[8,2,16,4096]{3,2,1,0:T(8,128)} %tv_shrink.1), channel_id=1, replica_groups=mesh['x_lo'=2,'y'=4,'x_hi'=2,'z'=8,'core'=2] {'x_lo','y'}, dimensions={0} | all-to-all | bytes 8388608 | tf_op jit(solution)/shard_map/all_to_all | solution.py:699
  346.1 2.3 copy.38
  (31 shorter events, 3.2 us)
Async XLA Ops:
  0.0 1.7 copy-start
  16.4 7.8 %copy-start.7 = (u32[256]{0:T(256)S(1)}, u32[256]{0:T(256)}, u32[]{:S(2)}) copy-start(u32[256]{0:T(256)} %constant.84) | copy-start | bytes 3076
  16.4 72.5 %copy-start.5 = (f32[9,256]{1,0:T(8,128)S(1)}, f32[9,256]{1,0:T(8,128)}, u32[]{:S(2)}) copy-start(f32[9,256]{1,0:T(8,128)} %constant.80) | copy-start | bytes 27652
  16.4 73.9 %all-to-all-start = ((f32[32,272,128]{2,1,0:T(8,128)}), f32[32,272,128]{2,1,0:T(8,128)}, u32[]{:S(2)}, u32[]{:S(2)}) async-start(f32[32,272,128]{2,1,0:T(8,128)} %filter_x_forward.1), calls=%async_computation | async-start | bytes 8912896 | tf_op jit(solution)/shard_map/all_to_all | solution.py:687
  94.9 4.9 %copy-start.6 = (f32[9]{0:T(128)S(1)}, f32[9]{0:T(128)}, u32[]{:S(2)}) copy-start(f32[9]{0:T(128)} %constant.71.clone) | copy-start | bytes 112
  94.9 91.6 %all-to-all-start.2 = ((f32[8,2,16,4096]{3,2,1,0:T(8,128)}), f32[8,2,16,4096]{3,2,1,0:T(8,128)}, u32[]{:S(2)}, u32[]{:S(2)}) async-start(f32[8,2,16,4096]{3,2,1,0:T(8,128)} %bitcast.25), calls=%async_computation.2 | async-start | bytes 8388608 | tf_op jit(solution)/shard_map/all_to_all | solution.py:690
  186.5 12.2 %copy-start.4 = (f32[16,256]{1,0:T(8,128)S(1)}, f32[16,256]{1,0:T(8,128)}, u32[]{:S(2)}) copy-start(f32[16,256]{1,0:T(8,128)} %constant.81) | copy-start | bytes 49156
  186.5 63.9 %all-to-all-start.1 = ((f32[32,2,128,128]{3,2,1,0:T(8,128)}), f32[32,2,128,128]{3,2,1,0:T(8,128)}, u32[]{:S(2)}, u32[]{:S(2)}) async-start(f32[32,2,128,128]{3,2,1,0:T(8,128)} %filter_y.1), calls=%async_computation.1 | async-start | bytes 8388608 | tf_op jit(solution)/shard_map/all_to_all | solution.py:692
  266.3 12.4 %collective-permute-start = (f32[2,8,4096]{2,1,0:T(8,128)S(1)}, f32[2,8,4096]{2,1,0:T(8,128)S(1)}, u32[]{:S(2)}, u32[]{:S(2)}) collective-permute-start(f32[2,8,4096]{2,1,0:T(8,128)S(1)} %get-tuple-element.16), channel_id=1, source_target_pairs={{0,32},{32,64},{64,96},{96,128},{128,160},{160,192},{192,224},{224... | collective-permute-start | bytes 786440 | tf_op jit(solution)/shard_map/ppermute | solution.py:650
  268.3 11.7 %collective-permute-start.1 = (f32[2,8,4096]{2,1,0:T(8,128)S(1)}, f32[2,8,4096]{2,1,0:T(8,128)S(1)}, u32[]{:S(2)}, u32[]{:S(2)}) collective-permute-start(f32[2,8,4096]{2,1,0:T(8,128)S(1)} %get-tuple-element.15), channel_id=1, source_target_pairs={{32,0},{64,32},{96,64},{128,96},{160,128},{192,160},{224,192},{1,2... | collective-permute-start | bytes 786440 | tf_op jit(solution)/shard_map/ppermute | solution.py:650
  278.8 1.2 copy-start.2
  280.0 0.7 copy-start.3
  346.1 2.4 copy-start.1

commit v6 on v5

--- a/solution.py
+++ b/solution.py
@@ -223,13 +223,14 @@
     return jnp.concatenate([factor] * (STEP_ROWS // factor.shape[0]), axis=0)
 
 
-def forward_x_kernel(f_ref, hol_ref, tw_ref, d_ref, wf_ref, wi_ref, o_ref, x_ref):
+def forward_x_kernel(f_ref, hol_ref, depth_ref, tw_ref, d_ref, wf_ref, wi_ref, o_ref, x_ref):
     step = pl.program_id(0)
 
     @pl.when(step == 0)
     def _():
         for j in range(32):
             o_ref[j, 256:272, :] = hol_ref[:, j * LANES : (j + 1) * LANES]
+            o_ref[j, 272:280, :] = depth_ref[...]
 
     def load(r, j):
         rows, lanes = slice(8 * r, 8 * r + 8), slice(j * LANES, (j + 1) * LANES)
@@ -285,7 +286,7 @@
     return jnp.asarray(twiddles()), jnp.asarray(forward), jnp.asarray(inverse)
 
 
-def forward_x(field, hologram_rows, transfer):
+def forward_x(field, hologram_rows, depth_rows, transfer):
     tw, wf, wi = x_tables()
     return pl.pallas_call(
         forward_x_kernel,
@@ -293,18 +294,19 @@
         in_specs=[
             pl.BlockSpec((2, STEP_ROWS, N), lambda i: (0, i, 0)),
             whole((16, N)),
+            whole((8, LANES)),
             whole((2, RADIX, INNER)),
             whole((2, RADIX, 1, INNER)),
             whole((1536, 512)),
             whole((1536, 512)),
         ],
-        out_specs=whole((32, 272, LANES)),
-        out_shape=jax.ShapeDtypeStruct((32, 272, LANES), F32),
+        out_specs=whole((32, 280, LANES)),
+        out_shape=jax.ShapeDtypeStruct((32, 280, LANES), F32),
         scratch_shapes=[pltpu.VMEM((RADIX * STEP_ROWS, 2 * INNER), F32)],
         compiler_params=params(),
         cost_estimate=cost_of(14),
         name="filter_x_forward",
-    )(field, hologram_rows, tw, transfer, wf, wi)
+    )(field, hologram_rows, depth_rows, tw, transfer, wf, wi)
 
 
 def backward_x(gradient, held, transfer):
@@ -337,10 +339,25 @@
 LONG = LAYERS // 2
 SHORT = LAYERS - 1 - LONG
 HOPS = 2 * LONG
+TURN_HIGH = 6.28125
+TURN_LOW = 2.0 * math.pi - TURN_HIGH
 
 
 def filter_y_kernel(
-    rot_ref, g_ref, t_ref, tt_ref, cs_ref, o_ref, u_ref, s_ref, h_ref, r_ref, a_ref, send_sem, recv_sem
+    rot_ref,
+    g_ref,
+    t_ref,
+    tt_ref,
+    sq_ref,
+    o_ref,
+    u_ref,
+    s_ref,
+    h_ref,
+    r_ref,
+    a_ref,
+    cs_ref,
+    send_sem,
+    recv_sem,
 ):
     step = pl.program_id(0)
     me = lax.axis_index("z")
@@ -403,6 +420,10 @@
 
         gather(0, LONG, block(LONG - h))
         gather(1, SHORT, block(h - LONG))
+
+    def factor(k, c, p):
+        row = cs_ref[k, c, p : p + 1, :]
+        return jnp.concatenate([row, row], axis=1)
 
     def progress(slot):
         @pl.loop(0, CLASSES)
@@ -425,6 +446,17 @@
             )
         pl.semaphore_wait(barrier, 2)
 
+        depths = jnp.concatenate([g_ref[p * 4, 272:273, :] for p in range(PLANES)], axis=0)
+        depths = jnp.concatenate([depths, depths], axis=1)
+
+        @pl.loop(0, CLASSES)
+        def _(k):
+            phase = depths * sq_ref[k]
+            whole_turns = jnp.floor(phase * (0.5 / math.pi) + 0.5)
+            phase = (phase - whole_turns * TURN_HIGH) - whole_turns * TURN_LOW
+            cs_ref[k, 0] = jnp.cos(phase)
+            cs_ref[k, 1] = jnp.sin(phase)
+
         def place(p, lanes, core, upper, lower):
             for parity, value in ((0, upper + lower), (1, upper - lower)):
                 high, low = halves(value)
@@ -444,7 +476,7 @@
         for core in range(2):
             tiles = []
             for upper in range(2):
-                rows = [g_ref[p * 4 + upper * 2 + core, 256:, :] for p in range(PLANES)]
+                rows = [g_ref[p * 4 + upper * 2 + core, 256:272, :] for p in range(PLANES)]
                 tiles.append(jnp.concatenate(rows, axis=0).T)
             place(PLANES, slice(0, LANES), core, tiles[0], tiles[1])
 
@@ -457,8 +489,8 @@
                 result = jnp.dot(u_ref[parity, p], t_ref[0], preferred_element_type=F32)
                 total = (
                     total
-                    + cs_ref[0, 2 * p : 2 * p + 1, :] * result[:LANES]
-                    + cs_ref[0, 2 * p + 1 : 2 * p + 2, :] * result[LANES:]
+                    + factor(step, 0, p) * result[:LANES]
+                    + factor(step, 1, p) * result[LANES:]
                 )
             return total
 
@@ -483,8 +515,8 @@
             for p in range(first, first + PLANES // 2):
                 product = jnp.concatenate(
                     [
-                        cs_ref[0, 2 * p : 2 * p + 1, :] * spectrum,
-                        cs_ref[0, 2 * p + 1 : 2 * p + 2, :] * spectrum,
+                        factor(k, 0, p) * spectrum,
+                        factor(k, 1, p) * spectrum,
                     ],
                     axis=0,
                 )
@@ -518,18 +550,20 @@
                         o_ref[owner * 4 + 2 + core, c, held, :] = lower[part]
 
 
-def filter_y(rotations, received, factors):
+def filter_y(rotations, received):
     forward, backward = class_tables()
     last = CLASSES - 1
+    squares = squares_of(class_frequencies())[:, None, :] * np.float32(math.pi / (N * N))
+    squares = jnp.asarray(np.repeat(squares, PLANES, axis=1))
     return pl.pallas_call(
         filter_y_kernel,
         grid=(2 * CLASSES,),
         in_specs=[
             pl.BlockSpec(memory_space=pltpu.SMEM),
-            whole((32, 272, LANES)),
+            whole((32, 280, LANES)),
             pl.BlockSpec((1, 768, 512), lambda i: (jnp.minimum(i, last), 0, 0)),
             pl.BlockSpec((1, 1536, 256), lambda i: (jnp.maximum(i - CLASSES, 0), 0, 0)),
-            pl.BlockSpec((1, 16, 512), lambda i: (lax.rem(i, CLASSES), 0, 0)),
+            whole((CLASSES, PLANES, INNER)),
         ],
         out_specs=whole((32, 2, 128, LANES)),
         out_shape=jax.ShapeDtypeStruct((32, 2, 128, LANES), F32),
@@ -539,6 +573,7 @@
             pltpu.VMEM((CLASSES, LANES, 2 * INNER), F32),
             pltpu.VMEM((CLASSES, LONG + SHORT, PART, 2 * INNER), F32),
             pltpu.VMEM((2, PLANES, 2 * LANES, INNER), F32),
+            pltpu.VMEM((CLASSES, 2, PLANES, INNER), F32),
             pltpu.SemaphoreType.DMA((CLASSES, 2)),
             pltpu.SemaphoreType.DMA((CLASSES, 2, HOPS)),
         ],
@@ -547,7 +582,7 @@
         ),
         cost_estimate=cost_of(90),
         name="filter_y",
-    )(rotations, received, jnp.asarray(forward), jnp.asarray(backward), factors)
+    )(rotations, received, jnp.asarray(forward), jnp.asarray(backward), squares)
 
 
 TV_ROWS = 8
@@ -674,21 +709,16 @@
     rotations = jnp.stack([weights * cosine, weights * sine, cosine, sine], axis=1)
 
     hologram_rows = lax.dynamic_slice_in_dim(hologram, depth_index * 16, 16, 0)
-    sent = forward_x(field, hologram_rows, x_forward)
-    defocus, sent = lax.optimization_barrier((defocus, sent))
-    depths = lax.all_gather(defocus, DEPTH, tiled=True)
+    depth_rows = jnp.full((8, LANES), defocus[0])
+    sent = forward_x(field, hologram_rows, depth_rows, x_forward)
+    held = jnp.transpose(field.reshape(2, PLANES, 16, N), (1, 0, 2, 3))
+    received = lax.all_to_all(sent, LAYER, 0, 0, tiled=True)
+    held, received, rotations = lax.optimization_barrier((held, received, rotations))
+    held = lax.all_to_all(held, DEPTH, 0, 0, tiled=True)
+    depths = received[::4, 272, 0]
+    sent = filter_y(rotations, received)
     x_phase = phase_of(depths[None, :, None], x_squares)
     x_backward = jnp.stack([jnp.cos(x_phase), jnp.sin(x_phase)]) * (-1.0 / (PLANES * N))
-    y_squares = jnp.asarray(squares_of(class_frequencies()))[:, None, None, :]
-    y_phase = phase_of(depths[None, :, None, None], y_squares)
-    factors = jnp.concatenate([jnp.cos(y_phase), jnp.sin(y_phase)], axis=2)
-    factors = factors.reshape(CLASSES, 2 * PLANES, INNER)
-    factors = jnp.concatenate([factors, factors], axis=2)
-    received = lax.all_to_all(sent, LAYER, 0, 0, tiled=True)
-    field, received, factors = lax.optimization_barrier((field, received, factors))
-    held = jnp.transpose(field.reshape(2, PLANES, 16, N), (1, 0, 2, 3))
-    held = lax.all_to_all(held, DEPTH, 0, 0, tiled=True)
-    sent = filter_y(rotations, received, factors)
     received = lax.all_to_all(sent, LAYER, 0, 0, tiled=True)
     moved = backward_x(received, held, x_backward)
     above = along_rows(moved[:, 120:], 1)

time: 349 us -> 334 us (0.957)
  blocking collectives: 120 us -> 56.5 us
  waiting for transfers between devices: 55.5 us -> 106 us
    unnamed x1 -> x0, blocking collectives: 63.4 us -> none
    all_to_all x2, waiting for transfers between devices: 50.5 us -> 101 us  [per_device(): received = lax.all_to_all(sent, LAYER, 0, 0, tiled=True)]
    reshape x2 -> x0, local copies, waits for them, and re-layouts: 4.76 us -> none  [the longest x1 4.65 us: per_device(): held = jnp.transpose(field.reshape(2, PLANES, 16, N), (1, 0, 2, 3))]
    all_to_all x2, starting transfers between devices: 19.9 us -> 15.4 us  [per_device(): received = lax.all_to_all(sent, LAYER, 0, 0, tiled=True)]
    another operation x1, local copies, waits for them, and re-layouts: 0.69 us -> 4.66 us  [per_device(): held = jnp.transpose(field.reshape(2, PLANES, 16, N), (1, 0, 2, 3))]
  transfers between devices with their start and end apart: 5 -> 5, of which waited for: 3 -> 4; matrix products, arithmetic and copies ran while one was open for 2% -> 2% of each run, Pallas kernels for 25% -> 26%
where the time goes in v6:
time: 334 us; the launch traced here: 333 us
  Pallas kernels  123 us (37%)
  waiting for transfers between devices  106 us (32%)
  blocking collectives  56.5 us (17%)
  starting transfers between devices  31.2 us (9%)
  local copies, waits for them, and re-layouts  11.8 us (4%)
  other arithmetic  3.44 us (1%)
    all_to_all x2, waiting for transfers between devices, per_device(): received = lax.all_to_all(sent, LAYER, 0, 0, tiled=True)  101 us
    pallas_call x1, Pallas kernels, filter_y(): pl.pallas_call(filter_y_kernel, grid=(2 * CLASSES,), in_specs=[pl.BlockSp...  85.9 us
    all_to_all x1, blocking collectives, per_device(): estimate = lax.all_to_all(estimate, DEPTH, 0, 0, tiled=True)  56.5 us
    all_to_all x2, starting transfers between devices, per_device(): received = lax.all_to_all(sent, LAYER, 0, 0, tiled=True)  15.4 us
    pallas_call x1, Pallas kernels, backward_x(): pl.pallas_call(backward_x_kernel, grid=(128 // STEP_ROWS,), in_specs=[pl....  14.8 us
    pallas_call x1, Pallas kernels, forward_x(): pl.pallas_call(forward_x_kernel, grid=(128 // STEP_ROWS,), in_specs=[pl.B...  13.3 us
    pallas_call x1, Pallas kernels, shrink(): pl.pallas_call(shrink_kernel, grid=(steps,), in_specs=[pl.BlockSpec(memor...  8.97 us
    ppermute x2, starting transfers between devices, along_rows(): return lax.ppermute(block, DEPTH + ROW, route)  7.96 us
  transfers between devices with their start and end apart: 5, of which 4 were waited for; matrix products, arithmetic and copies ran while one was open for 2% of the time, Pallas kernels for 26%

profile of v6, /device:TPU:2, one launch (start us, length us, event | category | flops | bytes accessed | tf_op | source)
XLA Modules:
  0.0 333.0 jit_solution(3248944223742325936)
XLA Ops:
  0.8 0.8 fusion.1
  1.7 0.7 constant_dynamic-slice_fusion.hol_ref
  3.6 13.3 %filter_x_forward.1 = f32[32,280,128]{2,1,0:T(8,128)} custom-call(f32[2,128,4096]{2,1,0:T(8,128)} %bitcast.24, f32[16,4096]{1,0:T(8,128)} %constant_dynamic-slice_fusion.hol_ref, f32[8,128]{1,0:T(8,128)} %broadcast_in_dim.4.depth_ref, f32[2,16,256]{2,1,0:T(8,128)} %constant.69.clone.tw_ref, f32[2,16,1,256]{3,2,1,0:T(1,128)} %pad_maximum_fusion.d_ref, ...), custom_call_target="tpu_custom_call" | custom-call | bytes 42000000 | tf_op jit(solution)/shard_map/filter_x_forward/pallas_call | solution.py:291
  16.9 7.7 %all-to-all-start = ((f32[32,280,128]{2,1,0:T(8,128)}), f32[32,280,128]{2,1,0:T(8,128)}, u32[]{:S(2)}, u32[]{:S(2)}) async-start(f32[32,280,128]{2,1,0:T(8,128)} %filter_x_forward.1), calls=%async_computation | async-start | bytes 9175040 | tf_op jit(solution)/shard_map/all_to_all | solution.py:715
  24.6 4.7 %copy.35 = f32[2,8,16,4096]{3,2,0,1:T(8,128)} copy(f32[2,8,16,4096]{3,2,1,0:T(8,128)} %bitcast.25) | data formatting | bytes 8388608 | tf_op jit(solution)/shard_map/reshape;squeeze | solution.py:714
  29.4 51.7 %all-to-all-done.g_ref = f32[32,280,128]{2,1,0:T(8,128)} async-done(((f32[32,280,128]{2,1,0:T(8,128)}), f32[32,280,128]{2,1,0:T(8,128)}, u32[]{:S(2)}, u32[]{:S(2)}) %all-to-all-start) | async-done | bytes 4587552 | tf_op jit(solution)/shard_map/all_to_all | solution.py:715
  81.1 7.8 %all-to-all-start.2 = ((f32[8,2,16,4096]{3,2,1,0:T(8,128)}), f32[8,2,16,4096]{3,2,1,0:T(8,128)}, u32[]{:S(2)}, u32[]{:S(2)}) async-start(f32[8,2,16,4096]{3,2,1,0:T(8,128)} %bitcast.26), calls=%async_computation.2 | async-start | bytes 8388608 | tf_op jit(solution)/shard_map/all_to_all | solution.py:717
  88.9 0.7 copy.31.rot_ref
  89.6 85.9 %filter_y.1 = f32[32,2,128,128]{3,2,1,0:T(8,128)} custom-call(f32[9,4]{1,0:T(8,128)} %copy.31.rot_ref, f32[32,280,128]{2,1,0:T(8,128)} %all-to-all-done.g_ref, bf16[9,768,512]{2,1,0:T(8,128)(2,1)} %constant.73.clone.t_ref, bf16[9,1536,256]{2,1,0:T(8,128)(2,1)} %constant.74.clone.tt_ref, f32[9,8,256]{2,1,0:T(8,128)} %constant.72.clone.sq_ref), custom_call_target="tpu_custom_call" | custom-call | bytes 270000000 | tf_op jit(solution)/shard_map/filter_y/pallas_call | solution.py:558
  175.4 7.7 %all-to-all-start.1 = ((f32[32,2,128,128]{3,2,1,0:T(8,128)}), f32[32,2,128,128]{3,2,1,0:T(8,128)}, u32[]{:S(2)}, u32[]{:S(2)}) async-start(f32[32,2,128,128]{3,2,1,0:T(8,128)} %filter_y.1), calls=%async_computation.1 | async-start | bytes 8388608 | tf_op jit(solution)/shard_map/all_to_all | solution.py:722
  183.2 0.9 slice_reduce_fusion
  184.6 0.7 maximum_multiply_fusion.d_ref
  185.4 49.6 %all-to-all-done.1.g_ref = f32[32,2,128,128]{3,2,1,0:T(8,128)} async-done(((f32[32,2,128,128]{3,2,1,0:T(8,128)}), f32[32,2,128,128]{3,2,1,0:T(8,128)}, u32[]{:S(2)}, u32[]{:S(2)}) %all-to-all-start.1) | async-done | bytes 4194336 | tf_op jit(solution)/shard_map/all_to_all | solution.py:722
  235.0 14.8 %filter_x_backward.1.m_ref.next_ref = f32[2,128,4096]{2,1,0:T(8,128)} custom-call(f32[32,2,128,128]{3,2,1,0:T(8,128)} %all-to-all-done.1.g_ref, f32[8,2,16,4096]{3,2,1,0:T(8,128)} %all-to-all-done.2.held_ref, f32[2,16,256]{2,1,0:T(8,128)} %constant.69.clone.tw_ref, f32[2,16,8,256]{3,2,1,0:T(8,128)} %maximum_multiply_fusion.d_ref, ...), custom_call_target="tpu_custom_call" | custom-call | bytes 48000000 | tf_op jit(solution)/shard_map/filter_x_backward/pallas_call | solution.py:314
  249.8 1.1 fusion.11
  250.9 1.9 collective-permute-start
  252.8 6.0 %collective-permute-start.1 = (f32[2,8,4096]{2,1,0:T(8,128)S(1)}, f32[2,8,4096]{2,1,0:T(8,128)S(1)}, u32[]{:S(2)}, u32[]{:S(2)}) collective-permute-start(f32[2,8,4096]{2,1,0:T(8,128)S(1)} %get-tuple-element.11), channel_id=1, source_target_pairs={{32,0},{64,32},{96,64},{128,96},{160,128},{192,160},{224,192},{1,2... | collective-permute-start | bytes 786440 | tf_op jit(solution)/shard_map/ppermute | solution.py:685
  258.9 0.6 add_convert_fusion.edge_ref
  259.5 3.8 %collective-permute-done.above_ref = f32[2,8,4096]{2,1,0:T(8,128)S(1)} collective-permute-done((f32[2,8,4096]{2,1,0:T(8,128)S(1)}, f32[2,8,4096]{2,1,0:T(8,128)S(1)}, u32[]{:S(2)}, u32[]{:S(2)}) %collective-permute-start) | collective-permute-done | bytes 262176 | tf_op jit(solution)/shard_map/ppermute | solution.py:685
  263.3 1.2 collective-permute-done.1.below_ref
  264.5 0.7 copy-done.3
  265.2 9.0 %tv_shrink.1 = f32[8,2,16,4096]{3,2,1,0:T(8,128)} custom-call(s32[2]{0:T(128)} %add_convert_fusion.edge_ref, f32[2,128,4096]{2,1,0:T(8,128)} %filter_x_backward.1.m_ref.next_ref, f32[2,128,4096]{2,1,0:T(8,128)} %filter_x_backward.1.m_ref.next_ref, f32[2,8,4096]{2,1,0:T(8,128)} %copy-done.2, f32[2,8,4096]{2,1,0:T(8,128)} %copy-done.3), custom_call_target="tpu_custom_call" | custom-call | bytes 27000000 | tf_op jit(solution)/shard_map/tv_shrink/pallas_call | solution.py:658
  274.2 56.5 %all_to_all.20 = f32[8,2,16,4096]{3,2,1,0:T(8,128)S(1)} all-to-all(f32[8,2,16,4096]{3,2,1,0:T(8,128)} %tv_shrink.1), channel_id=1, replica_groups=mesh['x_lo'=2,'y'=4,'x_hi'=2,'z'=8,'core'=2] {'x_lo','y'}, dimensions={0} | all-to-all | bytes 8388608 | tf_op jit(solution)/shard_map/all_to_all | solution.py:729
  330.6 2.3 copy.32
  (20 shorter events, 2.0 us)
Async XLA Ops:
  0.0 1.7 copy-start
  16.9 64.2 %all-to-all-start = ((f32[32,280,128]{2,1,0:T(8,128)}), f32[32,280,128]{2,1,0:T(8,128)}, u32[]{:S(2)}, u32[]{:S(2)}) async-start(f32[32,280,128]{2,1,0:T(8,128)} %filter_x_forward.1), calls=%async_computation | async-start | bytes 9175040 | tf_op jit(solution)/shard_map/all_to_all | solution.py:715
  24.6 4.7 %copy-start.5 = (f32[9]{0:T(128)S(1)}, f32[9]{0:T(128)}, u32[]{:S(2)}) copy-start(f32[9]{0:T(128)} %constant.68.clone) | copy-start | bytes 112
  81.1 94.4 %all-to-all-start.2 = ((f32[8,2,16,4096]{3,2,1,0:T(8,128)}), f32[8,2,16,4096]{3,2,1,0:T(8,128)}, u32[]{:S(2)}, u32[]{:S(2)}) async-start(f32[8,2,16,4096]{3,2,1,0:T(8,128)} %bitcast.26), calls=%async_computation.2 | async-start | bytes 8388608 | tf_op jit(solution)/shard_map/all_to_all | solution.py:717
  175.4 8.7 %copy-start.4 = (f32[16,256]{1,0:T(8,128)S(1)}, f32[16,256]{1,0:T(8,128)}, u32[]{:S(2)}) copy-start(f32[16,256]{1,0:T(8,128)} %constant.77) | copy-start | bytes 49156
  175.4 59.6 %all-to-all-start.1 = ((f32[32,2,128,128]{3,2,1,0:T(8,128)}), f32[32,2,128,128]{3,2,1,0:T(8,128)}, u32[]{:S(2)}, u32[]{:S(2)}) async-start(f32[32,2,128,128]{3,2,1,0:T(8,128)} %filter_y.1), calls=%async_computation.1 | async-start | bytes 8388608 | tf_op jit(solution)/shard_map/all_to_all | solution.py:722
  250.9 12.4 %collective-permute-start = (f32[2,8,4096]{2,1,0:T(8,128)S(1)}, f32[2,8,4096]{2,1,0:T(8,128)S(1)}, u32[]{:S(2)}, u32[]{:S(2)}) collective-permute-start(f32[2,8,4096]{2,1,0:T(8,128)S(1)} %get-tuple-element.12), channel_id=1, source_target_pairs={{0,32},{32,64},{64,96},{96,128},{128,160},{160,192},{192,224},{224... | collective-permute-start | bytes 786440 | tf_op jit(solution)/shard_map/ppermute | solution.py:685
  252.8 11.7 %collective-permute-start.1 = (f32[2,8,4096]{2,1,0:T(8,128)S(1)}, f32[2,8,4096]{2,1,0:T(8,128)S(1)}, u32[]{:S(2)}, u32[]{:S(2)}) collective-permute-start(f32[2,8,4096]{2,1,0:T(8,128)S(1)} %get-tuple-element.11), channel_id=1, source_target_pairs={{32,0},{64,32},{96,64},{128,96},{160,128},{192,160},{224,192},{1,2... | collective-permute-start | bytes 786440 | tf_op jit(solution)/shard_map/ppermute | solution.py:685
  263.3 1.2 copy-start.2
  264.5 0.7 copy-start.3
  330.6 2.4 copy-start.1

commit v7 on v6

--- a/solution.py
+++ b/solution.py
@@ -427,7 +427,8 @@
 
     def progress(slot):
         @pl.loop(0, CLASSES)
-        def _(k):
+        def _(i):
+            k = CLASSES - 1 - i
             h = slot - k
 
             @pl.when((h >= 0) & (h <= HOPS))

time: 334 us -> 329 us (0.985)
  transfers between devices with their start and end apart: 5 -> 5, of which waited for: 4 -> 4; matrix products, arithmetic and copies ran while one was open for 2% -> 3% of each run, Pallas kernels for 26% -> 25%
where the time goes in v7:
time: 329 us; the launch traced here: 328 us
  Pallas kernels  120 us (36%)
  waiting for transfers between devices  106 us (32%)
  blocking collectives  56.6 us (17%)
  starting transfers between devices  29.8 us (9%)
  local copies, waits for them, and re-layouts  11.8 us (4%)
  other arithmetic  3.44 us (1%)
    all_to_all x2, waiting for transfers between devices, per_device(): received = lax.all_to_all(sent, LAYER, 0, 0, tiled=True)  101 us
    pallas_call x1, Pallas kernels, filter_y(): pl.pallas_call(filter_y_kernel, grid=(2 * CLASSES,), in_specs=[pl.BlockSp...  82.6 us
    all_to_all x1, blocking collectives, per_device(): estimate = lax.all_to_all(estimate, DEPTH, 0, 0, tiled=True)  56.6 us
    pallas_call x1, Pallas kernels, backward_x(): pl.pallas_call(backward_x_kernel, grid=(128 // STEP_ROWS,), in_specs=[pl....  14.8 us
    all_to_all x2, starting transfers between devices, per_device(): received = lax.all_to_all(sent, LAYER, 0, 0, tiled=True)  14.1 us
    pallas_call x1, Pallas kernels, forward_x(): pl.pallas_call(forward_x_kernel, grid=(128 // STEP_ROWS,), in_specs=[pl.B...  13.3 us
    pallas_call x1, Pallas kernels, shrink(): pl.pallas_call(shrink_kernel, grid=(steps,), in_specs=[pl.BlockSpec(memor...  8.97 us
    ppermute x2, starting transfers between devices, along_rows(): return lax.ppermute(block, DEPTH + ROW, route)  7.96 us
  transfers between devices with their start and end apart: 5, of which 4 were waited for; matrix products, arithmetic and copies ran while one was open for 3% of the time, Pallas kernels for 25%

profile of v7, /device:TPU:2, one launch (start us, length us, event | category | flops | bytes accessed | tf_op | source)
XLA Modules:
  0.0 328.5 jit_solution(2452541737387949611)
XLA Ops:
  0.8 0.8 fusion.1
  1.7 0.7 constant_dynamic-slice_fusion.hol_ref
  3.6 13.3 %filter_x_forward.1 = f32[32,280,128]{2,1,0:T(8,128)} custom-call(f32[2,128,4096]{2,1,0:T(8,128)} %bitcast.24, f32[16,4096]{1,0:T(8,128)} %constant_dynamic-slice_fusion.hol_ref, f32[8,128]{1,0:T(8,128)} %broadcast_in_dim.4.depth_ref, f32[2,16,256]{2,1,0:T(8,128)} %constant.69.clone.tw_ref, f32[2,16,1,256]{3,2,1,0:T(1,128)} %pad_maximum_fusion.d_ref, ...), custom_call_target="tpu_custom_call" | custom-call | bytes 42000000 | tf_op jit(solution)/shard_map/filter_x_forward/pallas_call | solution.py:291
  16.9 7.7 %all-to-all-start = ((f32[32,280,128]{2,1,0:T(8,128)}), f32[32,280,128]{2,1,0:T(8,128)}, u32[]{:S(2)}, u32[]{:S(2)}) async-start(f32[32,280,128]{2,1,0:T(8,128)} %filter_x_forward.1), calls=%async_computation | async-start | bytes 9175040 | tf_op jit(solution)/shard_map/all_to_all | solution.py:716
  24.6 4.7 %copy.35 = f32[2,8,16,4096]{3,2,0,1:T(8,128)} copy(f32[2,8,16,4096]{3,2,1,0:T(8,128)} %bitcast.25) | data formatting | bytes 8388608 | tf_op jit(solution)/shard_map/reshape;squeeze | solution.py:715
  29.4 51.7 %all-to-all-done.g_ref = f32[32,280,128]{2,1,0:T(8,128)} async-done(((f32[32,280,128]{2,1,0:T(8,128)}), f32[32,280,128]{2,1,0:T(8,128)}, u32[]{:S(2)}, u32[]{:S(2)}) %all-to-all-start) | async-done | bytes 4587552 | tf_op jit(solution)/shard_map/all_to_all | solution.py:716
  81.1 7.8 %all-to-all-start.2 = ((f32[8,2,16,4096]{3,2,1,0:T(8,128)}), f32[8,2,16,4096]{3,2,1,0:T(8,128)}, u32[]{:S(2)}, u32[]{:S(2)}) async-start(f32[8,2,16,4096]{3,2,1,0:T(8,128)} %bitcast.26), calls=%async_computation.2 | async-start | bytes 8388608 | tf_op jit(solution)/shard_map/all_to_all | solution.py:718
  88.9 0.7 copy.31.rot_ref
  89.6 82.6 %filter_y.1 = f32[32,2,128,128]{3,2,1,0:T(8,128)} custom-call(f32[9,4]{1,0:T(8,128)} %copy.31.rot_ref, f32[32,280,128]{2,1,0:T(8,128)} %all-to-all-done.g_ref, bf16[9,768,512]{2,1,0:T(8,128)(2,1)} %constant.73.clone.t_ref, bf16[9,1536,256]{2,1,0:T(8,128)(2,1)} %constant.74.clone.tt_ref, f32[9,8,256]{2,1,0:T(8,128)} %constant.72.clone.sq_ref), custom_call_target="tpu_custom_call" | custom-call | bytes 270000000 | tf_op jit(solution)/shard_map/filter_y/pallas_call | solution.py:559
  172.2 6.4 %all-to-all-start.1 = ((f32[32,2,128,128]{3,2,1,0:T(8,128)}), f32[32,2,128,128]{3,2,1,0:T(8,128)}, u32[]{:S(2)}, u32[]{:S(2)}) async-start(f32[32,2,128,128]{3,2,1,0:T(8,128)} %filter_y.1), calls=%async_computation.1 | async-start | bytes 8388608 | tf_op jit(solution)/shard_map/all_to_all | solution.py:723
  178.6 0.9 slice_reduce_fusion
  180.0 0.7 maximum_multiply_fusion.d_ref
  180.7 49.6 %all-to-all-done.1.g_ref = f32[32,2,128,128]{3,2,1,0:T(8,128)} async-done(((f32[32,2,128,128]{3,2,1,0:T(8,128)}), f32[32,2,128,128]{3,2,1,0:T(8,128)}, u32[]{:S(2)}, u32[]{:S(2)}) %all-to-all-start.1) | async-done | bytes 4194336 | tf_op jit(solution)/shard_map/all_to_all | solution.py:723
  230.4 14.8 %filter_x_backward.1.m_ref.next_ref = f32[2,128,4096]{2,1,0:T(8,128)} custom-call(f32[32,2,128,128]{3,2,1,0:T(8,128)} %all-to-all-done.1.g_ref, f32[8,2,16,4096]{3,2,1,0:T(8,128)} %all-to-all-done.2.held_ref, f32[2,16,256]{2,1,0:T(8,128)} %constant.69.clone.tw_ref, f32[2,16,8,256]{3,2,1,0:T(8,128)} %maximum_multiply_fusion.d_ref, ...), custom_call_target="tpu_custom_call" | custom-call | bytes 48000000 | tf_op jit(solution)/shard_map/filter_x_backward/pallas_call | solution.py:314
  245.2 1.1 fusion.11
  246.2 1.9 collective-permute-start
  248.2 6.0 %collective-permute-start.1 = (f32[2,8,4096]{2,1,0:T(8,128)S(1)}, f32[2,8,4096]{2,1,0:T(8,128)S(1)}, u32[]{:S(2)}, u32[]{:S(2)}) collective-permute-start(f32[2,8,4096]{2,1,0:T(8,128)S(1)} %get-tuple-element.11), channel_id=1, source_target_pairs={{32,0},{64,32},{96,64},{128,96},{160,128},{192,160},{224,192},{1,2... | collective-permute-start | bytes 786440 | tf_op jit(solution)/shard_map/ppermute | solution.py:686
  254.2 0.6 add_convert_fusion.edge_ref
  254.9 3.8 %collective-permute-done.above_ref = f32[2,8,4096]{2,1,0:T(8,128)S(1)} collective-permute-done((f32[2,8,4096]{2,1,0:T(8,128)S(1)}, f32[2,8,4096]{2,1,0:T(8,128)S(1)}, u32[]{:S(2)}, u32[]{:S(2)}) %collective-permute-start) | collective-permute-done | bytes 262176 | tf_op jit(solution)/shard_map/ppermute | solution.py:686
  258.7 1.2 collective-permute-done.1.below_ref
  259.8 0.7 copy-done.3
  260.6 9.0 %tv_shrink.1 = f32[8,2,16,4096]{3,2,1,0:T(8,128)} custom-call(s32[2]{0:T(128)} %add_convert_fusion.edge_ref, f32[2,128,4096]{2,1,0:T(8,128)} %filter_x_backward.1.m_ref.next_ref, f32[2,128,4096]{2,1,0:T(8,128)} %filter_x_backward.1.m_ref.next_ref, f32[2,8,4096]{2,1,0:T(8,128)} %copy-done.2, f32[2,8,4096]{2,1,0:T(8,128)} %copy-done.3), custom_call_target="tpu_custom_call" | custom-call | bytes 27000000 | tf_op jit(solution)/shard_map/tv_shrink/pallas_call | solution.py:659
  269.5 56.6 %all_to_all.20 = f32[8,2,16,4096]{3,2,1,0:T(8,128)S(1)} all-to-all(f32[8,2,16,4096]{3,2,1,0:T(8,128)} %tv_shrink.1), channel_id=1, replica_groups=mesh['x_lo'=2,'y'=4,'x_hi'=2,'z'=8,'core'=2] {'x_lo','y'}, dimensions={0} | all-to-all | bytes 8388608 | tf_op jit(solution)/shard_map/all_to_all | solution.py:730
  326.1 2.3 copy.32
  (20 shorter events, 2.0 us)
Async XLA Ops:
  0.0 1.7 copy-start
  16.9 64.2 %all-to-all-start = ((f32[32,280,128]{2,1,0:T(8,128)}), f32[32,280,128]{2,1,0:T(8,128)}, u32[]{:S(2)}, u32[]{:S(2)}) async-start(f32[32,280,128]{2,1,0:T(8,128)} %filter_x_forward.1), calls=%async_computation | async-start | bytes 9175040 | tf_op jit(solution)/shard_map/all_to_all | solution.py:716
  24.6 4.7 %copy-start.5 = (f32[9]{0:T(128)S(1)}, f32[9]{0:T(128)}, u32[]{:S(2)}) copy-start(f32[9]{0:T(128)} %constant.68.clone) | copy-start | bytes 112
  81.1 91.1 %all-to-all-start.2 = ((f32[8,2,16,4096]{3,2,1,0:T(8,128)}), f32[8,2,16,4096]{3,2,1,0:T(8,128)}, u32[]{:S(2)}, u32[]{:S(2)}) async-start(f32[8,2,16,4096]{3,2,1,0:T(8,128)} %bitcast.26), calls=%async_computation.2 | async-start | bytes 8388608 | tf_op jit(solution)/shard_map/all_to_all | solution.py:718
  172.1 7.3 %copy-start.4 = (f32[16,256]{1,0:T(8,128)S(1)}, f32[16,256]{1,0:T(8,128)}, u32[]{:S(2)}) copy-start(f32[16,256]{1,0:T(8,128)} %constant.77) | copy-start | bytes 49156
  172.2 58.2 %all-to-all-start.1 = ((f32[32,2,128,128]{3,2,1,0:T(8,128)}), f32[32,2,128,128]{3,2,1,0:T(8,128)}, u32[]{:S(2)}, u32[]{:S(2)}) async-start(f32[32,2,128,128]{3,2,1,0:T(8,128)} %filter_y.1), calls=%async_computation.1 | async-start | bytes 8388608 | tf_op jit(solution)/shard_map/all_to_all | solution.py:723
  246.2 12.4 %collective-permute-start = (f32[2,8,4096]{2,1,0:T(8,128)S(1)}, f32[2,8,4096]{2,1,0:T(8,128)S(1)}, u32[]{:S(2)}, u32[]{:S(2)}) collective-permute-start(f32[2,8,4096]{2,1,0:T(8,128)S(1)} %get-tuple-element.12), channel_id=1, source_target_pairs={{0,32},{32,64},{64,96},{96,128},{128,160},{160,192},{192,224},{224... | collective-permute-start | bytes 786440 | tf_op jit(solution)/shard_map/ppermute | solution.py:686
  248.2 11.7 %collective-permute-start.1 = (f32[2,8,4096]{2,1,0:T(8,128)S(1)}, f32[2,8,4096]{2,1,0:T(8,128)S(1)}, u32[]{:S(2)}, u32[]{:S(2)}) collective-permute-start(f32[2,8,4096]{2,1,0:T(8,128)S(1)} %get-tuple-element.11), channel_id=1, source_target_pairs={{32,0},{64,32},{96,64},{128,96},{160,128},{192,160},{224,192},{1,2... | collective-permute-start | bytes 786440 | tf_op jit(solution)/shard_map/ppermute | solution.py:686
  258.7 1.2 copy-start.2
  259.8 0.7 copy-start.3
  326.1 2.4 copy-start.1
